TPU v7x, 32 devices: a whole 2x2x4 slice. The times are simulated.
32 devices in a mesh: fsdp: 2 (over x), ctx: 4 (over z), tp: 4 (over y, core).
Axes of the slice: x: 2, y: 2, z: 4, core: 2. Of those that a mesh axis runs over, the one named last changes fastest.
Arguments:
- tokens: bfloat16 [8192, 1024], P(('fsdp', 'ctx')), may hold values from -6 to 6
- w_qkv: bfloat16 [3, 1024, 1024], P(None, 'fsdp', 'tp'), may hold values from -0.25 to 0.25
- w_out: bfloat16 [1024, 1024], P('tp', 'fsdp'), may hold values from -0.75 to 0.75
- w_up: bfloat16 [1024, 4096], P('fsdp', 'tp'), may hold values from -0.1875 to 0.1875
- w_down: bfloat16 [4096, 1024], P('tp', 'fsdp'), may hold values from -0.09375 to 0.09375
- gains: bfloat16 [2, 1024], P(None, 'fsdp'), may hold values from 0.5 to 1.5
- shifts: bfloat16 [2, 1024], P(None, 'fsdp'), may hold values from -3 to 3
- lengths: int32 [2, 3], P('fsdp'), may hold values from 256 to 2048, as said below
- out_grad: bfloat16 [8192, 1024], P(('fsdp', 'ctx')), may hold values from -6 to 6
Outputs:
- out: bfloat16 [8192, 1024], P(('fsdp', 'ctx'))
- input_grad: bfloat16 [8192, 1024], P(('fsdp', 'ctx'))
- grad_qkv: float32 [3, 1024, 1024], P(None, 'fsdp', 'tp')
- grad_out: float32 [1024, 1024], P('tp', 'fsdp')
- grad_up: float32 [1024, 4096], P('fsdp', 'tp')
- grad_down: float32 [4096, 1024], P('tp', 'fsdp')
- grad_gains: float32 [2, 1024], P(None, 'fsdp')
- grad_shifts: float32 [2, 1024], P(None, 'fsdp')
Inputs may be any that keep to these rules, and one draw needn't show every extreme that they name: `lengths`: in each row one sequence has exactly 2048 tokens and the others 2048 // 8 to 1024; sequences lie end to end from the pack's first slot, and the slots after them up to 4096 are padding.
All inputs are finite; a program needn't handle non-finite values.
Results may differ from a plain program's by a relative error of at most 0.014.
The roundings to bfloat16 on the way count: a program that leaves them out, or rounds other values in their place, can miss the bound.
Values may be sent and summed in bfloat16 or wider, within the bound.
No kernel may reach another device: no remote copies, remote signals or barrier semaphores. Data moves between devices by JAX's collectives and lax.ppermute only.
A program may use at most 192 MiB of HBM per device.

v0:
```python
import math

import jax
import jax.numpy as jnp
from jax import lax
from jax.sharding import PartitionSpec as P

HEAD_DIM = 64
SEQS = 3


norm_eps = 1e-12
masked_low = -1e30


def layer_norm(rows, gain, shift):
    centre = rows - jnp.mean(rows, axis=-1, keepdims=True)
    spread = jnp.mean(centre * centre, axis=-1, keepdims=True)
    return centre * lax.rsqrt(spread + norm_eps) * gain + shift


def exact_gelu(values):
    return jax.nn.gelu(values, approximate=False)


def contract_rows(left, right):
    return lax.dot_general(
        left, right, (((0,), (0,)), ((), ())), preferred_element_type=jnp.float32
    )


def contract_cols(left, right):
    return lax.dot_general(
        left, right, (((1,), (1,)), ((), ())), preferred_element_type=jnp.float32
    )


def tp_total(terms):
    return lax.psum(terms, "tp")


def segment_of(lengths_row, total):
    seq_ends = jnp.cumsum(lengths_row)
    positions = jnp.arange(total, dtype=jnp.int32)
    return jnp.sum((positions[:, None] >= seq_ends[None, :]).astype(jnp.int32), axis=1)


def score_block(query_block, seg_block, key_heads, segments):
    raw_scores = jnp.einsum(
        "qhd,khd->hqk", query_block, key_heads, preferred_element_type=jnp.float32
    )
    allowed = (seg_block[:, None] == segments[None, :]) & (segments[None, :] < SEQS)
    return (raw_scores * (1.0 / math.sqrt(HEAD_DIM)), allowed)


def attend_forward(query_heads, seg_mine, key_heads, value_heads, segments):

    def one_block(inputs):
        query_block, seg_block = inputs
        scores, allowed = score_block(query_block, seg_block, key_heads, segments)
        has_key = jnp.any(allowed, axis=1)
        masked = jnp.where(allowed[None], scores, masked_low)
        row_max = jnp.where(has_key[None, :, None], jnp.max(masked, axis=2, keepdims=True), 0.0)
        exp_terms = jnp.where(allowed[None], jnp.exp(masked - row_max), 0.0)
        denominator = (
            jnp.sum(exp_terms, axis=2, keepdims=True)
            + (1.0 - has_key.astype(jnp.float32))[None, :, None]
        )
        attn_probs = (exp_terms / denominator).astype(jnp.bfloat16)
        context = jnp.einsum(
            "hqk,khd->qhd", attn_probs, value_heads, preferred_element_type=jnp.float32
        )
        log_total = row_max[:, :, 0] + jnp.log(denominator[:, :, 0])
        return (context.astype(jnp.bfloat16), log_total)

    return lax.map(one_block, (query_heads, seg_mine))


def attend_backward(
    query_heads, seg_mine, grad_heads, log_totals, key_heads, value_heads, segments
):
    score_scale = 1.0 / math.sqrt(HEAD_DIM)
    zero_keys = jnp.zeros(key_heads.shape, jnp.float32)

    def one_block(carry, inputs):
        key_grad, value_grad = carry
        query_block, seg_block, grad_block, log_block = inputs
        scores, allowed = score_block(query_block, seg_block, key_heads, segments)
        attn_probs = jnp.where(allowed[None], jnp.exp(scores - log_block[:, :, None]), 0.0)
        probs_low = attn_probs.astype(jnp.bfloat16)
        grad_probs = jnp.einsum(
            "qhd,khd->hqk", grad_block, value_heads, preferred_element_type=jnp.float32
        )
        row_delta = jnp.sum(attn_probs * grad_probs, axis=2, keepdims=True)
        grad_scores = (attn_probs * (grad_probs - row_delta) * score_scale).astype(jnp.bfloat16)
        query_grad = jnp.einsum(
            "hqk,khd->qhd", grad_scores, key_heads, preferred_element_type=jnp.float32
        )
        key_grad = key_grad + jnp.einsum(
            "hqk,qhd->khd", grad_scores, query_block, preferred_element_type=jnp.float32
        )
        value_grad = value_grad + jnp.einsum(
            "hqk,qhd->khd", probs_low, grad_block, preferred_element_type=jnp.float32
        )
        return ((key_grad, value_grad), query_grad)

    return lax.scan(
        one_block, (zero_keys, zero_keys), (query_heads, seg_mine, grad_heads, log_totals)
    )


def body(tokens, w_qkv, w_out, w_up, w_down, gains, shifts, lengths, out_grad):
    full_qkv, full_out, full_up, full_down, full_gains, full_shifts = (
        lax.all_gather(w_qkv, "fsdp", axis=1, tiled=True),
        lax.all_gather(w_out, "fsdp", axis=1, tiled=True),
        lax.all_gather(w_up, "fsdp", axis=0, tiled=True),
        lax.all_gather(w_down, "fsdp", axis=1, tiled=True),
        lax.all_gather(gains, "fsdp", axis=1, tiled=True),
        lax.all_gather(shifts, "fsdp", axis=1, tiled=True),
    )
    tok_rows = tokens.shape[0]
    local_width = full_qkv.shape[2]
    local_heads = local_width // HEAD_DIM
    block_rows = min(512, tok_rows)
    block_count = tok_rows // block_rows
    pack_rows = tok_rows * lax.axis_size("ctx")
    segments = segment_of(lengths[0], pack_rows)
    seg_mine = lax.dynamic_slice_in_dim(
        segments, lax.axis_index("ctx") * tok_rows, tok_rows
    ).reshape(block_count, block_rows)
    residual_in = tokens.astype(jnp.float32)
    projected = jnp.einsum(
        "td,sdc->stc", tokens, full_qkv, preferred_element_type=jnp.float32
    ).astype(jnp.bfloat16)
    key_rows, value_rows = (
        lax.all_gather(projected[1], "ctx", axis=0, tiled=True),
        lax.all_gather(projected[2], "ctx", axis=0, tiled=True),
    )
    key_heads = key_rows.reshape(pack_rows, local_heads, HEAD_DIM)
    value_heads = value_rows.reshape(pack_rows, local_heads, HEAD_DIM)
    query_heads = projected[0].reshape(block_count, block_rows, local_heads, HEAD_DIM)
    context_blocks, log_totals = attend_forward(
        query_heads, seg_mine, key_heads, value_heads, segments
    )
    context = context_blocks.reshape(tok_rows, local_width)
    attn_terms = jnp.dot(context, full_out, preferred_element_type=jnp.float32)
    resid_rows = residual_in + tp_total(attn_terms)
    grad_rows = out_grad.astype(jnp.float32)
    gain_full = full_gains.astype(jnp.float32)
    shift_full = full_shifts.astype(jnp.float32)
    hidden, norm_first = jax.vjp(layer_norm, resid_rows, gain_full[0], shift_full[0])
    hidden_part = hidden.astype(jnp.bfloat16)
    pre_act = jnp.dot(hidden_part, full_up, preferred_element_type=jnp.float32)
    activated, gelu_back = jax.vjp(exact_gelu, pre_act)
    act_low = activated.astype(jnp.bfloat16)
    ffn_terms = jnp.dot(act_low, full_down, preferred_element_type=jnp.float32)
    ffn_rows = tp_total(ffn_terms)
    result, norm_second = jax.vjp(layer_norm, hidden + ffn_rows, gain_full[1], shift_full[1])
    grad_mid, gain_second, shift_second = norm_second(grad_rows)
    mid_part = grad_mid.astype(jnp.bfloat16)
    result_part = result.astype(jnp.bfloat16)
    back_qkv, back_out, back_up, back_down = (
        lax.all_gather(w_qkv, "fsdp", axis=1, tiled=True),
        lax.all_gather(w_out, "fsdp", axis=1, tiled=True),
        lax.all_gather(w_up, "fsdp", axis=0, tiled=True),
        lax.all_gather(w_down, "fsdp", axis=1, tiled=True),
    )
    down_grad = contract_rows(act_low, mid_part)
    act_grad = contract_cols(mid_part, back_down)
    (pre_grad,) = gelu_back(act_grad)
    pre_low = pre_grad.astype(jnp.bfloat16)
    up_grad = contract_rows(hidden_part, pre_low)
    hidden_terms = contract_cols(pre_low, back_up)
    hidden_grad = grad_mid + tp_total(hidden_terms)
    resid_grad, gain_first, shift_first = norm_first(hidden_grad)
    attn_part = resid_grad.astype(jnp.bfloat16)
    out_proj_grad = contract_rows(context, attn_part)
    context_grad = contract_cols(attn_part, back_out).astype(jnp.bfloat16)
    grad_heads = context_grad.reshape(block_count, block_rows, local_heads, HEAD_DIM)
    (key_grad, value_grad), query_grad = attend_backward(
        query_heads, seg_mine, grad_heads, log_totals, key_heads, value_heads, segments
    )
    key_mine, value_mine = (
        lax.psum_scatter(
            key_grad.reshape(pack_rows, local_width), "ctx", scatter_dimension=0, tiled=True
        ),
        lax.psum_scatter(
            value_grad.reshape(pack_rows, local_width), "ctx", scatter_dimension=0, tiled=True
        ),
    )
    proj_grad = jnp.stack(
        [
            query_grad.reshape(tok_rows, local_width).astype(jnp.bfloat16),
            key_mine.astype(jnp.bfloat16),
            value_mine.astype(jnp.bfloat16),
        ]
    )
    qkv_grad = jnp.einsum("td,stc->sdc", tokens, proj_grad, preferred_element_type=jnp.float32)
    input_part = jnp.einsum("stc,sdc->td", proj_grad, back_qkv, preferred_element_type=jnp.float32)
    input_grad = (resid_grad + tp_total(input_part)).astype(jnp.bfloat16)
    gain_grad = jnp.stack([gain_first, gain_second])
    shift_grad = jnp.stack([shift_first, shift_second])
    qkv_grad, out_proj_grad, up_grad, down_grad, gain_grad, shift_grad = (
        lax.psum_scatter(qkv_grad, "fsdp", scatter_dimension=1, tiled=True),
        lax.psum_scatter(out_proj_grad, "fsdp", scatter_dimension=1, tiled=True),
        lax.psum_scatter(up_grad, "fsdp", scatter_dimension=0, tiled=True),
        lax.psum_scatter(down_grad, "fsdp", scatter_dimension=1, tiled=True),
        lax.psum_scatter(gain_grad, "fsdp", scatter_dimension=1, tiled=True),
        lax.psum_scatter(shift_grad, "fsdp", scatter_dimension=1, tiled=True),
    )
    qkv_grad, out_proj_grad, up_grad, down_grad, gain_grad, shift_grad = lax.psum(
        (qkv_grad, out_proj_grad, up_grad, down_grad, gain_grad, shift_grad), "ctx"
    )
    return (
        result_part,
        input_grad,
        qkv_grad,
        out_proj_grad,
        up_grad,
        down_grad,
        gain_grad,
        shift_grad,
    )


def solution(mesh):
    return jax.shard_map(
        body,
        mesh=mesh,
        in_specs=(
            P(("fsdp", "ctx"), None),
            P(None, "fsdp", "tp"),
            P("tp", "fsdp"),
            P("fsdp", "tp"),
            P("tp", "fsdp"),
            P(None, "fsdp"),
            P(None, "fsdp"),
            P("fsdp", None),
            P(("fsdp", "ctx"), None),
        ),
        out_specs=(
            P(("fsdp", "ctx"), None),
            P(("fsdp", "ctx"), None),
            P(None, "fsdp", "tp"),
            P("tp", "fsdp"),
            P("fsdp", "tp"),
            P("tp", "fsdp"),
            P(None, "fsdp"),
            P(None, "fsdp"),
        ),
        check_vma=False,
    )
```

profile of v0, /device:TPU:0, one launch (start us, length us, event | category | flops | bytes accessed | tf_op | source)
XLA Modules:
  0.0 1667.1 jit_solution(5852999273512513464)
XLA Ops:
  9.6 30.5 %all-gather.8.cloned.1.call-done = bf16[3,1024,256]{1,2,0:T(8,128)(2,1)} async-done(((bf16[3,512,256]{1,2,0:T(8,128)(2,1)}), bf16[3,1024,256]{1,2,0:T(8,128)(2,1)}) %all-gather.8.cloned.1.call-update) | async-done | bytes 1572880 | tf_op jit(solution)/shard_map/all_gather | solution.py:114
  55.7 35.5 %all-gather.14.cloned.1.call-done = bf16[1,4096,256]{1,2,0:T(8,128)(2,1)} async-done(((bf16[1,1024,256]{1,2,0:T(8,128)(2,1)}), bf16[1,4096,256]{1,2,0:T(8,128)(2,1)}) %all-gather.14.cloned.1.call-update) | async-done | bytes 2097168 | tf_op jit(solution)/shard_map/all_gather | solution.py:136
  91.2 46.9 %all-gather.16.cloned.1.call-done = bf16[1,4096,256]{1,2,0:T(8,128)(2,1)} async-done(((bf16[1,1024,256]{1,2,0:T(8,128)(2,1)}), bf16[1,4096,256]{1,2,0:T(8,128)(2,1)}) %all-gather.16.cloned.1.call-update) | async-done | bytes 2097168 | tf_op jit(solution)/shard_map/all_gather | solution.py:137
  138.0 99.9 %while.27 = (s32[]{:T(128)}, bf16[2,512,4,64]{1,3,2,0:T(8,128)(2,1)}, f32[2,4,512]{2,1,0:T(4,128)S(1)}, s32[2,512]{1,0:T(2,128)S(1)}, s32[4096]{0:T(1024)S(1)}, ...) while((s32[]{:T(128)}, ...), condition=%wide.region_6.7_spmd, body=%wide.region_2.6_spmd.sunk | while | flops 2271357440 | bytes 113924704 | solution.py:76
  140.3 15.8 fusion.181
  156.1 15.6 fusion.182
  171.8 16.2 fusion.183
  190.3 15.8 fusion.181
  206.1 15.6 fusion.182
  221.7 16.2 fusion.183
  253.3 74.2 %all-reduce.8.cloned.1.call-done = f32[1024,1024]{1,0:T(8,128)} async-done(((f32[1024,1024]{1,0:T(8,128)}), f32[1024,1024]{1,0:T(8,128)}) %all-reduce.8.cloned.1.call-update) | async-done | bytes 4194320 | tf_op jit(solution)/shard_map/psum | solution.py:39
  332.7 29.5 %all-gather.10.cloned.1.call-done = bf16[1024,1024]{1,0:T(8,128)(2,1)} async-done(((bf16[512,1024]{1,0:T(8,128)(2,1)}), bf16[1024,1024]{1,0:T(8,128)(2,1)}) %all-gather.10.cloned.1.call-update) | async-done | bytes 2097168 | tf_op jit(solution)/shard_map/all_gather | solution.py:116
  362.2 15.5 multiply_convert_fusion.1
  377.7 19.1 %all-gather.12.cloned.1.call-done = bf16[1024,1024]{1,0:T(8,128)(2,1)} async-done(((bf16[1024,512]{1,0:T(8,128)(2,1)}), bf16[1024,1024]{1,0:T(8,128)(2,1)}) %all-gather.12.cloned.1.call-update) | async-done | bytes 2097168 | tf_op jit(solution)/shard_map/all_gather | solution.py:117
  403.8 85.2 %all-reduce.10.cloned.1.call-done = f32[1024,1024]{1,0:T(8,128)} async-done(((f32[1024,1024]{1,0:T(8,128)}), f32[1024,1024]{1,0:T(8,128)}) %all-reduce.10.cloned.1.call-update) | async-done | bytes 4194320 | tf_op jit(solution)/shard_map/psum | solution.py:39
  513.4 85.7 %all-reduce.12.cloned.1.call-done = f32[1024,1024]{1,0:T(8,128)} async-done(((f32[1024,1024]{1,0:T(8,128)}), f32[1024,1024]{1,0:T(8,128)}) %all-reduce.12.cloned.1.call-update) | async-done | bytes 4194320 | tf_op jit(solution)/shard_map/psum | solution.py:39
  615.2 341.7 %while.28 = (s32[]{:T(128)}, f32[4096,4,64]{0,2,1:T(8,128)}, f32[4096,4,64]{0,2,1:T(8,128)}, bf16[2,512,4,64]{1,3,2,0:T(8,128)(2,1)}, bf16[2,512,4,64]{1,3,2,0:T...) while((s32[]{:T(128)}, f32[4096,4,64]{0,2,1:T(8,128)}, ...), condition=%wide.region_20.21_spmd.clone, body=%wide.region_18.20_spmd.clone.sunk | while | flops 5595217920 | bytes 414817440 | solution.py:107
  644.4 63.5 %fusion.197 = f32[4096,4,64]{0,2,1:T(8,128)} fusion(f32[4,512,4096]{2,1,0:T(8,128)} %fusion.195, f32[4,512,4096]{2,1,0:T(8,128)} %fusion.196, f32[4,512]{1,0:T(4,128)S(1)} %dynamic-slice_bitcast_fusion.2, pred[512,4096]{1,0:T(8,128)(4,1)} %compare_and_fusion.3, f32[4096,4,64]{0,2,1:T(8,128)} %get-tuple-element.498, pred[]{:T(512)S(6)} %compare.3, ...), kind=kOutput, calls=%fused_computation.48.clone.1 | convolution fusion | flops 1168119808 | bytes 147079680 | tf_op jit(solution)/shard_map/while/body/eval_jaxpr/hqk,qhd->khd/dot_general | solution.py:99
  708.0 60.0 %fusion.199 = bf16[2,512,4,64]{1,3,2,0:T(8,128)(2,1)} fusion(bf16[2,512,4,64]{1,3,2,0:T(8,128)(2,1)} %get-tuple-element.500, s32[]{:T(128)} %get-tuple-element.497, bf16[4096,4,64]{0,2,1:T(8,128)(2,1)S(1)} %get-tuple-element.517, f32[4,512,4096]{2,1,0:T(8,128)} %fusion.195, f32[4,512,4096]{2,1,0:T(8,128)} %fusion.196, ...), kind=kOutput, calls=%fused_computation.52.clone.1 | convolution fusion | flops 1166022656 | bytes 141050368 | tf_op jit(solution)/shard_map/while/body/eval_jaxpr/hqk,khd->qhd/dot_general | solution.py:96
  767.9 17.3 %fusion.198 = f32[4096,4,64]{0,2,1:T(8,128)} fusion(f32[4,512,4096]{2,1,0:T(8,128)} %fusion.196, f32[4,512]{1,0:T(4,128)S(1)} %dynamic-slice_bitcast_fusion.2, pred[512,4096]{1,0:T(8,128)(4,1)} %compare_and_fusion.3, f32[4096,4,64]{0,2,1:T(8,128)} %get-tuple-element.499, pred[]{:T(512)S(6)} %compare.3, ...), kind=kOutput, calls=%fused_computation.50.clone.1 | convolution fusion | flops 1109393408 | bytes 44310532 | tf_op jit(solution)/shard_map/while/body/eval_jaxpr/hqk,qhd->khd/dot_general | solution.py:102
  814.3 64.0 %fusion.197 = f32[4096,4,64]{0,2,1:T(8,128)} fusion(f32[4,512,4096]{2,1,0:T(8,128)} %fusion.195, f32[4,512,4096]{2,1,0:T(8,128)} %fusion.196, f32[4,512]{1,0:T(4,128)S(1)} %dynamic-slice_bitcast_fusion.2, pred[512,4096]{1,0:T(8,128)(4,1)} %compare_and_fusion.3, f32[4096,4,64]{0,2,1:T(8,128)} %get-tuple-element.498, pred[]{:T(512)S(6)} %compare.3, ...), kind=kOutput, calls=%fused_computation.48.clone.1 | convolution fusion | flops 1168119808 | bytes 147079680 | tf_op jit(solution)/shard_map/while/body/eval_jaxpr/hqk,qhd->khd/dot_general | solution.py:99
  878.3 60.0 %fusion.199 = bf16[2,512,4,64]{1,3,2,0:T(8,128)(2,1)} fusion(bf16[2,512,4,64]{1,3,2,0:T(8,128)(2,1)} %get-tuple-element.500, s32[]{:T(128)} %get-tuple-element.497, bf16[4096,4,64]{0,2,1:T(8,128)(2,1)S(1)} %get-tuple-element.517, f32[4,512,4096]{2,1,0:T(8,128)} %fusion.195, f32[4,512,4096]{2,1,0:T(8,128)} %fusion.196, ...), kind=kOutput, calls=%fused_computation.52.clone.1 | convolution fusion | flops 1166022656 | bytes 141050368 | tf_op jit(solution)/shard_map/while/body/eval_jaxpr/hqk,khd->qhd/dot_general | solution.py:96
  938.3 18.5 %fusion.198 = f32[4096,4,64]{0,2,1:T(8,128)} fusion(f32[4,512,4096]{2,1,0:T(8,128)} %fusion.196, f32[4,512]{1,0:T(4,128)S(1)} %dynamic-slice_bitcast_fusion.2, pred[512,4096]{1,0:T(8,128)(4,1)} %compare_and_fusion.3, f32[4096,4,64]{0,2,1:T(8,128)} %get-tuple-element.499, pred[]{:T(512)S(6)} %compare.3, ...), kind=kOutput, calls=%fused_computation.50.clone.1 | convolution fusion | flops 1109393408 | bytes 44310532 | tf_op jit(solution)/shard_map/while/body/eval_jaxpr/hqk,qhd->khd/dot_general | solution.py:102
  992.0 47.7 %reduce-scatter.15.cloned.1.call-done = f32[1024,256]{1,0:T(8,128)} async-done(((f32[4096,256]{1,0:T(8,128)}), f32[1024,256]{1,0:T(8,128)}) %reduce-scatter.15.cloned.1.call-update) | async-done | bytes 1048592 | tf_op jit(solution)/shard_map/reduce_scatter | solution.py:187
  1040.9 78.2 %reduce-scatter.13.cloned.1.call-done = f32[1024,256]{1,0:T(8,128)} async-done(((f32[4096,256]{1,0:T(8,128)}), f32[1024,256]{1,0:T(8,128)}) %reduce-scatter.13.cloned.1.call-update) | async-done | bytes 1048592 | tf_op jit(solution)/shard_map/reduce_scatter | solution.py:184
  1142.9 56.5 %reduce-scatter.23.cloned.1.call-done = f32[1024,512]{1,0:T(8,128)} async-done(((f32[1024,1024]{1,0:T(8,128)}), f32[1024,512]{1,0:T(8,128)}) %reduce-scatter.23.cloned.1.call-update) | async-done | bytes 2097168 | tf_op jit(solution)/shard_map/reduce_scatter | solution.py:207
  1199.4 56.7 %reduce-scatter.21.cloned.1.call-done = f32[512,1024]{1,0:T(8,128)} async-done(((f32[1024,1024]{1,0:T(8,128)}), f32[512,1024]{1,0:T(8,128)}) %reduce-scatter.21.cloned.1.call-update) | async-done | bytes 2097168 | tf_op jit(solution)/shard_map/reduce_scatter | solution.py:206
  1256.1 45.5 %reduce-scatter.17.cloned.1.call-done = f32[3,512,256]{1,2,0:T(8,128)} async-done(((f32[3,1024,256]{1,2,0:T(8,128)}), f32[3,512,256]{1,2,0:T(8,128)}) %reduce-scatter.17.cloned.1.call-update) | async-done | bytes 1572880 | tf_op jit(solution)/shard_map/reduce_scatter | solution.py:204
  1301.6 17.3 %reduce-scatter.25.cloned.1.call-done = f32[512,2]{1,0:T(8,128)} async-done(((f32[1024,2]{1,0:T(8,128)}), f32[512,2]{1,0:T(8,128)}) %reduce-scatter.25.cloned.1.call-update) | async-done | bytes 4112
  1320.0 16.2 reduce-scatter.27.cloned.1.call-done
  1349.7 74.4 %all-reduce.14.cloned.1.call-done = f32[1024,1024]{1,0:T(8,128)} async-done(((f32[1024,1024]{1,0:T(8,128)}), f32[1024,1024]{1,0:T(8,128)}) %all-reduce.14.cloned.1.call-update) | async-done | bytes 4194320 | tf_op jit(solution)/shard_map/psum | solution.py:39
  1429.2 221.3 %all-reduce.16.cloned.1.call-done = (f32[3,512,256]{1,2,0:T(8,128)}, f32[256,512]{1,0:T(8,128)}, f32[512,1024]{1,0:T(8,128)}, f32[1024,512]{1,0:T(8,128)}) async-done(((f32[3,512,256]{1,2,0:T(8,128)}, f32[256,512]{1,0:T(8,128)}, f32[512,1024]{1,0:T(8,128)}, f32[1024,512]{1,0:T(8,128)}), (f32[3,512,256]{1,2,0:T(8,128)}, f32[256,512]{1,0:T(8,128)}, f32[512,1024]{1,0:T(8,128)}, ...) | async-done | bytes 6291472 | tf_op jit(solution)/shard_map/psum | solution.py:211
  (218 shorter events, 237.5 us)
Async XLA Ops:
  7.2 32.9 %all-gather.8.cloned.1.call-start = ((), (), s32[]{:S(2)}) async-start(), calls=%async_computation.8 | async-start | bytes 2359296 | tf_op jit(solution)/shard_map/all_gather | solution.py:114
  9.5 81.6 %all-gather.14.cloned.1.call-start = ((), (), s32[]{:S(2)}) async-start(), calls=%async_computation.21 | async-start | bytes 2621440 | tf_op jit(solution)/shard_map/all_gather | solution.py:136
  45.1 92.9 %all-gather.16.cloned.1.call-start = ((), (), s32[]{:S(2)}) async-start(), calls=%async_computation.22 | async-start | bytes 2621440 | tf_op jit(solution)/shard_map/all_gather | solution.py:137
  45.8 281.7 %all-reduce.8.cloned.1.call-start = ((), (), s32[]{:S(2)}) async-start(), calls=%async_computation.9 | async-start | bytes 8388608 | tf_op jit(solution)/shard_map/psum | solution.py:39
  138.0 102.4 %copy-start.11 = (bf16[256,1024]{1,0:T(8,128)(2,1)S(1)}, bf16[256,1024]{1,0:T(8,128)(2,1)}, u32[]{:S(2)}) copy-start(bf16[256,1024]{1,0:T(8,128)(2,1)} %all_gather.31) | copy-start | bytes 1572868
  243.1 84.4 %copy-start.9 = (bf16[1024,1024]{1,0:T(8,128)(2,1)S(1)}, bf16[1024,1024]{1,0:T(8,128)(2,1)}, u32[]{:S(2)}) copy-start(bf16[1024,1024]{1,0:T(8,128)(2,1)} %param.13) | copy-start | bytes 6291460
  243.2 119.1 %all-gather.10.cloned.1.call-start = ((), (), s32[]{:S(2)}) async-start(), calls=%async_computation.10 | async-start | bytes 3145728 | tf_op jit(solution)/shard_map/all_gather | solution.py:116
  243.7 153.1 %all-gather.12.cloned.1.call-start = ((), (), s32[]{:S(2)}) async-start(), calls=%async_computation.11 | async-start | bytes 3145728 | tf_op jit(solution)/shard_map/all_gather | solution.py:117
  244.3 244.7 %all-reduce.10.cloned.1.call-start = ((), (), s32[]{:S(2)}) async-start(), calls=%async_computation.12 | async-start | bytes 8388608 | tf_op jit(solution)/shard_map/psum | solution.py:39
  248.7 356.8 %copy-start.21 = (f32[1,1024]{1,0:T(1,128)}, f32[1,1024]{1,0:T(1,128)S(1)}, u32[]{:S(2)}) copy-start(f32[1,1024]{1,0:T(1,128)S(1)} %get-tuple-element.329) | copy-start | bytes 12292
  253.3 235.7 %copy-start.28 = (f32[1,1024]{1,0:T(1,128)}, f32[1,1024]{1,0:T(1,128)S(1)}, u32[]{:S(2)}) copy-start(f32[1,1024]{1,0:T(1,128)S(1)} %get-tuple-element.331) | copy-start | bytes 12292
  330.2 275.3 %copy-start.17 = (f32[1024]{0:T(1024)}, f32[1024]{0:T(1024)S(1)}, u32[]{:S(2)}) copy-start(f32[1024]{0:T(1024)S(1)} %broadcast_multiply_fusion.1) | copy-start | bytes 12292
  332.7 272.8 %copy-start.19 = (f32[1024]{0:T(1024)}, f32[1024]{0:T(1024)S(1)}, u32[]{:S(2)}) copy-start(f32[1024]{0:T(1024)S(1)} %fusion.114) | copy-start | bytes 12292
  403.4 195.7 %all-reduce.12.cloned.1.call-start = ((), (), s32[]{:S(2)}) async-start(), calls=%async_computation.13 | async-start | bytes 8388608 | tf_op jit(solution)/shard_map/psum | solution.py:39
  500.6 7.0 copy-start.5
  500.6 98.5 %copy-start.25 = (f32[1024]{0:T(1024)}, f32[1024]{0:T(1024)S(1)}, u32[]{:S(2)}) copy-start(f32[1024]{0:T(1024)S(1)} %negate_multiply_fusion.2) | copy-start | bytes 12292
  513.3 526.3 %reduce-scatter.15.cloned.1.call-start = ((), (), s32[]{:S(2)}) async-start(), calls=%async_computation.15 | async-start | bytes 5242880 | tf_op jit(solution)/shard_map/reduce_scatter | solution.py:187
  599.1 6.4 copy-start.1
  607.3 7.9 copy-start.23
  618.2 13.1 copy-start.3
  788.1 13.1 copy-start.3
  962.6 156.5 %reduce-scatter.13.cloned.1.call-start = ((), (), s32[]{:S(2)}) async-start(), calls=%async_computation.14 | async-start | bytes 5242880 | tf_op jit(solution)/shard_map/reduce_scatter | solution.py:184
  968.3 174.5 %reduce-scatter.19.cloned.1.call-start = ((), (), s32[]{:S(2)}) async-start(), calls=%async_computation.18 | async-start | bytes 1572864 | tf_op jit(solution)/shard_map/reduce_scatter | solution.py:205
  973.6 225.7 %reduce-scatter.23.cloned.1.call-start = ((), (), s32[]{:S(2)}) async-start(), calls=%async_computation.20 | async-start | bytes 6291456 | tf_op jit(solution)/shard_map/reduce_scatter | solution.py:207
  980.4 275.7 %reduce-scatter.21.cloned.1.call-start = ((), (), s32[]{:S(2)}) async-start(), calls=%async_computation.19 | async-start | bytes 6291456 | tf_op jit(solution)/shard_map/reduce_scatter | solution.py:206
  988.7 132.5 %copy-start.10 = (bf16[1024,1024]{1,0:T(8,128)(2,1)S(1)}, bf16[1024,1024]{1,0:T(8,128)(2,1)}, u32[]{:S(2)}) copy-start(bf16[1024,1024]{1,0:T(8,128)(2,1)} %param.13) | copy-start | bytes 6291460
  988.7 312.8 %reduce-scatter.17.cloned.1.call-start = ((), (), s32[]{:S(2)}) async-start(), calls=%async_computation.17 | async-start | bytes 4718592 | tf_op jit(solution)/shard_map/reduce_scatter | solution.py:204
  1125.8 193.1 %reduce-scatter.25.cloned.1.call-start = ((), (), s32[]{:S(2)}) async-start(), calls=%async_computation.23 | async-start | bytes 786432
  1126.9 209.2 %reduce-scatter.27.cloned.1.call-start = ((), (), s32[]{:S(2)}) async-start(), calls=%async_computation.24 | async-start | bytes 786432
  1128.0 296.0 %all-reduce.14.cloned.1.call-start = ((), (), s32[]{:S(2)}) async-start(), calls=%async_computation.16 | async-start | bytes 8388608 | tf_op jit(solution)/shard_map/psum | solution.py:39
  1133.4 517.1 %all-reduce.16.cloned.1.call-start = ((), (), s32[]{:S(2)}) async-start(), calls=%async_computation.25 | async-start | bytes 12582912 | tf_op jit(solution)/shard_map/psum | solution.py:211
  1650.5 8.2 copy-start.12
  (30 other events, 77.4 us)
Sparse Core Ops, SparseCore 0:
  10.1 29.8 all-gather.7
  45.2 45.9 all-gather.13
  93.3 44.6 all-gather.15
  243.3 84.1 all-reduce.7
  329.0 33.2 all-gather.9
  363.7 33.1 all-gather.11
  403.5 85.4 all-reduce.9
  513.5 85.6 all-reduce.11
  962.7 76.8 reduce-scatter.14
  1041.8 77.2 reduce-scatter.12
  1122.0 20.8 reduce-scatter.18
  1145.0 54.3 reduce-scatter.22
  1201.8 54.2 reduce-scatter.20
  1258.2 43.3 reduce-scatter.16
  1304.3 14.5 reduce-scatter.24
  1321.6 14.5 reduce-scatter.26
  1338.5 85.4 all-reduce.13
  1426.5 223.9 all-reduce.15
where the time goes:
time: 1670 us
  waiting for transfers between devices  1030 us (62%)
  matrix products  465 us (28%)
  other arithmetic  71.4 us (4%)
  local copies, waits for them, and re-layouts  51.7 us (3%)
  blocking collectives  30.3 us (2%)
    psum x4, waiting for transfers between devices, tp_total(): return lax.psum(terms, 'tp')  319 us
    psum x1, waiting for transfers between devices, body(): lax.psum((qkv_grad, out_proj_grad, up_grad, down_grad, gain_grad, shift_g...  221 us
    dot_general x2, matrix products, one_block(): jnp.einsum('hqk,qhd->khd', grad_scores, query_block, preferred_element_ty...  128 us
    dot_general x2, matrix products, one_block(): jnp.einsum('hqk,khd->qhd', grad_scores, key_heads, preferred_element_type...  120 us
    reduce_scatter x1, waiting for transfers between devices, body(): lax.psum_scatter(key_grad.reshape(pack_rows, local_width), 'ctx', scatter...  78.2 us
    dot_general x4, matrix products, score_block(): jnp.einsum('qhd,khd->hqk', query_block, key_heads, preferred_element_type...  57.8 us
    reduce_scatter x1, waiting for transfers between devices, body(): lax.psum_scatter(up_grad, 'fsdp', scatter_dimension=0, tiled=True)  56.7 us
    reduce_scatter x1, waiting for transfers between devices, body(): lax.psum_scatter(down_grad, 'fsdp', scatter_dimension=1, tiled=True)  56.5 us
  transfers between devices with their start and end apart: 18, of which 18 were waited for; matrix products, arithmetic and copies ran while one was open for 4% of the time, Pallas kernels for 0%

commit v1 on v0

v1 whole, which is shorter than its diff:
```python
import functools
import math

import jax
import jax.numpy as jnp
from jax import lax
from jax.experimental import pallas as pl
from jax.experimental.pallas import tpu as pltpu
from jax.sharding import PartitionSpec as P

HEAD_DIM = 64
BLK = 256
LOW = -1e30
norm_eps = 1e-12
f32 = jnp.float32
bf16 = jnp.bfloat16


def contract(left, right, left_dim, right_dim):
    return lax.dot_general(
        left, right, (((left_dim,), (right_dim,)), ((), ())), preferred_element_type=f32
    )


def nn(left, right):
    return contract(left, right, 1, 0)


def nt(left, right):
    return contract(left, right, 1, 1)


def tn(left, right):
    return contract(left, right, 0, 0)


def row_limits(info, qbase, rows):
    end0, end1, end2 = info[0], info[1], info[2]
    pos = qbase + lax.broadcasted_iota(jnp.int32, (1, rows), 1)
    first = jnp.where(pos < end0, 0, jnp.where(pos < end1, end0, end1))
    last = jnp.where(pos < end0, end0, jnp.where(pos < end1, end1, end2))
    real = pos < end2
    return jnp.where(real, first, 0), jnp.where(real, last, 0), real


def key_range(info, qbase, rows):
    end0, end1, end2 = info[0], info[1], info[2]
    low = jnp.where(
        qbase < end0,
        0,
        jnp.where(qbase < end1, end0, jnp.where(qbase < end2, end1, 1 << 30)),
    )
    final = qbase + rows - 1
    high = jnp.where(final < end0, end0, jnp.where(final < end1, end1, end2))
    return low, high


def attend_kernel(
    heads, qcount, kcount, info, q_ref, k_ref, vt_ref, ctx_ref, lse_ref, m_sc, l_sc, acc_sc, qm_sc
):
    i = pl.program_id(0)
    rows = q_ref.shape[0]
    qbase = info[3 + i]
    first, last, real = row_limits(info, qbase, rows)
    low, high = key_range(info, qbase, rows)
    factor = math.log2(math.e) / math.sqrt(HEAD_DIM)
    m_sc[...] = jnp.full_like(m_sc, LOW)
    l_sc[...] = jnp.zeros_like(l_sc)
    acc_sc[...] = jnp.zeros_like(acc_sc)
    q = q_ref[...]
    head_of = lax.broadcasted_iota(jnp.int32, q.shape, 1) // HEAD_DIM
    for h in range(heads):
        qm_sc[h * rows : (h + 1) * rows, :] = jnp.where(head_of == h, q, jnp.zeros_like(q))

    def step(j, carry):
        base = info[3 + qcount + j]

        @pl.when((base + BLK > low) & (base < high))
        def _():
            span = pl.ds(pl.multiple_of(j * BLK, BLK), BLK)
            kb = k_ref[span, :]
            vt = vt_ref[:, span]
            posk = base + lax.broadcasted_iota(jnp.int32, (BLK, rows), 0)
            allowed = (posk >= first) & (posk < last)
            for h in range(heads):
                feats = slice(h * HEAD_DIM, (h + 1) * HEAD_DIM)
                s = nt(kb, qm_sc[h * rows : (h + 1) * rows, :])
                s = jnp.where(allowed, s * factor, LOW)
                m_old = m_sc[h : h + 1, :]
                m_new = jnp.maximum(m_old, jnp.max(s, axis=0, keepdims=True))
                p = jnp.exp2(s - m_new)
                alpha = jnp.exp2(m_old - m_new)
                l_sc[h : h + 1, :] = l_sc[h : h + 1, :] * alpha + jnp.sum(p, axis=0, keepdims=True)
                m_sc[h : h + 1, :] = m_new
                acc_sc[feats, :] = acc_sc[feats, :] * alpha + nn(vt[feats, :], p.astype(bf16))

        return carry

    lax.fori_loop(0, kcount, step, 0)
    for h in range(heads):
        feats = slice(h * HEAD_DIM, (h + 1) * HEAD_DIM)
        total = l_sc[h : h + 1, :]
        acc_sc[feats, :] = jnp.where(real, acc_sc[feats, :] / total, 0.0)
        lse_ref[h : h + 1, :] = jnp.where(real, m_sc[h : h + 1, :] + jnp.log2(total), -LOW)
    ctx_ref[...] = acc_sc[...].T.astype(bf16)


def whole(shape):
    return pl.BlockSpec(shape, lambda i, *_: (0,) * len(shape))


def attend(info, q, k, vt):
    rows, width = q.shape
    heads = width // HEAD_DIM
    keys = k.shape[0]
    qcount, kcount = rows // BLK, keys // BLK
    block = pl.BlockSpec((BLK, width), lambda i, *_: (i, 0))
    return pl.pallas_call(
        functools.partial(attend_kernel, heads, qcount, kcount),
        grid_spec=pltpu.PrefetchScalarGridSpec(
            num_scalar_prefetch=1,
            grid=(qcount,),
            in_specs=[block, whole((keys, width)), whole((width, keys))],
            out_specs=[block, pl.BlockSpec((heads, BLK), lambda i, *_: (0, i))],
            scratch_shapes=[
                pltpu.VMEM((heads, BLK), f32),
                pltpu.VMEM((heads, BLK), f32),
                pltpu.VMEM((width, BLK), f32),
                pltpu.VMEM((heads * BLK, width), bf16),
            ],
        ),
        out_shape=[
            jax.ShapeDtypeStruct((rows, width), bf16),
            jax.ShapeDtypeStruct((heads, rows), f32),
        ],
        cost_estimate=pl.CostEstimate(
            flops=8 * rows * keys * width,
            bytes_accessed=4 * keys * width,
            transcendentals=rows * keys * heads // 2,
        ),
        name="attend",
    )(info, q, k, vt)


def attend_back_kernel(
    heads, qcount, kcount, info, q_ref, do_ref, o_ref, lse_ref, k_ref, v_ref, kt_ref,
    dq_ref, own_ref, left_ref, right_ref, far_ref,
    dk_sc, dv_sc, dqt_sc, qm_sc, dom_sc, p_sc, ds_sc, delta_sc,
):
    i = pl.program_id(0)
    rows = q_ref.shape[0]
    qbase = info[3 + i]
    first, last, real = row_limits(info, qbase, rows)
    low, high = key_range(info, qbase, rows)
    scale = 1.0 / math.sqrt(HEAD_DIM)
    factor = math.log2(math.e) * scale

    @pl.when(i == 0)
    def _():
        dk_sc[...] = jnp.zeros_like(dk_sc)
        dv_sc[...] = jnp.zeros_like(dv_sc)

    dqt_sc[...] = jnp.zeros_like(dqt_sc)
    q = q_ref[...]
    do = do_ref[...]
    head_of = lax.broadcasted_iota(jnp.int32, q.shape, 1) // HEAD_DIM
    for h in range(heads):
        qm_sc[h * rows : (h + 1) * rows, :] = jnp.where(head_of == h, q, jnp.zeros_like(q))
        dom_sc[h * rows : (h + 1) * rows, :] = jnp.where(head_of == h, do, jnp.zeros_like(do))
    prod = (do.astype(f32) * o_ref[...].astype(f32)).T
    for h in range(heads):
        delta_sc[h : h + 1, :] = jnp.sum(
            prod[h * HEAD_DIM : (h + 1) * HEAD_DIM, :], axis=0, keepdims=True
        )

    def step(j, carry):
        base = info[3 + qcount + j]

        @pl.when((base + BLK > low) & (base < high))
        def _():
            span = pl.ds(pl.multiple_of(j * BLK, BLK), BLK)
            kb = k_ref[span, :]
            vb = v_ref[span, :]
            kt = kt_ref[:, span]
            posk = base + lax.broadcasted_iota(jnp.int32, (BLK, rows), 0)
            allowed = (posk >= first) & (posk < last)
            for h in range(heads):
                feats = slice(h * HEAD_DIM, (h + 1) * HEAD_DIM)
                cols = slice(h * rows, (h + 1) * rows)
                s = nt(kb[:, feats], q_ref[:, feats])
                dp = nt(vb[:, feats], do_ref[:, feats])
                p = jnp.where(allowed, jnp.exp2(s * factor - lse_ref[h : h + 1, :]), 0.0)
                ds = (p * (dp - delta_sc[h : h + 1, :])).astype(bf16)
                p_sc[:, cols] = p.astype(bf16)
                ds_sc[:, cols] = ds
                dqt_sc[feats, :] += nn(kt[feats, :], ds)
            dv_sc[span, :] += nn(p_sc[...], dom_sc[...])
            dk_sc[span, :] += nn(ds_sc[...], qm_sc[...])

        return carry

    lax.fori_loop(0, kcount, step, 0)
    dq_ref[...] = (dqt_sc[...] * scale).T.astype(bf16)

    @pl.when(i == pl.num_programs(0) - 1)
    def _():
        part = own_ref.shape[1]
        for n, out_ref in enumerate((own_ref, left_ref, right_ref, far_ref)):
            out_ref[0] = (dk_sc[n * part : (n + 1) * part, :] * scale).astype(bf16)
            out_ref[1] = dv_sc[n * part : (n + 1) * part, :].astype(bf16)


def attend_back(info, q, do, o, lse, k, v, kt):
    rows, width = q.shape
    heads = width // HEAD_DIM
    keys = k.shape[0]
    qcount, kcount = rows // BLK, keys // BLK
    block = pl.BlockSpec((BLK, width), lambda i, *_: (i, 0))
    pair = (2, keys // 4, width)
    return pl.pallas_call(
        functools.partial(attend_back_kernel, heads, qcount, kcount),
        grid_spec=pltpu.PrefetchScalarGridSpec(
            num_scalar_prefetch=1,
            grid=(qcount,),
            in_specs=[
                block,
                block,
                block,
                pl.BlockSpec((heads, BLK), lambda i, *_: (0, i)),
                whole((keys, width)),
                whole((keys, width)),
                whole((width, keys)),
            ],
            out_specs=[block] + [whole(pair)] * 4,
            scratch_shapes=[
                pltpu.VMEM((keys, width), f32),
                pltpu.VMEM((keys, width), f32),
                pltpu.VMEM((width, BLK), f32),
                pltpu.VMEM((heads * BLK, width), bf16),
                pltpu.VMEM((heads * BLK, width), bf16),
                pltpu.VMEM((BLK, heads * BLK), bf16),
                pltpu.VMEM((BLK, heads * BLK), bf16),
                pltpu.VMEM((heads, BLK), f32),
            ],
        ),
        out_shape=[jax.ShapeDtypeStruct((rows, width), bf16)]
        + [jax.ShapeDtypeStruct(pair, bf16)] * 4,
        cost_estimate=pl.CostEstimate(
            flops=20 * rows * keys * width,
            bytes_accessed=8 * keys * width,
            transcendentals=rows * keys * heads // 2,
        ),
        name="attend_back",
    )(info, q, do, o, lse, k, v, kt)


def tp_swap(x, bit):
    return lax.ppermute(x, "tp", [(i, i ^ bit) for i in range(4)])


def after(x, *others):
    return lax.optimization_barrier((x,) + others)[0]


def fsdp_whole(shard, dim):
    if lax.axis_size("fsdp") != 2:
        return lax.all_gather(shard, "fsdp", axis=dim, tiled=True)
    other = lax.ppermute(shard, "fsdp", [(0, 1), (1, 0)])
    low_half = lax.axis_index("fsdp") == 0
    return jnp.concatenate(
        [jnp.where(low_half, shard, other), jnp.where(low_half, other, shard)], axis=dim
    )


def fsdp_total(block_of, size, dim):
    count = lax.axis_size("fsdp")
    if count != 2:
        return lax.psum_scatter(block_of(0, size), "fsdp", scatter_dimension=dim, tiled=True)
    half = size // 2
    mine = lax.axis_index("fsdp")
    sent = block_of((1 - mine) * half, half).astype(bf16)
    got = lax.ppermute(sent, "fsdp", [(0, 1), (1, 0)])
    return block_of(mine * half, half) + got.astype(f32)


def ctx_total(terms):
    place = lax.axis_index("ctx")
    sent = terms.astype(bf16)
    got = lax.ppermute(sent, "ctx", [(0, 1), (3, 2)])
    side = lax.optimization_barrier((terms + got.astype(f32)).astype(bf16))
    across = lax.ppermute(side, "ctx", [(1, 2), (2, 1)])
    total = lax.optimization_barrier((side.astype(f32) + across.astype(f32)).astype(bf16))
    back = lax.ppermute(total, "ctx", [(1, 0), (2, 3)])
    return jnp.where((place == 1) | (place == 2), total, back).astype(f32)


def rows_out(own):
    far = tp_swap(own, 2)
    near = tp_swap(own, 1)
    return own, near, far, tp_swap(far, 1)


def rows_in(terms):
    toward = terms[2] + tp_swap(terms[3].astype(bf16), 1).astype(f32)
    got = tp_swap(toward.astype(bf16), 2)
    here = terms[0] + tp_swap(terms[1].astype(bf16), 1).astype(f32)
    return here + got.astype(f32)


def natural(parts, core, y):
    r0, r1, r2, r3 = parts
    a0, a1 = jnp.where(core, r1, r0), jnp.where(core, r0, r1)
    a2, a3 = jnp.where(core, r3, r2), jnp.where(core, r2, r3)
    return jnp.concatenate(
        [jnp.where(y, a2, a0), jnp.where(y, a3, a1), jnp.where(y, a0, a2), jnp.where(y, a1, a3)]
    )


def norm_rows(rows):
    centre = rows - jnp.mean(rows, axis=-1, keepdims=True)
    inverse = lax.rsqrt(jnp.mean(centre * centre, axis=-1, keepdims=True) + norm_eps)
    return centre * inverse, inverse


def norm_back(grad, gain, normed, inverse):
    dn = grad * gain
    return (
        dn
        - jnp.mean(dn, axis=-1, keepdims=True)
        - normed * jnp.mean(dn * normed, axis=-1, keepdims=True)
    ) * inverse


def gelu_pair(values):
    phi_sum = 0.5 + 0.5 * lax.erf(values * math.sqrt(0.5))
    density = jnp.exp(values * values * -0.5) * (1.0 / math.sqrt(2.0 * math.pi))
    return (values * phi_sum).astype(bf16), phi_sum + values * density


def body(tokens, w_qkv, w_out, w_up, w_down, gains, shifts, lengths, out_grad):
    place = lax.axis_index("ctx")
    t = lax.axis_index("tp")
    core, y = (t & 1) == 1, (t >> 1) == 1
    tok_rows, depth = tokens.shape
    quarter = tok_rows // 4
    order = (0, 2, 1, 3)

    def quarter_of(array, r):
        return lax.dynamic_slice_in_dim(array, (t ^ r) * quarter, quarter)

    half_a = jnp.concatenate([quarter_of(tokens, 0), quarter_of(tokens, 2)])
    half_b = jnp.concatenate([quarter_of(tokens, 1), quarter_of(tokens, 3)])
    left_a = lax.ppermute(half_a, "ctx", [(0, 1), (1, 2), (2, 3)])
    right_a = lax.ppermute(half_a, "ctx", [(3, 2), (2, 1), (1, 0)])
    far_a = jnp.where(
        place >= 2,
        lax.ppermute(left_a, "ctx", [(1, 2), (2, 3)]),
        lax.ppermute(right_a, "ctx", [(2, 1), (1, 0)]),
    )
    full_qkv = fsdp_whole(w_qkv, 1)
    full_vectors = fsdp_whole(after(jnp.concatenate([gains, shifts]), full_qkv), 1).astype(f32)
    own_out = fsdp_whole(after(w_out, full_qkv), 1)
    full_up = fsdp_whole(after(w_up, own_out), 0)
    full_down = fsdp_whole(after(w_down, full_up), 1)
    gain = full_vectors[:2]
    shift = full_vectors[2:]

    positions = jnp.stack([t ^ r for r in order]) * quarter
    chunks = jnp.stack([place, place - 1, place + 1, place ^ 2]) * tok_rows
    info = jnp.concatenate(
        [
            jnp.cumsum(lengths[0]),
            place * tok_rows + positions,
            (chunks[:, None] + positions[None, :]).reshape(-1),
        ]
    ).astype(jnp.int32)

    w_q, w_k, w_v = full_qkv[0], full_qkv[1], full_qkv[2]
    chunk_rows = [
        jnp.concatenate([half_a, half_b]),
        jnp.concatenate([left_a, tp_swap(left_a, 1)]),
        jnp.concatenate([right_a, tp_swap(right_a, 1)]),
        jnp.concatenate([far_a, tp_swap(far_a, 1)]),
    ]
    queries = nn(chunk_rows[0], w_q).astype(bf16)
    keys = jnp.concatenate([nn(rows, w_k).astype(bf16) for rows in chunk_rows])
    values_t = jnp.concatenate(
        [contract(w_v, rows, 0, 1).astype(bf16) for rows in chunk_rows], axis=1
    )
    context, log_totals = attend(info, queries, keys, values_t)

    out_y = tp_swap(own_out, 2)
    out_all = jnp.concatenate([own_out, out_y, tp_swap(own_out, 1), tp_swap(out_y, 1)])
    pieces = jnp.split(context, 4)
    context_own = jnp.concatenate(
        [pieces[0]] + [tp_swap(pieces[n], order[n]) for n in (1, 2, 3)], axis=1
    )
    resid_rows = quarter_of(tokens, 0).astype(f32) + nn(context_own, out_all)
    normed_first, inverse_first = norm_rows(resid_rows)
    hidden = normed_first * gain[0] + shift[0]
    hid0, hid1, hid2, hid3 = rows_out(hidden.astype(bf16))
    hid_near, hid_far = jnp.concatenate([hid0, hid1]), jnp.concatenate([hid2, hid3])

    act_near, slope_near = gelu_pair(nn(hid_near, full_up))
    act_far, slope_far = gelu_pair(nn(hid_far, full_up))
    terms_far = nn(act_far, full_down)
    terms_near = nn(act_near, full_down)
    ffn_rows = rows_in(
        (terms_near[:quarter], terms_near[quarter:], terms_far[:quarter], terms_far[quarter:])
    )
    normed_second, inverse_second = norm_rows(hidden + ffn_rows)
    result = (normed_second * gain[1] + shift[1]).astype(bf16)
    grad_rows = quarter_of(out_grad, 0).astype(f32)
    grad_mid = norm_back(grad_rows, gain[1], normed_second, inverse_second)

    mid0, mid1, mid2, mid3 = rows_out(grad_mid.astype(bf16))
    result_parts = rows_out(after(result, mid2))
    mid_near, mid_far = jnp.concatenate([mid0, mid1]), jnp.concatenate([mid2, mid3])
    pre_near = (nt(mid_near, full_down) * slope_near).astype(bf16)
    pre_far = (nt(mid_far, full_down) * slope_far).astype(bf16)
    terms_far = nt(pre_far, full_up)
    terms_near = nt(pre_near, full_up)
    hidden_grad = grad_mid + rows_in(
        (terms_near[:quarter], terms_near[quarter:], terms_far[:quarter], terms_far[quarter:])
    )

    act_all = jnp.concatenate([act_near, act_far])
    mid_all = jnp.concatenate([mid_near, mid_far])
    hid_all = jnp.concatenate([hid_near, hid_far])
    pre_all = jnp.concatenate([pre_near, pre_far])

    def column_block(left, right):
        return lambda start, size: tn(left, lax.dynamic_slice_in_dim(right, start, size, axis=1))

    def row_block(left, right):
        return lambda start, size: tn(lax.dynamic_slice_in_dim(left, start, size, axis=1), right)

    down_grad = ctx_total(fsdp_total(column_block(act_all, mid_all), depth, 1))
    up_grad = ctx_total(fsdp_total(row_block(hid_all, pre_all), depth, 0))

    resid_grad = norm_back(hidden_grad, gain[0], normed_first, inverse_first)
    attn_own = resid_grad.astype(bf16)
    back_own = nt(attn_own, out_all).astype(bf16)
    pieces = jnp.split(back_own, 4, axis=1)
    context_grad = jnp.concatenate(
        [pieces[0]] + [tp_swap(pieces[n], order[n]) for n in (1, 2, 3)]
    )
    attn0, attn1, attn2, attn3 = rows_out(after(attn_own, context_grad))
    attn_all = jnp.concatenate([attn0, attn2, attn1, attn3])
    out_proj_grad = ctx_total(fsdp_total(column_block(context, attn_all), depth, 1))

    vectors = jnp.stack(
        [
            jnp.sum(hidden_grad * normed_first, axis=0),
            jnp.sum(grad_rows * normed_second, axis=0),
            jnp.sum(hidden_grad, axis=0),
            jnp.sum(grad_rows, axis=0),
        ]
    )
    vectors = vectors + tp_swap(vectors, 1)
    vectors = vectors + tp_swap(vectors, 2)
    vectors = vectors + lax.ppermute(vectors, "ctx", [(i, i ^ 1) for i in range(4)])
    vectors = vectors + lax.ppermute(vectors, "ctx", [(i, i ^ 2) for i in range(4)])
    if lax.axis_size("fsdp") == 2:
        half = depth // 2
        mine = lax.axis_index("fsdp")
        sent = lax.dynamic_slice_in_dim(vectors, (1 - mine) * half, half, axis=1)
        vectors = lax.dynamic_slice_in_dim(vectors, mine * half, half, axis=1) + lax.ppermute(
            sent, "fsdp", [(0, 1), (1, 0)]
        )
    else:
        vectors = lax.psum_scatter(vectors, "fsdp", scatter_dimension=1, tiled=True)

    values = values_t.T
    keys_t = keys.T
    query_grad, own_kv, left_kv, right_kv, far_kv = attend_back(
        info, queries, context_grad, context, log_totals, keys, values, keys_t
    )
    rows_all = jnp.concatenate(chunk_rows)

    def key_total(n):
        grads = jnp.concatenate([own_kv[n], left_kv[n], right_kv[n], far_kv[n]])
        return fsdp_total(row_block(rows_all, grads), depth, 0)

    qkv_grad = jnp.stack(
        [
            ctx_total(fsdp_total(row_block(chunk_rows[0], query_grad), depth, 0)),
            ctx_total(key_total(0)),
            ctx_total(key_total(1)),
        ]
    )
    left_sum = left_kv.astype(f32) + lax.ppermute(far_kv, "ctx", [(2, 1), (3, 2)]).astype(f32)
    right_sum = right_kv.astype(f32) + lax.ppermute(far_kv, "ctx", [(0, 1), (1, 2)]).astype(f32)
    key_values = (
        own_kv.astype(f32)
        + lax.ppermute(left_sum.astype(bf16), "ctx", [(3, 2), (2, 1), (1, 0)]).astype(f32)
        + lax.ppermute(right_sum.astype(bf16), "ctx", [(0, 1), (1, 2), (2, 3)]).astype(f32)
    ).astype(bf16)
    terms = nt(query_grad, w_q) + nt(key_values[0], w_k) + nt(key_values[1], w_v)
    q0, q2, q1, q3 = jnp.split(terms, 4)
    input_own = (resid_grad + rows_in((q0, q1, q2, q3))).astype(bf16)
    return (
        natural(result_parts, core, y),
        natural(rows_out(input_own), core, y),
        qkv_grad,
        out_proj_grad,
        up_grad,
        down_grad,
        vectors[:2],
        vectors[2:],
    )


def solution(mesh):
    return jax.shard_map(
        body,
        mesh=mesh,
        in_specs=(
            P(("fsdp", "ctx"), None),
            P(None, "fsdp", "tp"),
            P("tp", "fsdp"),
            P("fsdp", "tp"),
            P("tp", "fsdp"),
            P(None, "fsdp"),
            P(None, "fsdp"),
            P("fsdp", None),
            P(("fsdp", "ctx"), None),
        ),
        out_specs=(
            P(("fsdp", "ctx"), None),
            P(("fsdp", "ctx"), None),
            P(None, "fsdp", "tp"),
            P("tp", "fsdp"),
            P("fsdp", "tp"),
            P("tp", "fsdp"),
            P(None, "fsdp"),
            P(None, "fsdp"),
        ),
        check_vma=False,
    )
```

time: 1670 us -> 620 us (0.37)
  waiting for transfers between devices: 1030 us -> 256 us
  matrix products: 465 us -> 60.8 us
  starting transfers between devices: 1.14 us -> 171 us
  Pallas kernels: 0 us -> 58.9 us
  other arithmetic: 71.4 us -> 34.5 us
  blocking collectives: 30.3 us -> 0 us
  local copies, waits for them, and re-layouts: 51.7 us -> 27.7 us
    psum x5 -> x0, waiting for transfers between devices: 541 us -> none  [the longest x4 319 us: tp_total(): return lax.psum(terms, 'tp')]
    dot_general x26 -> x34, matrix products: 465 us -> 60.8 us  [contract(): lax.dot_general(left, right, (((left_dim,), (right_dim,)), ((), ())), pre...]
    reduce_scatter x6 -> x0, waiting for transfers between devices: 294 us -> none  [the longest x1 78.2 us: body(): lax.psum_scatter(key_grad.reshape(pack_rows, local_width), 'ctx', scatter...]
    ppermute x0 -> x78, waiting for transfers between devices: none -> 256 us  [the longest x6 73.4 us: ctx_total(): back = lax.ppermute(total, 'ctx', [(1, 0), (2, 3)])]
    ppermute x0 -> x78, starting transfers between devices: none -> 171 us  [the longest x6 63.1 us: ctx_total(): got = lax.ppermute(sent, 'ctx', [(0, 1), (3, 2)])]
    all_gather x5 -> x0, waiting for transfers between devices: 161 us -> none  [the longest x1 46.9 us: body(): lax.all_gather(projected[2], 'ctx', axis=0, tiled=True)]
    pallas_call x0 -> x2, Pallas kernels: none -> 58.9 us  [the longest x1 33.6 us: attend_back(): pl.pallas_call(functools.partial(attend_back_kernel, heads, qcount, kcoun...]
    reduce_sum x11 -> x5, other arithmetic: 53.1 us -> 3.9 us  [the longest x1 2.33 us: body(): jnp.sum(hidden_grad * normed_first, axis=0)]
  transfers between devices with their start and end apart: 18 -> 78, of which waited for: 18 -> 29; matrix products, arithmetic and copies ran while one was open for 4% -> 17% of each run, Pallas kernels for 0% -> 10%
where the time goes in v1:
time: 620 us; the launch traced here: 611 us
  waiting for transfers between devices  256 us (41%)
  starting transfers between devices  171 us (28%)
  matrix products  60.8 us (10%)
  Pallas kernels  58.9 us (10%)
  other arithmetic  34.5 us (6%)
  local copies, waits for them, and re-layouts  27.7 us (4%)
    ppermute x6, waiting for transfers between devices, ctx_total(): back = lax.ppermute(total, 'ctx', [(1, 0), (2, 3)])  73.4 us
    ppermute x6, starting transfers between devices, ctx_total(): got = lax.ppermute(sent, 'ctx', [(0, 1), (3, 2)])  63.1 us
    ppermute x38, waiting for transfers between devices, tp_swap(): return lax.ppermute(x, 'tp', [(i, i ^ bit) for i in range(4)])  62.7 us
    dot_general x34, matrix products, contract(): lax.dot_general(left, right, (((left_dim,), (right_dim,)), ((), ())), pre...  60.8 us
    ppermute x5, waiting for transfers between devices, fsdp_whole(): other = lax.ppermute(shard, 'fsdp', [(0, 1), (1, 0)])  46.3 us
    ppermute x6, waiting for transfers between devices, fsdp_total(): got = lax.ppermute(sent, 'fsdp', [(0, 1), (1, 0)])  35.3 us
    pallas_call x1, Pallas kernels, attend_back(): pl.pallas_call(functools.partial(attend_back_kernel, heads, qcount, kcoun...  33.6 us
    ppermute x6, waiting for transfers between devices, ctx_total(): got = lax.ppermute(sent, 'ctx', [(0, 1), (3, 2)])  27.1 us
  transfers between devices with their start and end apart: 78, of which 29 were waited for; matrix products, arithmetic and copies ran while one was open for 17% of the time, Pallas kernels for 10%

profile of v1, /device:TPU:0, one launch (start us, length us, event | category | flops | bytes accessed | tf_op | source)
XLA Modules:
  0.0 611.4 jit_solution(17831791095076808330)
XLA Ops:
  7.1 6.5 %collective-permute-start.1 = (bf16[512,1024]{1,0:T(8,128)(2,1)}, bf16[512,1024]{1,0:T(8,128)(2,1)}, u32[]{:S(2)}, u32[]{:S(2)}) collective-permute-start(bf16[512,1024]{1,0:T(8,128)(2,1)} %pad_maximum_fusion.26), channel_id=1, source_target_pairs={{0,4},{4,8},{8,12},{1,5},{5,9},{9,13},{2,6},{6,10},{10,14},{3,7},{... | collective-permute-start | bytes 3145736 | tf_op jit(solution)/shard_map/ppermute | solution.py:353
  18.8 14.2 %collective-permute-done = bf16[3,512,256]{2,1,0:T(8,128)(2,1)} collective-permute-done((bf16[3,512,256]{2,1,0:T(8,128)(2,1)}, bf16[3,512,256]{2,1,0:T(8,128)(2,1)}, u32[]{:S(2)}, u32[]{:S(2)}) %collective-permute-start) | collective-permute-done | bytes 786464 | tf_op jit(solution)/shard_map/ppermute | solution.py:268
  51.2 4.0 collective-permute-done.12
  60.5 9.0 %collective-permute-done.6 = bf16[512,1024]{1,0:T(8,128)(2,1)S(1)} collective-permute-done((bf16[512,1024]{1,0:T(8,128)(2,1)}, bf16[512,1024]{1,0:T(8,128)(2,1)S(1)}, u32[]{:S(2)}, u32[]{:S(2)}) %collective-permute-start.6) | collective-permute-done | bytes 1048608 | tf_op jit(solution)/shard_map/ppermute | solution.py:358
  88.7 25.3 %attend.1 = (bf16[1024,256]{1,0:T(8,128)(2,1)}, f32[4,1024]{1,0:T(4,128)}) custom-call(s32[23]{0:T(128)} %pad_add_fusion.info, bf16[1024,256]{1,0:T(8,128)(2,1)} %convolution_convert_fusion.9.q_ref, bf16[4096,256]{1,0:T(8,128)(2,1)} %copy.25.k_ref, bf16[256,4096]{1,0:T(8,128)(2,1)} %copy.26.vt_ref), custom_call_target="tpu_custom_call" | custom-call | flops 8589934592 | bytes 4194304 | tf_op jit(solution)/shard_map/attend/pallas_call | solution.py:118
  117.4 16.4 %collective-permute-start.18 = (bf16[1024,512]{1,0:T(8,128)(2,1)S(1)}, bf16[1024,512]{1,0:T(8,128)(2,1)S(1)}, u32[]{:S(2)}, u32[]{:S(2)}) collective-permute-start(bf16[1024,512]{1,0:T(8,128)(2,1)S(1)} %copy-done.18), channel_id=1, source_target_pairs={{0,16},{16,0},{1,17},{17,1},{2,18},{18,2},{3,19},{19,3},{4,20},{20... | collective-permute-start | bytes 3145736 | tf_op jit(solution)/shard_map/ppermute | solution.py:268
  137.4 13.3 %collective-permute-done.20 = bf16[256,1024]{1,0:T(8,128)(2,1)S(1)} collective-permute-done((bf16[256,1024]{1,0:T(8,128)(2,1)S(1)}, bf16[256,1024]{1,0:T(8,128)(2,1)S(1)}, u32[]{:S(2)}, u32[]{:S(2)}) %collective-permute-start.20) | collective-permute-done | bytes 524320 | tf_op jit(solution)/shard_map/ppermute | solution.py:258
  150.7 7.1 %collective-permute-done.18 = bf16[1024,512]{1,0:T(8,128)(2,1)S(1)} collective-permute-done((bf16[1024,512]{1,0:T(8,128)(2,1)S(1)}, bf16[1024,512]{1,0:T(8,128)(2,1)S(1)}, u32[]{:S(2)}, u32[]{:S(2)}) %collective-permute-start.18) | collective-permute-done | bytes 1048608 | tf_op jit(solution)/shard_map/ppermute | solution.py:268
  157.9 21.9 %collective-permute-done.17 = bf16[512,1024]{1,0:T(8,128)(2,1)S(1)} collective-permute-done((bf16[512,1024]{1,0:T(8,128)(2,1)}, bf16[512,1024]{1,0:T(8,128)(2,1)S(1)}, u32[]{:S(2)}, u32[]{:S(2)}) %collective-permute-start.17) | collective-permute-done | bytes 1048608 | tf_op jit(solution)/shard_map/ppermute | solution.py:268
  193.0 12.7 %collective-permute-done.23 = bf16[256,1024]{1,0:T(8,128)(2,1)S(1)} collective-permute-done((bf16[256,1024]{1,0:T(8,128)(2,1)S(1)}, bf16[256,1024]{1,0:T(8,128)(2,1)S(1)}, u32[]{:S(2)}, u32[]{:S(2)}) %collective-permute-start.23) | collective-permute-done | bytes 524320 | tf_op jit(solution)/shard_map/ppermute | solution.py:258
  208.0 13.1 %collective-permute-done.24 = bf16[256,1024]{1,0:T(8,128)(2,1)} collective-permute-done((bf16[256,1024]{1,0:T(8,128)(2,1)S(1)}, bf16[256,1024]{1,0:T(8,128)(2,1)}, u32[]{:S(2)}, u32[]{:S(2)}) %collective-permute-start.24) | collective-permute-done | bytes 524320 | tf_op jit(solution)/shard_map/ppermute | solution.py:258
  240.1 17.4 %collective-permute-done.65 = bf16[512,1024]{1,0:T(8,128)(2,1)S(1)} collective-permute-done((bf16[512,1024]{1,0:T(8,128)(2,1)S(1)}, bf16[512,1024]{1,0:T(8,128)(2,1)S(1)}, u32[]{:S(2)}, u32[]{:S(2)}) %collective-permute-start.65) | collective-permute-done | bytes 1048608 | tf_op jit(solution)/shard_map/ppermute | solution.py:282
  260.4 9.1 %collective-permute-start.66 = (bf16[512,1024]{1,0:T(8,128)(2,1)}, bf16[512,1024]{1,0:T(8,128)(2,1)}, u32[]{:S(2)}, u32[]{:S(2)}) collective-permute-start(bf16[512,1024]{1,0:T(8,128)(2,1)} %get-tuple-element.132), channel_id=1, source_target_pairs={{0,4},{12,8},{1,5},{13,9},{2,6},{14,10},{3,7},{15,11},{16,20},{28,... | collective-permute-start | bytes 3145736 | tf_op jit(solution)/shard_map/ppermute | solution.py:289
  269.6 10.0 %collective-permute-done.69 = bf16[1024,512]{1,0:T(8,128)(2,1)S(1)} collective-permute-done((bf16[1024,512]{1,0:T(8,128)(2,1)S(1)}, bf16[1024,512]{1,0:T(8,128)(2,1)S(1)}, u32[]{:S(2)}, u32[]{:S(2)}) %collective-permute-start.69) | collective-permute-done | bytes 1048608 | tf_op jit(solution)/shard_map/ppermute | solution.py:282
  290.0 6.2 %collective-permute-start.75 = (f32[4,1024]{1,0:T(4,128)S(1)}, f32[4,1024]{1,0:T(4,128)S(1)}, u32[]{:S(2)}, u32[]{:S(2)}) collective-permute-start(f32[4,1024]{1,0:T(4,128)S(1)} %fusion.160), channel_id=1, source_target_pairs={{0,4},{4,0},{8,12},{12,8},{1,5},{5,1},{9,13},{13,9},{2,6},{6,2},{1... | collective-permute-start | bytes 49160 | tf_op jit(solution)/shard_map/ppermute | solution.py:462
  297.9 8.2 %collective-permute-start.76 = (f32[4,1024]{1,0:T(4,128)S(1)}, f32[4,1024]{1,0:T(4,128)S(1)}, u32[]{:S(2)}, u32[]{:S(2)}) collective-permute-start(f32[4,1024]{1,0:T(4,128)S(1)} %add.297), channel_id=1, source_target_pairs={{0,8},{4,12},{8,0},{12,4},{1,9},{5,13},{9,1},{13,5},{2,10},{6,14},... | collective-permute-start | bytes 49160 | tf_op jit(solution)/shard_map/ppermute | solution.py:463
  320.7 33.6 %attend_back.1 = (bf16[1024,256]{1,0:T(8,128)(2,1)}, bf16[2,1024,256]{2,1,0:T(8,128)(2,1)}, bf16[2,1024,256]{2,1,0:T(8,128)(2,1)}, bf16[2,1024,256]{2,1,0:T(8,128)(2,1)}, bf16[2,1024,256]{2,1,0:T(8,128)(2,1)}) custom-call(s32[23]{0:T(128)} %pad_add_fusion.info, bf16[1024,256]{1,0:T(8,128)(2,1)} %convolution_convert_fusion.9.q_ref, ...), custom_call_target="tpu_custom_call" | custom-call | flops 21474836480 | bytes 8388608 | tf_op jit(solution)/shard_map/attend_back/pallas_call | solution.py:220
  356.3 20.8 %collective-permute-start.46 = (bf16[512,256]{1,0:T(8,128)(2,1)S(1)}, bf16[512,256]{1,0:T(8,128)(2,1)S(1)}, u32[]{:S(2)}, u32[]{:S(2)}) collective-permute-start(bf16[512,256]{1,0:T(8,128)(2,1)S(1)} %convolution_convert_fusion.11), channel_id=1, source_target_pairs={{0,16},{16,0},{1,17},{17,1},{2,18},{18,2},{3,19},{19,3},{4,20},{20... | collective-permute-start | bytes 786440 | tf_op jit(solution)/shard_map/ppermute | solution.py:282
  378.8 3.5 fusion.24
  382.4 3.6 fusion.21
  393.5 3.5 fusion.127
  403.6 4.4 collective-permute-start.38
  413.0 44.9 %collective-permute-start.70 = (bf16[1024,512]{1,0:T(8,128)(2,1)S(1)}, bf16[1024,512]{1,0:T(8,128)(2,1)S(1)}, u32[]{:S(2)}, u32[]{:S(2)}) collective-permute-start(bf16[1024,512]{1,0:T(8,128)(2,1)S(1)} %copy-done.45), channel_id=1, source_target_pairs={{0,4},{12,8},{1,5},{13,9},{2,6},{14,10},{3,7},{15,11},{16,20},{28,... | collective-permute-start | bytes 3145736 | tf_op jit(solution)/shard_map/ppermute | solution.py:289
  458.7 3.8 collective-permute-start.39
  467.6 5.8 collective-permute-done.61
  475.1 6.4 %collective-permute-done.70 = bf16[1024,512]{1,0:T(8,128)(2,1)S(1)} collective-permute-done((bf16[1024,512]{1,0:T(8,128)(2,1)S(1)}, bf16[1024,512]{1,0:T(8,128)(2,1)S(1)}, u32[]{:S(2)}, u32[]{:S(2)}) %collective-permute-start.70) | collective-permute-done | bytes 1048608 | tf_op jit(solution)/shard_map/ppermute | solution.py:289
  481.5 4.4 collective-permute-start.62
  486.3 18.5 %collective-permute-done.62 = bf16[256,512]{1,0:T(8,128)(2,1)S(1)} collective-permute-done((bf16[256,512]{1,0:T(8,128)(2,1)S(1)}, bf16[256,512]{1,0:T(8,128)(2,1)S(1)}, u32[]{:S(2)}, u32[]{:S(2)}) %collective-permute-start.62) | collective-permute-done | bytes 262176 | tf_op jit(solution)/shard_map/ppermute | solution.py:289
  518.9 11.0 %collective-permute-done.42 = bf16[256,1024]{1,0:T(8,128)(2,1)S(1)} collective-permute-done((bf16[256,1024]{1,0:T(8,128)(2,1)S(1)}, bf16[256,1024]{1,0:T(8,128)(2,1)S(1)}, u32[]{:S(2)}, u32[]{:S(2)}) %collective-permute-start.42) | collective-permute-done | bytes 524320 | tf_op jit(solution)/shard_map/ppermute | solution.py:258
  531.5 16.8 %collective-permute-done.53 = bf16[512,256]{1,0:T(8,128)(2,1)S(1)} collective-permute-done((bf16[512,256]{1,0:T(8,128)(2,1)S(1)}, bf16[512,256]{1,0:T(8,128)(2,1)S(1)}, u32[]{:S(2)}, u32[]{:S(2)}) %collective-permute-start.53) | collective-permute-done | bytes 262176 | tf_op jit(solution)/shard_map/ppermute | solution.py:293
  549.5 40.6 %collective-permute-done.64 = bf16[256,512]{1,0:T(8,128)(2,1)S(1)} collective-permute-done((bf16[256,512]{1,0:T(8,128)(2,1)S(1)}, bf16[256,512]{1,0:T(8,128)(2,1)S(1)}, u32[]{:S(2)}, u32[]{:S(2)}) %collective-permute-start.64) | collective-permute-done | bytes 262176 | tf_op jit(solution)/shard_map/ppermute | solution.py:293
  593.1 13.1 %collective-permute-done.72 = bf16[1024,512]{1,0:T(8,128)(2,1)S(1)} collective-permute-done((bf16[1024,512]{1,0:T(8,128)(2,1)S(1)}, bf16[1024,512]{1,0:T(8,128)(2,1)S(1)}, u32[]{:S(2)}, u32[]{:S(2)}) %collective-permute-start.72) | collective-permute-done | bytes 1048608 | tf_op jit(solution)/shard_map/ppermute | solution.py:293
  (367 shorter events, 179.4 us)
Async XLA Ops:
  5.8 39.4 %collective-permute-start.3 = (bf16[512,1024]{1,0:T(8,128)(2,1)}, bf16[512,1024]{1,0:T(8,128)(2,1)}, u32[]{:S(2)}, u32[]{:S(2)}) collective-permute-start(bf16[512,1024]{1,0:T(8,128)(2,1)} %pad_maximum_fusion.26), channel_id=1, source_target_pairs={{12,8},{8,4},{4,0},{13,9},{9,5},{5,1},{14,10},{10,6},{6,2},{15,11}... | collective-permute-start | bytes 3145736 | tf_op jit(solution)/shard_map/ppermute | solution.py:354
  7.1 32.4 %collective-permute-start.1 = (bf16[512,1024]{1,0:T(8,128)(2,1)}, bf16[512,1024]{1,0:T(8,128)(2,1)}, u32[]{:S(2)}, u32[]{:S(2)}) collective-permute-start(bf16[512,1024]{1,0:T(8,128)(2,1)} %pad_maximum_fusion.26), channel_id=1, source_target_pairs={{0,4},{4,8},{8,12},{1,5},{5,9},{9,13},{2,6},{6,10},{10,14},{3,7},{... | collective-permute-start | bytes 3145736 | tf_op jit(solution)/shard_map/ppermute | solution.py:353
  45.2 24.3 %collective-permute-start.6 = (bf16[512,1024]{1,0:T(8,128)(2,1)}, bf16[512,1024]{1,0:T(8,128)(2,1)S(1)}, u32[]{:S(2)}, u32[]{:S(2)}) collective-permute-start(bf16[512,1024]{1,0:T(8,128)(2,1)} %collective-permute-done.3), channel_id=1, source_target_pairs={{8,4},{4,0},{9,5},{5,1},{10,6},{6,2},{11,7},{7,3},{24,20},{20,16},... | collective-permute-start | bytes 3145736 | tf_op jit(solution)/shard_map/ppermute | solution.py:358
  46.6 23.0 %collective-permute-start.5 = (bf16[512,1024]{1,0:T(8,128)(2,1)}, bf16[512,1024]{1,0:T(8,128)(2,1)S(1)}, u32[]{:S(2)}, u32[]{:S(2)}) collective-permute-start(bf16[512,1024]{1,0:T(8,128)(2,1)} %collective-permute-done.1), channel_id=1, source_target_pairs={{4,8},{8,12},{5,9},{9,13},{6,10},{10,14},{7,11},{11,15},{20,24},{2... | collective-permute-start | bytes 3145736 | tf_op jit(solution)/shard_map/ppermute | solution.py:357
  55.3 62.1 %collective-permute-start.13 = (bf16[256,1024]{1,0:T(8,128)(2,1)}, bf16[256,1024]{1,0:T(8,128)(2,1)}, u32[]{:S(2)}, u32[]{:S(2)}) collective-permute-start(bf16[256,1024]{1,0:T(8,128)(2,1)} %pad_maximum_fusion.27), channel_id=1, source_target_pairs={{0,1},{1,0},{2,3},{3,2},{4,5},{5,4},{6,7},{7,6},{8,9},{9,8},{10,11... | collective-permute-start | bytes 1572872 | tf_op jit(solution)/shard_map/ppermute | solution.py:258
  55.3 78.6 %collective-permute-start.14 = (bf16[256,1024]{1,0:T(8,128)(2,1)}, bf16[256,1024]{1,0:T(8,128)(2,1)}, u32[]{:S(2)}, u32[]{:S(2)}) collective-permute-start(bf16[256,1024]{1,0:T(8,128)(2,1)} %collective-permute-done.12), channel_id=1, source_target_pairs={{0,1},{1,0},{2,3},{3,2},{4,5},{5,4},{6,7},{7,6},{8,9},{9,8},{10,11... | collective-permute-start | bytes 1572872 | tf_op jit(solution)/shard_map/ppermute | solution.py:258
  117.4 40.4 %collective-permute-start.18 = (bf16[1024,512]{1,0:T(8,128)(2,1)S(1)}, bf16[1024,512]{1,0:T(8,128)(2,1)S(1)}, u32[]{:S(2)}, u32[]{:S(2)}) collective-permute-start(bf16[1024,512]{1,0:T(8,128)(2,1)S(1)} %copy-done.18), channel_id=1, source_target_pairs={{0,16},{16,0},{1,17},{17,1},{2,18},{18,2},{3,19},{19,3},{4,20},{20... | collective-permute-start | bytes 3145736 | tf_op jit(solution)/shard_map/ppermute | solution.py:268
  133.8 46.0 %collective-permute-start.17 = (bf16[512,1024]{1,0:T(8,128)(2,1)}, bf16[512,1024]{1,0:T(8,128)(2,1)S(1)}, u32[]{:S(2)}, u32[]{:S(2)}) collective-permute-start(bf16[512,1024]{1,0:T(8,128)(2,1)} %param.12), channel_id=1, source_target_pairs={{0,16},{16,0},{1,17},{17,1},{2,18},{18,2},{3,19},{19,3},{4,20},{20... | collective-permute-start | bytes 3145736 | tf_op jit(solution)/shard_map/ppermute | solution.py:268
  150.7 30.7 %collective-permute-start.21 = (bf16[256,1024]{1,0:T(8,128)(2,1)S(1)}, bf16[256,1024]{1,0:T(8,128)(2,1)S(1)}, u32[]{:S(2)}, u32[]{:S(2)}) collective-permute-start(bf16[256,1024]{1,0:T(8,128)(2,1)S(1)} %collective-permute-done.20), channel_id=1, source_target_pairs={{0,1},{1,0},{2,3},{3,2},{4,5},{5,4},{6,7},{7,6},{8,9},{9,8},{10,11... | collective-permute-start | bytes 1572872 | tf_op jit(solution)/shard_map/ppermute | solution.py:258
  231.4 26.0 %collective-permute-start.65 = (bf16[512,1024]{1,0:T(8,128)(2,1)S(1)}, bf16[512,1024]{1,0:T(8,128)(2,1)S(1)}, u32[]{:S(2)}, u32[]{:S(2)}) collective-permute-start(bf16[512,1024]{1,0:T(8,128)(2,1)S(1)} %convolution_convert_fusion.1), channel_id=1, source_target_pairs={{0,16},{16,0},{1,17},{17,1},{2,18},{18,2},{3,19},{19,3},{4,20},{20... | collective-permute-start | bytes 3145736 | tf_op jit(solution)/shard_map/ppermute | solution.py:282
  236.5 43.1 %collective-permute-start.69 = (bf16[1024,512]{1,0:T(8,128)(2,1)S(1)}, bf16[1024,512]{1,0:T(8,128)(2,1)S(1)}, u32[]{:S(2)}, u32[]{:S(2)}) collective-permute-start(bf16[1024,512]{1,0:T(8,128)(2,1)S(1)} %convolution_convert_fusion), channel_id=1, source_target_pairs={{0,16},{16,0},{1,17},{17,1},{2,18},{18,2},{3,19},{19,3},{4,20},{20... | collective-permute-start | bytes 3145736 | tf_op jit(solution)/shard_map/ppermute | solution.py:282
  239.2 43.2 %collective-permute-start.29 = (bf16[256,1024]{1,0:T(8,128)(2,1)S(1)}, bf16[256,1024]{1,0:T(8,128)(2,1)S(1)}, u32[]{:S(2)}, u32[]{:S(2)}) collective-permute-start(bf16[256,1024]{1,0:T(8,128)(2,1)S(1)} %slice.203), channel_id=1, source_target_pairs={{0,1},{1,0},{2,3},{3,2},{4,5},{5,4},{6,7},{7,6},{8,9},{9,8},{10,11... | collective-permute-start | bytes 1572872 | tf_op jit(solution)/shard_map/ppermute | solution.py:258
  239.5 43.0 %collective-permute-start.32 = (bf16[256,1024]{1,0:T(8,128)(2,1)S(1)}, bf16[256,1024]{1,0:T(8,128)(2,1)S(1)}, u32[]{:S(2)}, u32[]{:S(2)}) collective-permute-start(bf16[256,1024]{1,0:T(8,128)(2,1)S(1)} %fusion.35), channel_id=1, source_target_pairs={{0,2},{1,3},{2,0},{3,1},{4,6},{5,7},{6,4},{7,5},{8,10},{9,11},{10,... | collective-permute-start | bytes 1572872 | tf_op jit(solution)/shard_map/ppermute | solution.py:258
  260.4 204.4 %collective-permute-start.66 = (bf16[512,1024]{1,0:T(8,128)(2,1)}, bf16[512,1024]{1,0:T(8,128)(2,1)}, u32[]{:S(2)}, u32[]{:S(2)}) collective-permute-start(bf16[512,1024]{1,0:T(8,128)(2,1)} %get-tuple-element.132), channel_id=1, source_target_pairs={{0,4},{12,8},{1,5},{13,9},{2,6},{14,10},{3,7},{15,11},{16,20},{28,... | collective-permute-start | bytes 3145736 | tf_op jit(solution)/shard_map/ppermute | solution.py:289
  316.7 94.8 %collective-permute-start.59 = (bf16[256,1024]{1,0:T(8,128)(2,1)}, bf16[256,1024]{1,0:T(8,128)(2,1)S(1)}, u32[]{:S(2)}, u32[]{:S(2)}) collective-permute-start(bf16[256,1024]{1,0:T(8,128)(2,1)} %get-tuple-element.33), channel_id=1, source_target_pairs={{0,1},{1,0},{2,3},{3,2},{4,5},{5,4},{6,7},{7,6},{8,9},{9,8},{10,11... | collective-permute-start | bytes 1572872 | tf_op jit(solution)/shard_map/ppermute | solution.py:258
  317.2 93.5 %collective-permute-start.58 = (bf16[256,1024]{1,0:T(8,128)(2,1)}, bf16[256,1024]{1,0:T(8,128)(2,1)S(1)}, u32[]{:S(2)}, u32[]{:S(2)}) collective-permute-start(bf16[256,1024]{1,0:T(8,128)(2,1)} %get-tuple-element.33), channel_id=1, source_target_pairs={{0,2},{1,3},{2,0},{3,1},{4,6},{5,7},{6,4},{7,5},{8,10},{9,11},{10,... | collective-permute-start | bytes 1572872 | tf_op jit(solution)/shard_map/ppermute | solution.py:258
  356.3 30.5 %collective-permute-start.46 = (bf16[512,256]{1,0:T(8,128)(2,1)S(1)}, bf16[512,256]{1,0:T(8,128)(2,1)S(1)}, u32[]{:S(2)}, u32[]{:S(2)}) collective-permute-start(bf16[512,256]{1,0:T(8,128)(2,1)S(1)} %convolution_convert_fusion.11), channel_id=1, source_target_pairs={{0,16},{16,0},{1,17},{17,1},{2,18},{18,2},{3,19},{19,3},{4,20},{20... | collective-permute-start | bytes 786440 | tf_op jit(solution)/shard_map/ppermute | solution.py:282
  403.6 54.7 %collective-permute-start.38 = (bf16[2,1024,256]{2,1,0:T(8,128)(2,1)S(1)}, bf16[2,1024,256]{2,1,0:T(8,128)(2,1)S(1)}, u32[]{:S(2)}, u32[]{:S(2)}) collective-permute-start(bf16[2,1024,256]{2,1,0:T(8,128)(2,1)S(1)} %copy-done.30), channel_id=1, source_target_pairs={{0,4},{4,8},{1,5},{5,9},{2,6},{6,10},{3,7},{7,11},{16,20},{20,24},... | collective-permute-start | bytes 3145736 | tf_op jit(solution)/shard_map/ppermute | solution.py:493
  410.7 48.0 %collective-permute-start.36 = (bf16[2,1024,256]{2,1,0:T(8,128)(2,1)S(1)}, bf16[2,1024,256]{2,1,0:T(8,128)(2,1)S(1)}, u32[]{:S(2)}, u32[]{:S(2)}) collective-permute-start(bf16[2,1024,256]{2,1,0:T(8,128)(2,1)S(1)} %copy-done.30), channel_id=1, source_target_pairs={{8,4},{12,8},{9,5},{13,9},{10,6},{14,10},{11,7},{15,11},{24,20},{2... | collective-permute-start | bytes 3145736 | tf_op jit(solution)/shard_map/ppermute | solution.py:492
  412.3 45.8 %collective-permute-start.52 = (bf16[512,256]{1,0:T(8,128)(2,1)S(1)}, bf16[512,256]{1,0:T(8,128)(2,1)S(1)}, u32[]{:S(2)}, u32[]{:S(2)}) collective-permute-start(bf16[512,256]{1,0:T(8,128)(2,1)S(1)} %add_convert_fusion.13), channel_id=1, source_target_pairs={{4,8},{8,4},{5,9},{9,5},{6,10},{10,6},{7,11},{11,7},{20,24},{24,20... | collective-permute-start | bytes 786440 | tf_op jit(solution)/shard_map/ppermute | solution.py:291
  413.0 68.5 %collective-permute-start.70 = (bf16[1024,512]{1,0:T(8,128)(2,1)S(1)}, bf16[1024,512]{1,0:T(8,128)(2,1)S(1)}, u32[]{:S(2)}, u32[]{:S(2)}) collective-permute-start(bf16[1024,512]{1,0:T(8,128)(2,1)S(1)} %copy-done.45), channel_id=1, source_target_pairs={{0,4},{12,8},{1,5},{13,9},{2,6},{14,10},{3,7},{15,11},{16,20},{28,... | collective-permute-start | bytes 3145736 | tf_op jit(solution)/shard_map/ppermute | solution.py:289
  458.1 91.4 %collective-permute-start.25 = (bf16[256,1024]{1,0:T(8,128)(2,1)S(1)}, bf16[256,1024]{1,0:T(8,128)(2,1)S(1)}, u32[]{:S(2)}, u32[]{:S(2)}) collective-permute-start(bf16[256,1024]{1,0:T(8,128)(2,1)S(1)} %get-tuple-element.26), channel_id=1, source_target_pairs={{0,2},{1,3},{2,0},{3,1},{4,6},{5,7},{6,4},{7,5},{8,10},{9,11},{10,... | collective-permute-start | bytes 1572872 | tf_op jit(solution)/shard_map/ppermute | solution.py:258
  458.7 47.5 %collective-permute-start.39 = (bf16[2,1024,256]{2,1,0:T(8,128)(2,1)S(1)}, bf16[2,1024,256]{2,1,0:T(8,128)(2,1)S(1)}, u32[]{:S(2)}, u32[]{:S(2)}) collective-permute-start(bf16[2,1024,256]{2,1,0:T(8,128)(2,1)S(1)} %add_convert_fusion.5), channel_id=1, source_target_pairs={{0,4},{4,8},{8,12},{1,5},{5,9},{9,13},{2,6},{6,10},{10,14},{3,7},{... | collective-permute-start | bytes 3145736 | tf_op jit(solution)/shard_map/ppermute | solution.py:497
  462.9 44.2 %collective-permute-start.37 = (bf16[2,1024,256]{2,1,0:T(8,128)(2,1)S(1)}, bf16[2,1024,256]{2,1,0:T(8,128)(2,1)S(1)}, u32[]{:S(2)}, u32[]{:S(2)}) collective-permute-start(bf16[2,1024,256]{2,1,0:T(8,128)(2,1)S(1)} %add_convert_fusion.6), channel_id=1, source_target_pairs={{12,8},{8,4},{4,0},{13,9},{9,5},{5,1},{14,10},{10,6},{6,2},{15,11}... | collective-permute-start | bytes 3145736 | tf_op jit(solution)/shard_map/ppermute | solution.py:496
  473.3 36.7 %collective-permute-start.49 = (bf16[512,256]{1,0:T(8,128)(2,1)S(1)}, bf16[512,256]{1,0:T(8,128)(2,1)S(1)}, u32[]{:S(2)}, u32[]{:S(2)}) collective-permute-start(bf16[512,256]{1,0:T(8,128)(2,1)S(1)} %add_convert_fusion.14), channel_id=1, source_target_pairs={{4,0},{8,12},{5,1},{9,13},{6,2},{10,14},{7,3},{11,15},{20,16},{24,... | collective-permute-start | bytes 786440 | tf_op jit(solution)/shard_map/ppermute | solution.py:293
  481.5 23.3 %collective-permute-start.62 = (bf16[256,512]{1,0:T(8,128)(2,1)S(1)}, bf16[256,512]{1,0:T(8,128)(2,1)S(1)}, u32[]{:S(2)}, u32[]{:S(2)}) collective-permute-start(bf16[256,512]{1,0:T(8,128)(2,1)S(1)} %get-tuple-element.130), channel_id=1, source_target_pairs={{0,4},{12,8},{1,5},{13,9},{2,6},{14,10},{3,7},{15,11},{16,20},{28,... | collective-permute-start | bytes 786440 | tf_op jit(solution)/shard_map/ppermute | solution.py:289
  513.9 34.4 %collective-permute-start.53 = (bf16[512,256]{1,0:T(8,128)(2,1)S(1)}, bf16[512,256]{1,0:T(8,128)(2,1)S(1)}, u32[]{:S(2)}, u32[]{:S(2)}) collective-permute-start(bf16[512,256]{1,0:T(8,128)(2,1)S(1)} %add_convert_fusion.12), channel_id=1, source_target_pairs={{4,0},{8,12},{5,1},{9,13},{6,2},{10,14},{7,3},{11,15},{20,16},{24,... | collective-permute-start | bytes 786440 | tf_op jit(solution)/shard_map/ppermute | solution.py:293
  516.0 75.0 %collective-permute-start.68 = (bf16[512,1024]{1,0:T(8,128)(2,1)S(1)}, bf16[512,1024]{1,0:T(8,128)(2,1)S(1)}, u32[]{:S(2)}, u32[]{:S(2)}) collective-permute-start(bf16[512,1024]{1,0:T(8,128)(2,1)S(1)} %add_convert_fusion.2), channel_id=1, source_target_pairs={{4,0},{8,12},{5,1},{9,13},{6,2},{10,14},{7,3},{11,15},{20,16},{24,... | collective-permute-start | bytes 3145736 | tf_op jit(solution)/shard_map/ppermute | solution.py:293
  517.6 72.6 %collective-permute-start.64 = (bf16[256,512]{1,0:T(8,128)(2,1)S(1)}, bf16[256,512]{1,0:T(8,128)(2,1)S(1)}, u32[]{:S(2)}, u32[]{:S(2)}) collective-permute-start(bf16[256,512]{1,0:T(8,128)(2,1)S(1)} %add_convert_fusion.8), channel_id=1, source_target_pairs={{4,0},{8,12},{5,1},{9,13},{6,2},{10,14},{7,3},{11,15},{20,16},{24,... | collective-permute-start | bytes 786440 | tf_op jit(solution)/shard_map/ppermute | solution.py:293
  529.9 76.3 %collective-permute-start.72 = (bf16[1024,512]{1,0:T(8,128)(2,1)S(1)}, bf16[1024,512]{1,0:T(8,128)(2,1)S(1)}, u32[]{:S(2)}, u32[]{:S(2)}) collective-permute-start(bf16[1024,512]{1,0:T(8,128)(2,1)S(1)} %add_convert_fusion), channel_id=1, source_target_pairs={{4,0},{8,12},{5,1},{9,13},{6,2},{10,14},{7,3},{11,15},{20,16},{24,... | collective-permute-start | bytes 3145736 | tf_op jit(solution)/shard_map/ppermute | solution.py:293
  548.2 43.3 %collective-permute-start.43 = (bf16[256,1024]{1,0:T(8,128)(2,1)S(1)}, bf16[256,1024]{1,0:T(8,128)(2,1)S(1)}, u32[]{:S(2)}, u32[]{:S(2)}) collective-permute-start(bf16[256,1024]{1,0:T(8,128)(2,1)S(1)} %fusion.34), channel_id=1, source_target_pairs={{0,2},{1,3},{2,0},{3,1},{4,6},{5,7},{6,4},{7,5},{8,10},{9,11},{10,... | collective-permute-start | bytes 1572872 | tf_op jit(solution)/shard_map/ppermute | solution.py:258
  549.5 58.0 %collective-permute-start.27 = (bf16[256,1024]{1,0:T(8,128)(2,1)S(1)}, bf16[256,1024]{1,0:T(8,128)(2,1)S(1)}, u32[]{:S(2)}, u32[]{:S(2)}) collective-permute-start(bf16[256,1024]{1,0:T(8,128)(2,1)S(1)} %get-tuple-element.26), channel_id=1, source_target_pairs={{0,1},{1,0},{2,3},{3,2},{4,5},{5,4},{6,7},{7,6},{8,9},{9,8},{10,11... | collective-permute-start | bytes 1572872 | tf_op jit(solution)/shard_map/ppermute | solution.py:258
  (99 other events, 1037.6 us)

commit v2 on v1

v2 whole, which is shorter than its diff:
```python
import functools
import math

import jax
import jax.numpy as jnp
from jax import lax
from jax.experimental import pallas as pl
from jax.experimental.pallas import tpu as pltpu
from jax.sharding import PartitionSpec as P

HEAD_DIM = 64
BLK = 256
LOW = -1e30
norm_eps = 1e-12
f32 = jnp.float32
bf16 = jnp.bfloat16


def contract(left, right, left_dim, right_dim):
    return lax.dot_general(
        left, right, (((left_dim,), (right_dim,)), ((), ())), preferred_element_type=f32
    )


def nn(left, right):
    return contract(left, right, 1, 0)


def nt(left, right):
    return contract(left, right, 1, 1)


def tn(left, right):
    return contract(left, right, 0, 0)


def row_limits(info, qbase, rows):
    end0, end1, end2 = info[0], info[1], info[2]
    pos = qbase + lax.broadcasted_iota(jnp.int32, (1, rows), 1)
    first = jnp.where(pos < end0, 0, jnp.where(pos < end1, end0, end1))
    last = jnp.where(pos < end0, end0, jnp.where(pos < end1, end1, end2))
    real = pos < end2
    return jnp.where(real, first, 0), jnp.where(real, last, 0), real


def key_range(info, qbase, rows):
    end0, end1, end2 = info[0], info[1], info[2]
    low = jnp.where(
        qbase < end0,
        0,
        jnp.where(qbase < end1, end0, jnp.where(qbase < end2, end1, 1 << 30)),
    )
    final = qbase + rows - 1
    high = jnp.where(final < end0, end0, jnp.where(final < end1, end1, end2))
    return low, high


def stage(sources, offsets, width, k_sc, v_sc, sems):
    copies = []
    start = 0
    for n, (source, (k_at, v_at)) in enumerate(zip(sources, offsets)):
        size = source.shape[0]
        for m, (at, target) in enumerate(((k_at, k_sc), (v_at, v_sc))):
            copies.append(
                pltpu.make_async_copy(
                    source.at[:, pl.ds(at, width)],
                    target.at[pl.ds(start, size), :],
                    sems.at[2 * n + m],
                )
            )
        start += size
    for copy in copies:
        copy.start()
    for copy in copies:
        copy.wait()


def transposed(source, target, count):
    def step(j, carry):
        span = pl.ds(pl.multiple_of(j * BLK, BLK), BLK)
        target[:, span] = source[span, :].T
        return carry

    lax.fori_loop(0, count, step, 0)


def masked_heads(block, target, heads):
    rows = block.shape[0]
    head_of = lax.broadcasted_iota(jnp.int32, block.shape, 1) // HEAD_DIM
    for h in range(heads):
        target[h * rows : (h + 1) * rows, :] = jnp.where(head_of == h, block, jnp.zeros_like(block))


def attend_kernel(heads, kcount, kfirst, opens, closes, offsets, info, q_ref, *refs):
    count = len(offsets)
    sources, refs = refs[:count], refs[count:]
    if not opens:
        (m_in, l_in, acc_in), refs = refs[:3], refs[3:]
    if closes:
        (ctx_ref, lse_ref), refs = refs[:2], refs[2:]
    else:
        (m_out, l_out, acc_out), refs = refs[:3], refs[3:]
    m_sc, l_sc, acc_sc, qm_sc, k_sc, v_sc, vt_sc, sems = refs
    i = pl.program_id(0)
    rows, width = q_ref.shape
    qbase = info[3 + i]
    first, last, real = row_limits(info, qbase, rows)
    low, high = key_range(info, qbase, rows)
    factor = math.log2(math.e) / math.sqrt(HEAD_DIM)

    @pl.when(i == 0)
    def _():
        stage(sources, offsets, width, k_sc, v_sc, sems)
        transposed(v_sc, vt_sc, kcount)

    if opens:
        m_sc[...] = jnp.full_like(m_sc, LOW)
        l_sc[...] = jnp.zeros_like(l_sc)
        acc_sc[...] = jnp.zeros_like(acc_sc)
    else:
        m_sc[...] = m_in[...]
        l_sc[...] = l_in[...]
        acc_sc[...] = acc_in[...]
    masked_heads(q_ref[...], qm_sc, heads)
    span_of = [slice(h * HEAD_DIM, (h + 1) * HEAD_DIM) for h in range(heads)]

    def step(j, carry):
        base = info[kfirst + j]

        @pl.when((base + BLK > low) & (base < high))
        def _():
            span = pl.ds(pl.multiple_of(j * BLK, BLK), BLK)
            kb = k_sc[span, :]
            vt = vt_sc[:, span]
            posk = base + lax.broadcasted_iota(jnp.int32, (BLK, rows), 0)
            allowed = (posk >= first) & (posk < last)
            s = [
                jnp.where(allowed, nt(kb, qm_sc[h * rows : (h + 1) * rows, :]) * factor, LOW)
                for h in range(heads)
            ]
            m_old = m_sc[...]
            m_new = [
                jnp.maximum(m_old[h : h + 1, :], jnp.max(s[h], axis=0, keepdims=True))
                for h in range(heads)
            ]
            alpha = [jnp.exp2(m_old[h : h + 1, :] - m_new[h]) for h in range(heads)]
            p = [jnp.exp2(s[h] - m_new[h]) for h in range(heads)]
            sums = [jnp.sum(p[h], axis=0, keepdims=True) for h in range(heads)]
            pv = [nn(vt[span_of[h], :], p[h].astype(bf16)) for h in range(heads)]
            m_sc[...] = jnp.concatenate(m_new)
            l_sc[...] = l_sc[...] * jnp.concatenate(alpha) + jnp.concatenate(sums)
            for h in range(heads):
                acc_sc[span_of[h], :] = acc_sc[span_of[h], :] * alpha[h] + pv[h]

        return carry

    lax.fori_loop(0, kcount, step, 0)
    if closes:
        for h in range(heads):
            total = l_sc[h : h + 1, :]
            acc_sc[span_of[h], :] = jnp.where(real, acc_sc[span_of[h], :] / total, 0.0)
            lse_ref[h : h + 1, :] = jnp.where(real, m_sc[h : h + 1, :] + jnp.log2(total), -LOW)
        ctx_ref[...] = acc_sc[...].T.astype(bf16)
    else:
        m_out[...] = m_sc[...]
        l_out[...] = l_sc[...]
        acc_out[...] = acc_sc[...]


def whole(shape):
    return pl.BlockSpec(shape, lambda i, *_: (0,) * len(shape))


def attend(info, q, sources, offsets, kfirst, state=None, closes=False):
    rows, width = q.shape
    heads = width // HEAD_DIM
    keys = sum(source.shape[0] for source in sources)
    opens = state is None
    block = pl.BlockSpec((BLK, width), lambda i, *_: (i, 0))
    per_head = pl.BlockSpec((heads, BLK), lambda i, *_: (0, i))
    per_feature = pl.BlockSpec((width, BLK), lambda i, *_: (0, i))
    stats = jax.ShapeDtypeStruct((heads, rows), f32)
    carried = [per_head, per_head, per_feature]
    return pl.pallas_call(
        functools.partial(attend_kernel, heads, keys // BLK, kfirst, opens, closes, offsets),
        grid_spec=pltpu.PrefetchScalarGridSpec(
            num_scalar_prefetch=1,
            grid=(rows // BLK,),
            in_specs=[block]
            + [pl.BlockSpec(memory_space=pl.ANY)] * len(sources)
            + ([] if opens else carried),
            out_specs=[block, per_head] if closes else carried,
            scratch_shapes=[
                pltpu.VMEM((heads, BLK), f32),
                pltpu.VMEM((heads, BLK), f32),
                pltpu.VMEM((width, BLK), f32),
                pltpu.VMEM((heads * BLK, width), bf16),
                pltpu.VMEM((keys, width), bf16),
                pltpu.VMEM((keys, width), bf16),
                pltpu.VMEM((width, keys), bf16),
                pltpu.SemaphoreType.DMA((2 * len(sources),)),
            ],
        ),
        out_shape=[jax.ShapeDtypeStruct((rows, width), bf16), stats]
        if closes
        else [stats, stats, jax.ShapeDtypeStruct((width, rows), f32)],
        cost_estimate=pl.CostEstimate(
            flops=20 * rows * keys * width,
            bytes_accessed=4 * keys * width,
            transcendentals=rows * keys * heads // 2,
        ),
        name="attend_near" if opens else "attend_far",
    )(info, q, *sources, *(() if opens else state))


def attend_back_kernel(
    heads, kcount, kfirst, offsets, info, q_ref, do_ref, o_ref, lse_ref, *refs
):
    count = len(offsets)
    sources, refs = refs[:count], refs[count:]
    dq_ref, *outs = refs[:5]
    dk_sc, dv_sc, dqt_sc, qm_sc, dom_sc, delta_sc, k_sc, v_sc, kt_sc, sems = refs[5:]
    i = pl.program_id(0)
    rows, width = q_ref.shape
    qbase = info[3 + i]
    first, last, real = row_limits(info, qbase, rows)
    low, high = key_range(info, qbase, rows)
    scale = 1.0 / math.sqrt(HEAD_DIM)
    factor = math.log2(math.e) * scale

    @pl.when(i == 0)
    def _():
        dk_sc[...] = jnp.zeros_like(dk_sc)
        dv_sc[...] = jnp.zeros_like(dv_sc)
        stage(sources, offsets, width, k_sc, v_sc, sems)
        transposed(k_sc, kt_sc, kcount)

    dqt_sc[...] = jnp.zeros_like(dqt_sc)
    do = do_ref[...]
    masked_heads(q_ref[...], qm_sc, heads)
    masked_heads(do, dom_sc, heads)
    prod = (do.astype(f32) * o_ref[...].astype(f32)).T
    span_of = [slice(h * HEAD_DIM, (h + 1) * HEAD_DIM) for h in range(heads)]
    rows_of = [slice(h * rows, (h + 1) * rows) for h in range(heads)]
    for h in range(heads):
        delta_sc[h : h + 1, :] = jnp.sum(prod[span_of[h], :], axis=0, keepdims=True)

    def step(j, carry):
        base = info[kfirst + j]

        @pl.when((base + BLK > low) & (base < high))
        def _():
            span = pl.ds(pl.multiple_of(j * BLK, BLK), BLK)
            kb = k_sc[span, :]
            vb = v_sc[span, :]
            kt = kt_sc[:, span]
            posk = base + lax.broadcasted_iota(jnp.int32, (BLK, rows), 0)
            allowed = (posk >= first) & (posk < last)
            s = [nt(kb, qm_sc[rows_of[h], :]) for h in range(heads)]
            dp = [nt(vb, dom_sc[rows_of[h], :]) for h in range(heads)]
            p = [
                jnp.where(allowed, jnp.exp2(s[h] * factor - lse_ref[0, h : h + 1, :]), 0.0)
                for h in range(heads)
            ]
            ds = [(p[h] * (dp[h] - delta_sc[h : h + 1, :])).astype(bf16) for h in range(heads)]
            low_p = [p[h].astype(bf16) for h in range(heads)]
            dv_sc[span, :] += nn(jnp.concatenate(low_p, axis=1), dom_sc[...])
            dk_sc[span, :] += nn(jnp.concatenate(ds, axis=1), qm_sc[...])
            for h in range(heads):
                dqt_sc[span_of[h], :] += nn(kt[span_of[h], :], ds[h])

        return carry

    lax.fori_loop(0, kcount, step, 0)
    dq_ref[...] = (dqt_sc[...] * scale).T.astype(bf16)

    @pl.when(i == pl.num_programs(0) - 1)
    def _():
        part = outs[0].shape[1]
        for n, out_ref in enumerate(outs):
            out_ref[0] = (dk_sc[n * part : (n + 1) * part, :] * scale).astype(bf16)
            out_ref[1] = dv_sc[n * part : (n + 1) * part, :].astype(bf16)


def attend_back(info, q, do, o, lse, sources, offsets, kfirst, pick, width):
    rows = q.shape[0]
    heads = width // HEAD_DIM
    keys = sum(source.shape[0] for source in sources)
    block = pl.BlockSpec((BLK, width), lambda i, *_: (i, pick))
    pair = (2, keys // 4, width)
    offsets = tuple((k_at + pick * width, v_at + pick * width) for k_at, v_at in offsets)
    return pl.pallas_call(
        functools.partial(attend_back_kernel, heads, keys // BLK, kfirst, offsets),
        grid_spec=pltpu.PrefetchScalarGridSpec(
            num_scalar_prefetch=1,
            grid=(rows // BLK,),
            in_specs=[
                block,
                block,
                block,
                pl.BlockSpec((1, heads, BLK), lambda i, *_: (pick, 0, i)),
            ]
            + [pl.BlockSpec(memory_space=pl.ANY)] * len(sources),
            out_specs=[pl.BlockSpec((BLK, width), lambda i, *_: (i, 0))] + [whole(pair)] * 4,
            scratch_shapes=[
                pltpu.VMEM((keys, width), f32),
                pltpu.VMEM((keys, width), f32),
                pltpu.VMEM((width, BLK), f32),
                pltpu.VMEM((heads * BLK, width), bf16),
                pltpu.VMEM((heads * BLK, width), bf16),
                pltpu.VMEM((heads, BLK), f32),
                pltpu.VMEM((keys, width), bf16),
                pltpu.VMEM((keys, width), bf16),
                pltpu.VMEM((width, keys), bf16),
                pltpu.SemaphoreType.DMA((2 * len(sources),)),
            ],
        ),
        out_shape=[jax.ShapeDtypeStruct((rows, width), bf16)]
        + [jax.ShapeDtypeStruct(pair, bf16)] * 4,
        cost_estimate=pl.CostEstimate(
            flops=30 * rows * keys * width,
            bytes_accessed=8 * keys * width,
            transcendentals=rows * keys * heads // 2,
        ),
        name="attend_back",
    )(info, q, do, o, lse.reshape(-1, heads, rows), *sources)


def tp_swap(x, bit):
    return lax.ppermute(x, "tp", [(i, i ^ bit) for i in range(4)])


def gate_kernel(*refs):
    pass


def gate(through, *waits):
    through = tuple(through)
    anywhere = pl.BlockSpec(memory_space=pl.ANY)
    return pl.pallas_call(
        gate_kernel,
        in_specs=[anywhere] * (len(through) + len(waits)),
        out_specs=[anywhere] * len(through),
        out_shape=[jax.ShapeDtypeStruct(x.shape, x.dtype) for x in through],
        input_output_aliases={n: n for n in range(len(through))},
        name="gate",
    )(*through, *waits)


def tie(x, *others):
    for other in others:
        x = x + (other[(0,) * other.ndim].astype(f32) * 0.0).astype(x.dtype)
    return x


def fsdp_whole(shard, dim):
    if lax.axis_size("fsdp") != 2:
        full = lax.all_gather(shard, "fsdp", axis=dim, tiled=True)
        return full, full
    other = lax.ppermute(shard, "fsdp", [(0, 1), (1, 0)])
    low_half = lax.axis_index("fsdp") == 0
    return jnp.concatenate(
        [jnp.where(low_half, shard, other), jnp.where(low_half, other, shard)], axis=dim
    ), other


def fsdp_send(block_of, size, dim):
    if lax.axis_size("fsdp") != 2:
        mine = lax.psum_scatter(block_of(0, size), "fsdp", scatter_dimension=dim, tiled=True)
        return mine, jnp.zeros(mine.shape, bf16)
    half = size // 2
    place = lax.axis_index("fsdp")
    return block_of(place * half, half), block_of((1 - place) * half, half).astype(bf16)


def fsdp_swap(x):
    if lax.axis_size("fsdp") != 2:
        return x
    return lax.ppermute(x, "fsdp", [(0, 1), (1, 0)])


def ctx_swap(x, bit):
    return lax.ppermute(x, "ctx", [(i, i ^ bit) for i in range(4)])


def ctx_split(terms, bit):
    upper = (lax.axis_index("ctx") & bit) != 0
    size = terms.shape[0] // 2
    low_half, high_half = terms[:size], terms[size:]
    return (
        jnp.where(upper, high_half, low_half),
        jnp.where(upper, low_half, high_half).astype(bf16),
    )


def ctx_join(total, got, bit):
    upper = (lax.axis_index("ctx") & bit) != 0
    return jnp.concatenate([jnp.where(upper, got, total), jnp.where(upper, total, got)])


def rows_out(own):
    far = tp_swap(own, 2)
    near = tp_swap(own, 1)
    return own, near, far, tp_swap(far, 1)


def rows_in(terms):
    toward = terms[2] + tp_swap(terms[3].astype(bf16), 1).astype(f32)
    got = tp_swap(toward.astype(bf16), 2)
    here = terms[0] + tp_swap(terms[1].astype(bf16), 1).astype(f32)
    return here + got.astype(f32)


def natural(parts, core, y):
    r0, r1, r2, r3 = parts
    a0, a1 = jnp.where(core, r1, r0), jnp.where(core, r0, r1)
    a2, a3 = jnp.where(core, r3, r2), jnp.where(core, r2, r3)
    return jnp.concatenate(
        [jnp.where(y, a2, a0), jnp.where(y, a3, a1), jnp.where(y, a0, a2), jnp.where(y, a1, a3)]
    )


def norm_rows(rows):
    centre = rows - jnp.mean(rows, axis=-1, keepdims=True)
    inverse = lax.rsqrt(jnp.mean(centre * centre, axis=-1, keepdims=True) + norm_eps)
    return centre * inverse, inverse


def norm_back(grad, gain, normed, inverse):
    dn = grad * gain
    return (
        dn
        - jnp.mean(dn, axis=-1, keepdims=True)
        - normed * jnp.mean(dn * normed, axis=-1, keepdims=True)
    ) * inverse


def gelu_pair(values):
    phi_sum = 0.5 + 0.5 * lax.erf(values * math.sqrt(0.5))
    density = jnp.exp(values * values * -0.5) * (1.0 / math.sqrt(2.0 * math.pi))
    return (values * phi_sum).astype(bf16), phi_sum + values * density


def body(tokens, w_qkv, w_out, w_up, w_down, gains, shifts, lengths, out_grad):
    place = lax.axis_index("ctx")
    t = lax.axis_index("tp")
    core, y = (t & 1) == 1, (t >> 1) == 1
    tok_rows, depth = tokens.shape
    width = w_qkv.shape[2]
    quarter = tok_rows // 4
    order = (0, 2, 1, 3)

    def quarter_of(array, r):
        return lax.dynamic_slice_in_dim(array, (t ^ r) * quarter, quarter)

    half_a = jnp.concatenate([quarter_of(tokens, 0), quarter_of(tokens, 2)])
    left_a = lax.ppermute(half_a, "ctx", [(0, 1), (1, 2), (2, 3)])
    right_a = lax.ppermute(half_a, "ctx", [(3, 2), (2, 1), (1, 0)])
    half_b = jnp.concatenate([quarter_of(tokens, 1), quarter_of(tokens, 3)])
    far_left = lax.ppermute(left_a, "ctx", [(1, 2), (2, 3)])
    far_right = lax.ppermute(right_a, "ctx", [(2, 1), (1, 0)])
    full_qkv, got_qkv = fsdp_whole(w_qkv, 1)
    own_out, got_out = fsdp_whole(tie(w_out, got_qkv), 1)
    full_vectors, _ = fsdp_whole(jnp.concatenate([tie(gains, got_qkv), shifts]), 1)
    full_up, got_up = fsdp_whole(tie(w_up, got_qkv), 0)
    full_down, got_down = fsdp_whole(tie(w_down, got_qkv), 1)
    full_vectors = full_vectors.astype(f32)
    gain = full_vectors[:2]
    shift = full_vectors[2:]

    positions = jnp.stack([t ^ r for r in order]) * quarter
    chunks = jnp.stack([place, place - 1, place + 1, place ^ 2]) * tok_rows
    info = jnp.concatenate(
        [
            jnp.cumsum(lengths[0]),
            place * tok_rows + positions,
            (chunks[:, None] + positions[None, :]).reshape(-1),
        ]
    ).astype(jnp.int32)

    w_q, w_k, w_v = full_qkv[0], full_qkv[1], full_qkv[2]
    w_all = jnp.concatenate([w_q, w_k, w_v], axis=1)
    w_kv = w_all[:, width:]
    own = [nn(rows, w_all).astype(bf16) for rows in (half_a, half_b)]
    near = [
        nn(rows, w_kv).astype(bf16)
        for rows in (left_a, tp_swap(left_a, 1), right_a, tp_swap(right_a, 1))
    ]
    queries = jnp.concatenate([part[:, :width] for part in own])
    own_at, other_at = (width, 2 * width), (0, width)
    near_at = (own_at,) * 2 + (other_at,) * 4
    state = attend(info, queries, own + near, near_at, 7)
    far_left, far_right = gate((far_left, far_right), state[0])
    far_a = jnp.where(place >= 2, far_left, far_right)
    out_y = tp_swap(own_out, 2)
    out_all = jnp.concatenate([own_out, out_y, tp_swap(own_out, 1), tp_swap(out_y, 1)])
    far = [nn(rows, w_kv).astype(bf16) for rows in (far_a, tp_swap(far_a, 1))]
    context, log_totals = attend(info, queries, far, (other_at,) * 2, 19, state, True)
    (context,) = gate((context,), got_up, got_down, out_all)

    pieces = jnp.split(context, 4)
    context_own = jnp.concatenate(
        [pieces[0]] + [tp_swap(pieces[n], order[n]) for n in (1, 2, 3)], axis=1
    )
    resid_rows = quarter_of(tokens, 0).astype(f32) + nn(context_own, out_all)
    normed_first, inverse_first = norm_rows(resid_rows)
    hidden = normed_first * gain[0] + shift[0]
    hid0, hid1, hid2, hid3 = rows_out(hidden.astype(bf16))
    hid_near, hid_far = jnp.concatenate([hid0, hid1]), jnp.concatenate([hid2, hid3])

    act_near, slope_near = gelu_pair(nn(hid_near, full_up))
    act_far, slope_far = gelu_pair(nn(hid_far, full_up))
    terms_far = nn(act_far, full_down)
    terms_near = nn(act_near, full_down)
    ffn_rows = rows_in(
        (terms_near[:quarter], terms_near[quarter:], terms_far[:quarter], terms_far[quarter:])
    )
    normed_second, inverse_second = norm_rows(hidden + ffn_rows)
    result = (normed_second * gain[1] + shift[1]).astype(bf16)
    grad_rows = quarter_of(out_grad, 0).astype(f32)
    grad_mid = norm_back(grad_rows, gain[1], normed_second, inverse_second)

    mid0, mid1, mid2, mid3 = rows_out(grad_mid.astype(bf16))
    mid_near, mid_far = jnp.concatenate([mid0, mid1]), jnp.concatenate([mid2, mid3])

    def column_block(left, right):
        return lambda start, size: tn(left, lax.dynamic_slice_in_dim(right, start, size, axis=1))

    def row_block(left, right):
        return lambda start, size: tn(lax.dynamic_slice_in_dim(left, start, size, axis=1), right)

    act_all = jnp.concatenate([act_near, act_far])
    mid_all = jnp.concatenate([mid_near, mid_far])
    down_terms, down_send = fsdp_send(column_block(act_all, mid_all), depth, 1)
    down_got = fsdp_swap(down_send)

    pre_near = (nt(mid_near, full_down) * slope_near).astype(bf16)
    pre_far = (nt(mid_far, full_down) * slope_far).astype(bf16)
    terms_far = nt(pre_far, full_up)
    terms_near = nt(pre_near, full_up)
    hidden_grad = grad_mid + rows_in(
        (terms_near[:quarter], terms_near[quarter:], terms_far[:quarter], terms_far[quarter:])
    )
    hid_all = jnp.concatenate([hid_near, hid_far])
    pre_all = jnp.concatenate([pre_near, pre_far])
    up_terms, up_send = fsdp_send(row_block(hid_all, pre_all), depth, 0)
    resid_grad = norm_back(hidden_grad, gain[0], normed_first, inverse_first)
    attn_own = resid_grad.astype(bf16)

    attn_own, up_send, down_got = gate((attn_own, up_send, down_got))
    up_got = fsdp_swap(up_send)
    down_kept, send = ctx_split(down_terms + down_got.astype(f32), 1)
    down_got = ctx_swap(send, 1)
    back_own = nt(attn_own, out_all).astype(bf16)
    pieces = jnp.split(back_own, 4, axis=1)
    context_grad = jnp.concatenate(
        [pieces[0]] + [tp_swap(pieces[n], order[n]) for n in (1, 2, 3)]
    )

    context_grad, down_got, attn_own, result = gate((context_grad, down_got, attn_own, result))
    down_kept, send = ctx_split(down_kept + down_got.astype(f32), 2)
    down_got = ctx_swap(send, 2)
    attn_near, attn_far = tp_swap(attn_own, 1), tp_swap(attn_own, 2)
    result_near, result_far = tp_swap(result, 1), tp_swap(result, 2)
    vectors = jnp.stack(
        [
            jnp.sum(hidden_grad * normed_first, axis=0),
            jnp.sum(grad_rows * normed_second, axis=0),
            jnp.sum(hidden_grad, axis=0),
            jnp.sum(grad_rows, axis=0),
        ]
    )
    vectors_got = tp_swap(vectors, 1)

    sources = own + near + far
    sources_at = (own_at,) * 2 + (other_at,) * 6
    part = width // 2
    dq_1, own_1, left_1, right_1, far_1 = attend_back(
        info, queries, context_grad, context, log_totals, sources, sources_at, 7, 0, part
    )
    info_2, far_1, down_got, up_got, attn_far, result_far, vectors_got = gate(
        (info, far_1, down_got, up_got, attn_far, result_far, vectors_got),
        attn_near,
        result_near,
    )
    left_hop, right_hop = [(2, 1), (3, 2)], [(0, 1), (1, 2)]
    from_left_1 = lax.ppermute(far_1, "ctx", left_hop)
    from_right_1 = lax.ppermute(far_1, "ctx", right_hop)
    down_total = (down_kept + down_got.astype(f32)).astype(bf16)
    down_total = lax.optimization_barrier(down_total)
    down_got = ctx_swap(down_total, 2)
    up_kept, send = ctx_split(up_terms + up_got.astype(f32), 1)
    up_got = ctx_swap(send, 1)
    attn_all = jnp.concatenate([attn_own, attn_far, attn_near, tp_swap(attn_far, 1)])
    result_parts = (result, result_near, result_far, tp_swap(result_far, 1))
    out_terms, out_send = fsdp_send(column_block(context, attn_all), depth, 1)
    out_got = fsdp_swap(out_send)
    vectors = vectors + vectors_got
    vectors_got = tp_swap(vectors, 2)

    dq_2, own_2, left_2, right_2, far_2 = attend_back(
        info_2, queries, context_grad, context, log_totals, sources, sources_at, 7, 1, part
    )
    far_2, from_left_1, from_right_1, down_got, up_got, vectors_got = gate(
        (far_2, from_left_1, from_right_1, down_got, up_got, vectors_got), out_got
    )

    def hop(own_kv, left_kv, right_kv, from_left, from_right):
        left_sum = (left_kv.astype(f32) + from_left.astype(f32)).astype(bf16)
        right_sum = (right_kv.astype(f32) + from_right.astype(f32)).astype(bf16)
        return (
            lax.ppermute(left_sum, "ctx", [(3, 2), (2, 1), (1, 0)]),
            lax.ppermute(right_sum, "ctx", [(0, 1), (1, 2), (2, 3)]),
        )

    home_1 = hop(own_1, left_1, right_1, from_left_1, from_right_1)
    from_left_2 = lax.ppermute(far_2, "ctx", left_hop)
    from_right_2 = lax.ppermute(far_2, "ctx", right_hop)
    vectors = vectors + vectors_got
    vectors_got = ctx_swap(vectors, 1)
    down_total = ctx_join(down_total, down_got, 2)
    up_kept, up_send = ctx_split(up_kept + up_got.astype(f32), 2)

    home_1a, home_1b, from_left_2, from_right_2, vectors_got, down_total, up_send = gate(
        (*home_1, from_left_2, from_right_2, vectors_got, down_total, up_send)
    )
    home_2 = hop(own_2, left_2, right_2, from_left_2, from_right_2)
    rows_own = jnp.concatenate([half_a, half_b])
    total_1 = (own_1.astype(f32) + home_1a.astype(f32) + home_1b.astype(f32)).astype(bf16)
    grads_1 = jnp.concatenate([dq_1, dq_2, total_1[0], total_1[1]], axis=1)
    qkv_terms_1, qkv_send_1 = fsdp_send(row_block(rows_own, grads_1), depth, 0)
    qkv_got_1 = fsdp_swap(qkv_send_1)
    weights_1 = jnp.concatenate([w_q, w_k[:, :part], w_v[:, :part]], axis=1)
    weights_2 = jnp.concatenate([w_k[:, part:], w_v[:, part:]], axis=1)
    terms_1 = nt(grads_1, weights_1)
    vectors = vectors + vectors_got
    vectors_got = ctx_swap(vectors, 2)

    home_2a, home_2b, qkv_got_1, vectors_got, down_total, up_send = gate(
        (*home_2, qkv_got_1, vectors_got, down_total, up_send)
    )
    total_2 = (own_2.astype(f32) + home_2a.astype(f32) + home_2b.astype(f32)).astype(bf16)
    grads_2 = jnp.concatenate([total_2[0], total_2[1]], axis=1)
    terms = terms_1 + nt(grads_2, weights_2)
    q0, q2, q1, q3 = jnp.split(terms, 4)
    toward = q2 + tp_swap(q3.astype(bf16), 1).astype(f32)
    input_got = tp_swap(toward.astype(bf16), 2)
    here = q0 + tp_swap(q1.astype(bf16), 1).astype(f32)
    qkv_terms_2, qkv_send_2 = fsdp_send(row_block(rows_own, grads_2), depth, 0)
    qkv_got_2 = fsdp_swap(qkv_send_2)
    down_got = ctx_swap(down_total, 1)
    up_got = ctx_swap(up_send, 2)
    vectors = vectors + vectors_got
    split_vectors = lax.axis_size("fsdp") == 2
    if split_vectors:
        half = depth // 2
        mine = lax.axis_index("fsdp")
        vectors_got = fsdp_swap(
            lax.dynamic_slice_in_dim(vectors, (1 - mine) * half, half, axis=1)
        )
        vectors = lax.dynamic_slice_in_dim(vectors, mine * half, half, axis=1)
    else:
        vectors = lax.psum_scatter(vectors, "fsdp", scatter_dimension=1, tiled=True)
        vectors_got = jnp.zeros_like(vectors)

    input_got, qkv_got_2, down_got, up_got, vectors_got = gate(
        (input_got, qkv_got_2, down_got, up_got, vectors_got)
    )
    vectors = vectors + vectors_got
    input_own = (resid_grad + here + input_got.astype(f32)).astype(bf16)
    input_near, input_far = tp_swap(input_own, 1), tp_swap(input_own, 2)
    down_grad = ctx_join(down_total, down_got, 1).astype(f32)
    up_total = lax.optimization_barrier((up_kept + up_got.astype(f32)).astype(bf16))
    up_got = ctx_swap(up_total, 2)
    out_shape = out_terms.shape
    rest = jnp.concatenate(
        [
            qkv_terms_1 + qkv_got_1.astype(f32),
            qkv_terms_2 + qkv_got_2.astype(f32),
            (out_terms + out_got.astype(f32)).reshape(qkv_terms_1.shape[0], -1),
        ],
        axis=1,
    )
    rest_kept, send = ctx_split(rest, 1)
    rest_got = ctx_swap(send, 1)

    input_far, input_near, up_got, rest_got = gate((input_far, input_near, up_got, rest_got))
    input_parts = (input_own, input_near, input_far, tp_swap(input_far, 1))
    up_total = ctx_join(up_total, up_got, 2)
    up_got = ctx_swap(up_total, 1)
    rest_kept, send = ctx_split(rest_kept + rest_got.astype(f32), 2)
    rest_got = ctx_swap(send, 2)
    rest_total = (rest_kept + rest_got.astype(f32)).astype(bf16)
    rest_total = lax.optimization_barrier(rest_total)
    rest_total = ctx_join(rest_total, ctx_swap(rest_total, 2), 2)
    rest_total = ctx_join(rest_total, ctx_swap(rest_total, 1), 1).astype(f32)
    up_grad = ctx_join(up_total, up_got, 1).astype(f32)
    qkv_1, qkv_2 = rest_total[:, : 2 * width], rest_total[:, 2 * width : 3 * width]
    qkv_grad = jnp.stack(
        [
            qkv_1[:, :width],
            jnp.concatenate([qkv_1[:, width : width + part], qkv_2[:, :part]], axis=1),
            jnp.concatenate([qkv_1[:, width + part :], qkv_2[:, part:]], axis=1),
        ]
    )
    return (
        natural(result_parts, core, y),
        natural(input_parts, core, y),
        qkv_grad,
        rest_total[:, 3 * width :].reshape(out_shape),
        up_grad,
        down_grad,
        vectors[:2],
        vectors[2:],
    )


def solution(mesh):
    return jax.shard_map(
        body,
        mesh=mesh,
        in_specs=(
            P(("fsdp", "ctx"), None),
            P(None, "fsdp", "tp"),
            P("tp", "fsdp"),
            P("fsdp", "tp"),
            P("tp", "fsdp"),
            P(None, "fsdp"),
            P(None, "fsdp"),
            P("fsdp", None),
            P(("fsdp", "ctx"), None),
        ),
        out_specs=(
            P(("fsdp", "ctx"), None),
            P(("fsdp", "ctx"), None),
            P(None, "fsdp", "tp"),
            P("tp", "fsdp"),
            P("fsdp", "tp"),
            P("tp", "fsdp"),
            P(None, "fsdp"),
            P(None, "fsdp"),
        ),
        check_vma=False,
    )
```

time: 620 us -> 514 us (0.83)
  waiting for transfers between devices: 256 us -> 172 us
  starting transfers between devices: 171 us -> 97.3 us
  other arithmetic: 34.5 us -> 57.1 us
  Pallas kernels: 58.9 us -> 80.7 us
    ppermute x33 -> x30, starting transfers between devices: 129 us -> 65.3 us  [the longest x14 31.3 us: ctx_swap(): return lax.ppermute(x, 'ctx', [(i, i ^ bit) for i in range(4)])]
    ppermute x33 -> x30, waiting for transfers between devices: 147 us -> 88.4 us  [the longest x14 68.5 us: ctx_swap(): return lax.ppermute(x, 'ctx', [(i, i ^ bit) for i in range(4)])]
    ppermute x5, waiting for transfers between devices: 46.3 us -> 20.1 us  [fsdp_whole(): other = lax.ppermute(shard, 'fsdp', [(0, 1), (1, 0)])]
    pallas_call x2 -> x14, Pallas kernels: 58.9 us -> 80.7 us  [the longest x2 46.6 us: attend_back(): pl.pallas_call(functools.partial(attend_back_kernel, heads, keys // BLK,...]
    ppermute x5, starting transfers between devices: 21.1 us -> 5.76 us  [fsdp_whole(): other = lax.ppermute(shard, 'fsdp', [(0, 1), (1, 0)])]
    convert_element_type x20 -> x21, other arithmetic: 8.23 us -> 19 us  [the longest x2 3.57 us: hop(): left_sum = (left_kv.astype(f32) + from_left.astype(f32)).astype(bf16)]
    concatenate x6 -> x1, local copies, waits for them, and re-layouts: 8.68 us -> 0.03 us  [body(): jnp.concatenate([attn_own, attn_far, attn_near, tp_swap(attn_far, 1)])]
    concatenate x2 -> x8, other arithmetic: 0.18 us -> 7.45 us  [the longest x1 4.01 us: body(): jnp.concatenate([own_out, out_y, tp_swap(own_out, 1), tp_swap(out_y, 1)])]
  transfers between devices with their start and end apart: 78 -> 75, of which waited for: 29 -> 29; matrix products, arithmetic and copies ran while one was open for 17% -> 23% of each run, Pallas kernels for 10% -> 16%
where the time goes in v2:
time: 514 us; the launch traced here: 505 us
  waiting for transfers between devices  172 us (33%)
  starting transfers between devices  97.3 us (19%)
  Pallas kernels  80.7 us (16%)
  matrix products  63.2 us (12%)
  other arithmetic  57.1 us (11%)
  local copies, waits for them, and re-layouts  30.1 us (6%)
    ppermute x14, waiting for transfers between devices, ctx_swap(): return lax.ppermute(x, 'ctx', [(i, i ^ bit) for i in range(4)])  68.5 us
    dot_general x30, matrix products, contract(): lax.dot_general(left, right, (((left_dim,), (right_dim,)), ((), ())), pre...  63.2 us
    ppermute x38, waiting for transfers between devices, tp_swap(): return lax.ppermute(x, 'tp', [(i, i ^ bit) for i in range(4)])  58.4 us
    pallas_call x2, Pallas kernels, attend_back(): pl.pallas_call(functools.partial(attend_back_kernel, heads, keys // BLK,...  46.6 us
    pallas_call x2, Pallas kernels, attend(): pl.pallas_call(functools.partial(attend_kernel, heads, keys // BLK, kfirs...  34.1 us
    ppermute x14, starting transfers between devices, ctx_swap(): return lax.ppermute(x, 'ctx', [(i, i ^ bit) for i in range(4)])  31.3 us
    ppermute x38, starting transfers between devices, tp_swap(): return lax.ppermute(x, 'tp', [(i, i ^ bit) for i in range(4)])  20.4 us
    ppermute x5, waiting for transfers between devices, fsdp_whole(): other = lax.ppermute(shard, 'fsdp', [(0, 1), (1, 0)])  20.1 us
  transfers between devices with their start and end apart: 75, of which 29 were waited for; matrix products, arithmetic and copies ran while one was open for 23% of the time, Pallas kernels for 16%

profile of v2, /device:TPU:0, one launch (start us, length us, event | category | flops | bytes accessed | tf_op | source)
XLA Modules:
  0.0 504.6 jit_solution(17596582976383970432)
XLA Ops:
  6.4 4.6 collective-permute-start.2
  13.4 8.1 %collective-permute-done = bf16[3,512,256]{2,1,0:T(8,128)(2,1)} collective-permute-done((bf16[3,512,256]{2,1,0:T(8,128)(2,1)}, bf16[3,512,256]{2,1,0:T(8,128)(2,1)}, u32[]{:S(2)}, u32[]{:S(2)}) %collective-permute-start) | collective-permute-done | bytes 786464 | tf_op jit(solution)/shard_map/ppermute | solution.py:360
  33.9 3.7 collective-permute-done.4
  50.6 27.8 %attend_near.1 = (f32[4,1024]{1,0:T(4,128)}, f32[4,1024]{1,0:T(4,128)}, f32[256,1024]{1,0:T(8,128)}) custom-call(s32[23]{0:T(128)} %pad_add_fusion.info.refs_0_, bf16[1024,256]{1,0:T(8,128)(2,1)} %pad_maximum_fusion.23.q_ref, bf16[512,768]{1,0:T(8,128)(2,1)} %copy-done.124, bf16[512,768]{1,0:T(8,128)(2,1)} %copy-done.125, ...), custom_call_target="tpu_custom_call" | custom-call | flops 16106127360 | bytes 3145728 | tf_op jit(solution)/shard_map/attend_near/pallas_call | solution.py:184
  82.6 4.0 pad_maximum_fusion.refs_3_
  89.6 6.3 %attend_far.1 = (bf16[1024,256]{1,0:T(8,128)(2,1)}, f32[4,1024]{1,0:T(4,128)}) custom-call(s32[23]{0:T(128)} %pad_add_fusion.info.refs_0_, bf16[1024,256]{1,0:T(8,128)(2,1)} %pad_maximum_fusion.23.q_ref, bf16[512,512]{1,0:T(8,128)(2,1)} %convolution_convert_fusion.7.refs_0_.refs_6_, bf16[512,512]{1,0:T(8,128)(2,1)} %convolution_convert_fusion.6.refs_1_.refs_7_, ...), custom_call_target="tpu_custom_call" | custom-call | flops 5368709120 | bytes 1048576 | tf_op jit(solution)/shard_map/attend_far/pallas_call | solution.py:184
  96.0 12.0 %collective-permute-done.10.refs_2_ = bf16[1024,512]{1,0:T(8,128)(2,1)S(1)} collective-permute-done((bf16[1024,512]{1,0:T(8,128)(2,1)}, bf16[1024,512]{1,0:T(8,128)(2,1)S(1)}, u32[]{:S(2)}, u32[]{:S(2)}) %collective-permute-start.10) | collective-permute-done | bytes 1048608 | tf_op jit(solution)/shard_map/ppermute | solution.py:360
  122.0 12.7 %collective-permute-done.20 = bf16[256,1024]{1,0:T(8,128)(2,1)S(1)} collective-permute-done((bf16[256,1024]{1,0:T(8,128)(2,1)S(1)}, bf16[256,1024]{1,0:T(8,128)(2,1)S(1)}, u32[]{:S(2)}, u32[]{:S(2)}) %collective-permute-start.20) | collective-permute-done | bytes 524320 | tf_op jit(solution)/shard_map/ppermute | solution.py:330
  146.8 12.7 %collective-permute-done.23 = bf16[256,1024]{1,0:T(8,128)(2,1)S(1)} collective-permute-done((bf16[256,1024]{1,0:T(8,128)(2,1)S(1)}, bf16[256,1024]{1,0:T(8,128)(2,1)S(1)}, u32[]{:S(2)}, u32[]{:S(2)}) %collective-permute-start.23) | collective-permute-done | bytes 524320 | tf_op jit(solution)/shard_map/ppermute | solution.py:330
  163.2 12.1 %collective-permute-done.26 = bf16[256,1024]{1,0:T(8,128)(2,1)} collective-permute-done((bf16[256,1024]{1,0:T(8,128)(2,1)S(1)}, bf16[256,1024]{1,0:T(8,128)(2,1)}, u32[]{:S(2)}, u32[]{:S(2)}) %collective-permute-start.26) | collective-permute-done | bytes 524320 | tf_op jit(solution)/shard_map/ppermute | solution.py:330
  183.1 12.8 %multiply_convert_fusion.1 = bf16[512,1024]{1,0:T(8,128)(2,1)S(1)} fusion(f32[512,1024]{1,0:T(8,128)S(1)} %copy-done.145, bf16[256,1024]{1,0:T(8,128)(2,1)S(1)} %collective-permute-done.24, bf16[256,1024]{1,0:T(8,128)(2,1)S(1)} %fusion.102, bf16[1024,512]{1,0:T(8,128)(2,1)S(1)} %copy-done.85, bf16[1024,512]{1,0:T(8,128)(2,1)S(1)} %copy-done.83), kind=kOutput, calls=%fused_computation.15 | convolution fusion | flops 1085276160 | bytes 6291456 | tf_op jit(solution)/shard_map/dot_general | solution.py:20
  204.8 7.2 %collective-permute-done.29 = bf16[256,1024]{1,0:T(8,128)(2,1)S(1)} collective-permute-done((bf16[256,1024]{1,0:T(8,128)(2,1)S(1)}, bf16[256,1024]{1,0:T(8,128)(2,1)S(1)}, u32[]{:S(2)}, u32[]{:S(2)}) %collective-permute-start.29) | collective-permute-done | bytes 524320 | tf_op jit(solution)/shard_map/ppermute | solution.py:330
  215.7 11.2 %collective-permute-done.30.refs_2_ = bf16[1024,512]{1,0:T(8,128)(2,1)S(1)} collective-permute-done((bf16[1024,512]{1,0:T(8,128)(2,1)S(1)}, bf16[1024,512]{1,0:T(8,128)(2,1)S(1)}, u32[]{:S(2)}, u32[]{:S(2)}) %collective-permute-start.30) | collective-permute-done | bytes 1048608 | tf_op jit(solution)/shard_map/ppermute | solution.py:379
  231.3 3.9 collective-permute-start.34
  238.8 3.8 collective-permute-done.33
  248.5 5.7 %collective-permute-start.35 = (bf16[256,512]{1,0:T(8,128)(2,1)S(1)}, bf16[256,512]{1,0:T(8,128)(2,1)S(1)}, u32[]{:S(2)}, u32[]{:S(2)}) collective-permute-start(bf16[256,512]{1,0:T(8,128)(2,1)S(1)} %select_convert_fusion.5), channel_id=1, source_target_pairs={{0,8},{4,12},{8,0},{12,4},{1,9},{5,13},{9,1},{13,5},{2,10},{6,14},... | collective-permute-start | bytes 786440 | tf_op jit(solution)/shard_map/ppermute | solution.py:383
  260.3 5.1 %collective-permute-done.35.refs_2_ = bf16[256,512]{1,0:T(8,128)(2,1)S(1)} collective-permute-done((bf16[256,512]{1,0:T(8,128)(2,1)S(1)}, bf16[256,512]{1,0:T(8,128)(2,1)S(1)}, u32[]{:S(2)}, u32[]{:S(2)}) %collective-permute-start.35) | collective-permute-done | bytes 262176 | tf_op jit(solution)/shard_map/ppermute | solution.py:383
  265.4 23.3 %attend_back.2 = (bf16[1024,128]{1,0:T(8,128)(2,1)}, bf16[2,1024,128]{2,1,0:T(8,128)(2,1)}, bf16[2,1024,128]{2,1,0:T(8,128)(2,1)}, bf16[2,1024,128]{2,1,0:T(8,128)(2,1)}, bf16[2,1024,128]{2,1,0:T(8,128)(2,1)}) custom-call(s32[23]{0:T(128)} %pad_add_fusion.info.refs_0_, bf16[1024,256]{1,0:T(8,128)(2,1)} %pad_maximum_fusion.23.q_ref, ...), custom_call_target="tpu_custom_call" | custom-call | flops 16106127360 | bytes 4194304 | tf_op jit(solution)/shard_map/attend_back/pallas_call | solution.py:292
  297.2 3.6 convert_add_fusion
  309.0 4.0 collective-permute-start.49
  313.0 23.3 %attend_back.3 = (bf16[1024,128]{1,0:T(8,128)(2,1)}, bf16[2,1024,128]{2,1,0:T(8,128)(2,1)}, bf16[2,1024,128]{2,1,0:T(8,128)(2,1)}, bf16[2,1024,128]{2,1,0:T(8,128)(2,1)}, bf16[2,1024,128]{2,1,0:T(8,128)(2,1)}) custom-call(s32[23]{0:T(128)} %get-tuple-element.84.info, bf16[1024,256]{1,0:T(8,128)(2,1)} %pad_maximum_fusion.23.q_ref, ...), custom_call_target="tpu_custom_call" | custom-call | flops 16106127360 | bytes 4194304 | tf_op jit(solution)/shard_map/attend_back/pallas_call | solution.py:292
  345.9 5.2 %collective-permute-start.51 = (bf16[2,1024,128]{2,1,0:T(8,128)(2,1)S(1)}, bf16[2,1024,128]{2,1,0:T(8,128)(2,1)S(1)}, u32[]{:S(2)}, u32[]{:S(2)}) collective-permute-start(bf16[2,1024,128]{2,1,0:T(8,128)(2,1)S(1)} %add_convert_fusion.4), channel_id=1, source_target_pairs={{0,4},{4,8},{8,12},{1,5},{5,9},{9,13},{2,6},{6,10},{10,14},{3,7},{... | collective-permute-start | bytes 1572872 | tf_op jit(solution)/shard_map/ppermute | solution.py:613
  356.1 8.0 %collective-permute-done.54.refs_4_ = f32[4,1024]{1,0:T(4,128)S(1)} collective-permute-done((f32[4,1024]{1,0:T(4,128)S(1)}, f32[4,1024]{1,0:T(4,128)S(1)}, u32[]{:S(2)}, u32[]{:S(2)}) %collective-permute-start.54) | collective-permute-done | bytes 16416 | tf_op jit(solution)/shard_map/ppermute | solution.py:383
  371.7 5.2 %collective-permute-start.56 = (bf16[2,1024,128]{2,1,0:T(8,128)(2,1)}, bf16[2,1024,128]{2,1,0:T(8,128)(2,1)S(1)}, u32[]{:S(2)}, u32[]{:S(2)}) collective-permute-start(bf16[2,1024,128]{2,1,0:T(8,128)(2,1)} %add_convert_fusion.1), channel_id=1, source_target_pairs={{0,4},{4,8},{8,12},{1,5},{5,9},{9,13},{2,6},{6,10},{10,14},{3,7},{... | collective-permute-start | bytes 1572872 | tf_op jit(solution)/shard_map/ppermute | solution.py:613
  381.5 3.8 collective-permute-start.58
  387.1 5.0 collective-permute-done.57.refs_2_
  420.8 7.3 %collective-permute-done.64.refs_3_ = bf16[128,1024]{1,0:T(8,128)(2,1)S(1)} collective-permute-done((bf16[128,1024]{1,0:T(8,128)(2,1)S(1)}, bf16[128,1024]{1,0:T(8,128)(2,1)S(1)}, u32[]{:S(2)}, u32[]{:S(2)}) %collective-permute-start.64) | collective-permute-done | bytes 262176 | tf_op jit(solution)/shard_map/ppermute | solution.py:383
  438.2 13.5 %collective-permute-done.68.refs_2_ = bf16[128,1024]{1,0:T(8,128)(2,1)S(1)} collective-permute-done((bf16[128,1024]{1,0:T(8,128)(2,1)S(1)}, bf16[128,1024]{1,0:T(8,128)(2,1)S(1)}, u32[]{:S(2)}, u32[]{:S(2)}) %collective-permute-start.68) | collective-permute-done | bytes 262176 | tf_op jit(solution)/shard_map/ppermute | solution.py:383
  458.9 11.1 %collective-permute-done.71 = bf16[128,1024]{1,0:T(8,128)(2,1)S(1)} collective-permute-done((bf16[128,1024]{1,0:T(8,128)(2,1)S(1)}, bf16[128,1024]{1,0:T(8,128)(2,1)S(1)}, u32[]{:S(2)}, u32[]{:S(2)}) %collective-permute-start.71) | collective-permute-done | bytes 262176 | tf_op jit(solution)/shard_map/ppermute | solution.py:383
  475.1 9.1 %collective-permute-done.72 = bf16[128,1024]{1,0:T(8,128)(2,1)S(1)} collective-permute-done((bf16[128,1024]{1,0:T(8,128)(2,1)S(1)}, bf16[128,1024]{1,0:T(8,128)(2,1)S(1)}, u32[]{:S(2)}, u32[]{:S(2)}) %collective-permute-start.72) | collective-permute-done | bytes 262176 | tf_op jit(solution)/shard_map/ppermute | solution.py:383
  484.3 7.5 %collective-permute-done.74 = bf16[256,1024]{1,0:T(8,128)(2,1)S(1)} collective-permute-done((bf16[256,1024]{1,0:T(8,128)(2,1)S(1)}, bf16[256,1024]{1,0:T(8,128)(2,1)S(1)}, u32[]{:S(2)}, u32[]{:S(2)}) %collective-permute-start.74) | collective-permute-done | bytes 524320 | tf_op jit(solution)/shard_map/ppermute | solution.py:383
  495.4 5.8 %collective-permute-done.73 = bf16[256,1024]{1,0:T(8,128)(2,1)S(1)} collective-permute-done((bf16[256,1024]{1,0:T(8,128)(2,1)S(1)}, bf16[256,1024]{1,0:T(8,128)(2,1)S(1)}, u32[]{:S(2)}, u32[]{:S(2)}) %collective-permute-start.73) | collective-permute-done | bytes 524320 | tf_op jit(solution)/shard_map/ppermute | solution.py:383
  (573 shorter events, 211.3 us)
Async XLA Ops:
  0.6 20.9 %collective-permute-start = (bf16[3,512,256]{2,1,0:T(8,128)(2,1)}, bf16[3,512,256]{2,1,0:T(8,128)(2,1)}, u32[]{:S(2)}, u32[]{:S(2)}) collective-permute-start(bf16[3,512,256]{2,1,0:T(8,128)(2,1)} %param.10), channel_id=1, source_target_pairs={{0,16},{16,0},{1,17},{17,1},{2,18},{18,2},{3,19},{19,3},{4,20},{20... | collective-permute-start | bytes 2359304 | tf_op jit(solution)/shard_map/ppermute | solution.py:360
  6.4 26.0 %collective-permute-start.2 = (bf16[512,1024]{1,0:T(8,128)(2,1)}, bf16[512,1024]{1,0:T(8,128)(2,1)}, u32[]{:S(2)}, u32[]{:S(2)}) collective-permute-start(bf16[512,1024]{1,0:T(8,128)(2,1)} %pad_maximum_fusion.17), channel_id=1, source_target_pairs={{0,4},{4,8},{8,12},{1,5},{5,9},{9,13},{2,6},{6,10},{10,14},{3,7},{... | collective-permute-start | bytes 3145736 | tf_op jit(solution)/shard_map/ppermute | solution.py:457
  11.1 26.5 %collective-permute-start.4 = (bf16[512,1024]{1,0:T(8,128)(2,1)}, bf16[512,1024]{1,0:T(8,128)(2,1)}, u32[]{:S(2)}, u32[]{:S(2)}) collective-permute-start(bf16[512,1024]{1,0:T(8,128)(2,1)} %pad_maximum_fusion.17), channel_id=1, source_target_pairs={{12,8},{8,4},{4,0},{13,9},{9,5},{5,1},{14,10},{10,6},{6,2},{15,11}... | collective-permute-start | bytes 3145736 | tf_op jit(solution)/shard_map/ppermute | solution.py:458
  30.5 65.5 %collective-permute-start.9 = (bf16[512,1024]{1,0:T(8,128)(2,1)}, bf16[512,1024]{1,0:T(8,128)(2,1)S(1)}, u32[]{:S(2)}, u32[]{:S(2)}) collective-permute-start(bf16[512,1024]{1,0:T(8,128)(2,1)} %broadcast_add_fusion.1), channel_id=1, source_target_pairs={{0,16},{16,0},{1,17},{17,1},{2,18},{18,2},{3,19},{19,3},{4,20},{20... | collective-permute-start | bytes 3145736 | tf_op jit(solution)/shard_map/ppermute | solution.py:360
  32.5 50.0 %collective-permute-start.1 = (bf16[4,512]{1,0:T(4,128)(2,1)S(1)}, bf16[4,512]{1,0:T(4,128)(2,1)S(1)}, u32[]{:S(2)}, u32[]{:S(2)}) collective-permute-start(bf16[4,512]{1,0:T(4,128)(2,1)S(1)} %pad_maximum_fusion.36), channel_id=1, source_target_pairs={{0,16},{16,0},{1,17},{17,1},{2,18},{18,2},{3,19},{19,3},{4,20},{20... | collective-permute-start | bytes 12296 | tf_op jit(solution)/shard_map/ppermute | solution.py:360
  38.5 39.9 %collective-permute-start.12 = (bf16[256,1024]{1,0:T(8,128)(2,1)}, bf16[256,1024]{1,0:T(8,128)(2,1)}, u32[]{:S(2)}, u32[]{:S(2)}) collective-permute-start(bf16[256,1024]{1,0:T(8,128)(2,1)} %pad_maximum_fusion.24), channel_id=1, source_target_pairs={{0,2},{1,3},{2,0},{3,1},{4,6},{5,7},{6,4},{7,5},{8,10},{9,11},{10,... | collective-permute-start | bytes 1572872 | tf_op jit(solution)/shard_map/ppermute | solution.py:330
  45.6 33.1 %collective-permute-start.3 = (bf16[512,1024]{1,0:T(8,128)(2,1)}, bf16[512,1024]{1,0:T(8,128)(2,1)S(1)}, u32[]{:S(2)}, u32[]{:S(2)}) collective-permute-start(bf16[512,1024]{1,0:T(8,128)(2,1)} %collective-permute-done.2), channel_id=1, source_target_pairs={{4,8},{8,12},{5,9},{9,13},{6,10},{10,14},{7,11},{11,15},{20,24},{2... | collective-permute-start | bytes 3145736 | tf_op jit(solution)/shard_map/ppermute | solution.py:460
  47.8 31.2 %collective-permute-start.5 = (bf16[512,1024]{1,0:T(8,128)(2,1)}, bf16[512,1024]{1,0:T(8,128)(2,1)}, u32[]{:S(2)}, u32[]{:S(2)}) collective-permute-start(bf16[512,1024]{1,0:T(8,128)(2,1)} %collective-permute-done.4), channel_id=1, source_target_pairs={{8,4},{4,0},{9,5},{5,1},{10,6},{6,2},{11,7},{7,3},{24,20},{20,16},... | collective-permute-start | bytes 3145736 | tf_op jit(solution)/shard_map/ppermute | solution.py:461
  82.5 25.5 %collective-permute-start.10 = (bf16[1024,512]{1,0:T(8,128)(2,1)}, bf16[1024,512]{1,0:T(8,128)(2,1)S(1)}, u32[]{:S(2)}, u32[]{:S(2)}) collective-permute-start(bf16[1024,512]{1,0:T(8,128)(2,1)} %broadcast_add_fusion), channel_id=1, source_target_pairs={{0,16},{16,0},{1,17},{17,1},{2,18},{18,2},{3,19},{19,3},{4,20},{20... | collective-permute-start | bytes 3145736 | tf_op jit(solution)/shard_map/ppermute | solution.py:360
  202.1 24.9 %collective-permute-start.30 = (bf16[1024,512]{1,0:T(8,128)(2,1)S(1)}, bf16[1024,512]{1,0:T(8,128)(2,1)S(1)}, u32[]{:S(2)}, u32[]{:S(2)}) collective-permute-start(bf16[1024,512]{1,0:T(8,128)(2,1)S(1)} %convolution_convert_fusion), channel_id=1, source_target_pairs={{0,16},{16,0},{1,17},{17,1},{2,18},{18,2},{3,19},{19,3},{4,20},{20... | collective-permute-start | bytes 3145736 | tf_op jit(solution)/shard_map/ppermute | solution.py:379
  256.5 33.1 %collective-permute-start.36 = (bf16[512,1024]{1,0:T(8,128)(2,1)}, bf16[512,1024]{1,0:T(8,128)(2,1)}, u32[]{:S(2)}, u32[]{:S(2)}) collective-permute-start(bf16[512,1024]{1,0:T(8,128)(2,1)} %get-tuple-element.79), channel_id=1, source_target_pairs={{0,16},{16,0},{1,17},{17,1},{2,18},{18,2},{3,19},{19,3},{4,20},{20... | collective-permute-start | bytes 3145736 | tf_op jit(solution)/shard_map/ppermute | solution.py:379
  258.2 31.3 %collective-permute-start.37 = (bf16[256,1024]{1,0:T(8,128)(2,1)S(1)}, bf16[256,1024]{1,0:T(8,128)(2,1)}, u32[]{:S(2)}, u32[]{:S(2)}) collective-permute-start(bf16[256,1024]{1,0:T(8,128)(2,1)S(1)} %copy-done.1), channel_id=1, source_target_pairs={{0,2},{1,3},{2,0},{3,1},{4,6},{5,7},{6,4},{7,5},{8,10},{9,11},{10,... | collective-permute-start | bytes 1572872 | tf_op jit(solution)/shard_map/ppermute | solution.py:330
  259.2 30.4 %collective-permute-start.40 = (bf16[256,1024]{1,0:T(8,128)(2,1)S(1)}, bf16[256,1024]{1,0:T(8,128)(2,1)}, u32[]{:S(2)}, u32[]{:S(2)}) collective-permute-start(bf16[256,1024]{1,0:T(8,128)(2,1)S(1)} %copy-done.1), channel_id=1, source_target_pairs={{0,1},{1,0},{2,3},{3,2},{4,5},{5,4},{6,7},{7,6},{8,9},{9,8},{10,11... | collective-permute-start | bytes 1572872 | tf_op jit(solution)/shard_map/ppermute | solution.py:330
  259.2 30.4 %collective-permute-start.38 = (bf16[256,1024]{1,0:T(8,128)(2,1)S(1)}, bf16[256,1024]{1,0:T(8,128)(2,1)S(1)}, u32[]{:S(2)}, u32[]{:S(2)}) collective-permute-start(bf16[256,1024]{1,0:T(8,128)(2,1)S(1)} %copy-done.9), channel_id=1, source_target_pairs={{0,2},{1,3},{2,0},{3,1},{4,6},{5,7},{6,4},{7,5},{8,10},{9,11},{10,... | collective-permute-start | bytes 1572872 | tf_op jit(solution)/shard_map/ppermute | solution.py:330
  265.4 24.2 %collective-permute-start.41 = (bf16[256,1024]{1,0:T(8,128)(2,1)S(1)}, bf16[256,1024]{1,0:T(8,128)(2,1)S(1)}, u32[]{:S(2)}, u32[]{:S(2)}) collective-permute-start(bf16[256,1024]{1,0:T(8,128)(2,1)S(1)} %copy-done.9), channel_id=1, source_target_pairs={{0,1},{1,0},{2,3},{3,2},{4,5},{5,4},{6,7},{7,6},{8,9},{9,8},{10,11... | collective-permute-start | bytes 1572872 | tf_op jit(solution)/shard_map/ppermute | solution.py:330
  290.6 45.7 %collective-permute-start.43 = (bf16[2,1024,128]{2,1,0:T(8,128)(2,1)}, bf16[2,1024,128]{2,1,0:T(8,128)(2,1)S(1)}, u32[]{:S(2)}, u32[]{:S(2)}) collective-permute-start(bf16[2,1024,128]{2,1,0:T(8,128)(2,1)} %get-tuple-element.89), channel_id=1, source_target_pairs={{8,4},{12,8},{9,5},{13,9},{10,6},{14,10},{11,7},{15,11},{24,20},{2... | collective-permute-start | bytes 1572872 | tf_op jit(solution)/shard_map/ppermute | solution.py:587
  291.3 45.1 %collective-permute-start.44 = (bf16[2,1024,128]{2,1,0:T(8,128)(2,1)}, bf16[2,1024,128]{2,1,0:T(8,128)(2,1)S(1)}, u32[]{:S(2)}, u32[]{:S(2)}) collective-permute-start(bf16[2,1024,128]{2,1,0:T(8,128)(2,1)} %get-tuple-element.89), channel_id=1, source_target_pairs={{0,4},{4,8},{1,5},{5,9},{2,6},{6,10},{3,7},{7,11},{16,20},{20,24},... | collective-permute-start | bytes 1572872 | tf_op jit(solution)/shard_map/ppermute | solution.py:588
  295.7 40.6 %collective-permute-start.45 = (bf16[256,512]{1,0:T(8,128)(2,1)S(1)}, bf16[256,512]{1,0:T(8,128)(2,1)S(1)}, u32[]{:S(2)}, u32[]{:S(2)}) collective-permute-start(bf16[256,512]{1,0:T(8,128)(2,1)S(1)} %add_convert_fusion.9), channel_id=1, source_target_pairs={{0,8},{4,12},{8,0},{12,4},{1,9},{5,13},{9,1},{13,5},{2,10},{6,14},... | collective-permute-start | bytes 786440 | tf_op jit(solution)/shard_map/ppermute | solution.py:383
  301.8 34.6 %collective-permute-start.46 = (bf16[256,1024]{1,0:T(8,128)(2,1)}, bf16[256,1024]{1,0:T(8,128)(2,1)S(1)}, u32[]{:S(2)}, u32[]{:S(2)}) collective-permute-start(bf16[256,1024]{1,0:T(8,128)(2,1)} %select_convert_fusion.1), channel_id=1, source_target_pairs={{0,4},{4,0},{8,12},{12,8},{1,5},{5,1},{9,13},{13,9},{2,6},{6,2},{1... | collective-permute-start | bytes 1572872 | tf_op jit(solution)/shard_map/ppermute | solution.py:383
  309.0 27.4 %collective-permute-start.49 = (bf16[256,512]{1,0:T(8,128)(2,1)S(1)}, bf16[256,512]{1,0:T(8,128)(2,1)S(1)}, u32[]{:S(2)}, u32[]{:S(2)}) collective-permute-start(bf16[256,512]{1,0:T(8,128)(2,1)S(1)} %convolution_convert_fusion.13), channel_id=1, source_target_pairs={{0,16},{16,0},{1,17},{17,1},{2,18},{18,2},{3,19},{19,3},{4,20},{20... | collective-permute-start | bytes 786440 | tf_op jit(solution)/shard_map/ppermute | solution.py:379
  337.6 26.5 %collective-permute-start.52 = (bf16[2,1024,128]{2,1,0:T(8,128)(2,1)}, bf16[2,1024,128]{2,1,0:T(8,128)(2,1)S(1)}, u32[]{:S(2)}, u32[]{:S(2)}) collective-permute-start(bf16[2,1024,128]{2,1,0:T(8,128)(2,1)} %get-tuple-element.97), channel_id=1, source_target_pairs={{8,4},{12,8},{9,5},{13,9},{10,6},{14,10},{11,7},{15,11},{24,20},{2... | collective-permute-start | bytes 1572872 | tf_op jit(solution)/shard_map/ppermute | solution.py:617
  338.4 25.7 %collective-permute-start.53 = (bf16[2,1024,128]{2,1,0:T(8,128)(2,1)}, bf16[2,1024,128]{2,1,0:T(8,128)(2,1)S(1)}, u32[]{:S(2)}, u32[]{:S(2)}) collective-permute-start(bf16[2,1024,128]{2,1,0:T(8,128)(2,1)} %get-tuple-element.97), channel_id=1, source_target_pairs={{0,4},{4,8},{1,5},{5,9},{2,6},{6,10},{3,7},{7,11},{16,20},{20,24},... | collective-permute-start | bytes 1572872 | tf_op jit(solution)/shard_map/ppermute | solution.py:618
  343.2 20.8 %collective-permute-start.50 = (bf16[2,1024,128]{2,1,0:T(8,128)(2,1)S(1)}, bf16[2,1024,128]{2,1,0:T(8,128)(2,1)S(1)}, u32[]{:S(2)}, u32[]{:S(2)}) collective-permute-start(bf16[2,1024,128]{2,1,0:T(8,128)(2,1)S(1)} %add_convert_fusion.5), channel_id=1, source_target_pairs={{12,8},{8,4},{4,0},{13,9},{9,5},{5,1},{14,10},{10,6},{6,2},{15,11}... | collective-permute-start | bytes 1572872 | tf_op jit(solution)/shard_map/ppermute | solution.py:612
  368.2 18.8 %collective-permute-start.55 = (bf16[2,1024,128]{2,1,0:T(8,128)(2,1)}, bf16[2,1024,128]{2,1,0:T(8,128)(2,1)S(1)}, u32[]{:S(2)}, u32[]{:S(2)}) collective-permute-start(bf16[2,1024,128]{2,1,0:T(8,128)(2,1)} %add_convert_fusion.2), channel_id=1, source_target_pairs={{12,8},{8,4},{4,0},{13,9},{9,5},{5,1},{14,10},{10,6},{6,2},{15,11}... | collective-permute-start | bytes 1572872 | tf_op jit(solution)/shard_map/ppermute | solution.py:612
  405.1 23.0 %collective-permute-start.63 = (bf16[512,512]{1,0:T(8,128)(2,1)S(1)}, bf16[512,512]{1,0:T(8,128)(2,1)S(1)}, u32[]{:S(2)}, u32[]{:S(2)}) collective-permute-start(bf16[512,512]{1,0:T(8,128)(2,1)S(1)} %copy-done.4), channel_id=1, source_target_pairs={{0,4},{4,0},{8,12},{12,8},{1,5},{5,1},{9,13},{13,9},{2,6},{6,2},{1... | collective-permute-start | bytes 1572872 | tf_op jit(solution)/shard_map/ppermute | solution.py:383
  407.4 22.4 %collective-permute-start.59 = (bf16[256,1024]{1,0:T(8,128)(2,1)}, bf16[256,1024]{1,0:T(8,128)(2,1)}, u32[]{:S(2)}, u32[]{:S(2)}) collective-permute-start(bf16[256,1024]{1,0:T(8,128)(2,1)} %get-tuple-element.145), channel_id=1, source_target_pairs={{0,1},{1,0},{2,3},{3,2},{4,5},{5,4},{6,7},{7,6},{8,9},{9,8},{10,11... | collective-permute-start | bytes 1572872 | tf_op jit(solution)/shard_map/ppermute | solution.py:330
  409.1 19.0 %collective-permute-start.61 = (bf16[256,1024]{1,0:T(8,128)(2,1)S(1)}, bf16[256,1024]{1,0:T(8,128)(2,1)S(1)}, u32[]{:S(2)}, u32[]{:S(2)}) collective-permute-start(bf16[256,1024]{1,0:T(8,128)(2,1)S(1)} %fusion.7), channel_id=1, source_target_pairs={{0,2},{1,3},{2,0},{3,1},{4,6},{5,7},{6,4},{7,5},{8,10},{9,11},{10,... | collective-permute-start | bytes 1572872 | tf_op jit(solution)/shard_map/ppermute | solution.py:330
  431.8 19.9 %collective-permute-start.66 = (bf16[256,1024]{1,0:T(8,128)(2,1)S(1)}, bf16[256,1024]{1,0:T(8,128)(2,1)S(1)}, u32[]{:S(2)}, u32[]{:S(2)}) collective-permute-start(bf16[256,1024]{1,0:T(8,128)(2,1)S(1)} %fusion.10), channel_id=1, source_target_pairs={{0,2},{1,3},{2,0},{3,1},{4,6},{5,7},{6,4},{7,5},{8,10},{9,11},{10,... | collective-permute-start | bytes 1572872 | tf_op jit(solution)/shard_map/ppermute | solution.py:330
  432.7 19.0 %collective-permute-start.67 = (bf16[256,1024]{1,0:T(8,128)(2,1)S(1)}, bf16[256,1024]{1,0:T(8,128)(2,1)S(1)}, u32[]{:S(2)}, u32[]{:S(2)}) collective-permute-start(bf16[256,1024]{1,0:T(8,128)(2,1)S(1)} %fusion.10), channel_id=1, source_target_pairs={{0,1},{1,0},{2,3},{3,2},{4,5},{5,4},{6,7},{7,6},{8,9},{9,8},{10,11... | collective-permute-start | bytes 1572872 | tf_op jit(solution)/shard_map/ppermute | solution.py:330
  433.7 20.1 %collective-permute-start.69 = (bf16[256,1024]{1,0:T(8,128)(2,1)S(1)}, bf16[256,1024]{1,0:T(8,128)(2,1)}, u32[]{:S(2)}, u32[]{:S(2)}) collective-permute-start(bf16[256,1024]{1,0:T(8,128)(2,1)S(1)} %select_convert_fusion), channel_id=1, source_target_pairs={{0,4},{4,0},{8,12},{12,8},{1,5},{5,1},{9,13},{13,9},{2,6},{6,2},{1... | collective-permute-start | bytes 1572872 | tf_op jit(solution)/shard_map/ppermute | solution.py:383
  470.3 21.6 %collective-permute-start.74 = (bf16[256,1024]{1,0:T(8,128)(2,1)S(1)}, bf16[256,1024]{1,0:T(8,128)(2,1)S(1)}, u32[]{:S(2)}, u32[]{:S(2)}) collective-permute-start(bf16[256,1024]{1,0:T(8,128)(2,1)S(1)} %pad_maximum_fusion.29), channel_id=1, source_target_pairs={{0,4},{4,0},{8,12},{12,8},{1,5},{5,1},{9,13},{13,9},{2,6},{6,2},{1... | collective-permute-start | bytes 1572872 | tf_op jit(solution)/shard_map/ppermute | solution.py:383
  475.1 18.6 %collective-permute-start.70 = (bf16[256,1024]{1,0:T(8,128)(2,1)S(1)}, bf16[256,1024]{1,0:T(8,128)(2,1)S(1)}, u32[]{:S(2)}, u32[]{:S(2)}) collective-permute-start(bf16[256,1024]{1,0:T(8,128)(2,1)S(1)} %copy-done.34), channel_id=1, source_target_pairs={{0,1},{1,0},{2,3},{3,2},{4,5},{5,4},{6,7},{7,6},{8,9},{9,8},{10,11... | collective-permute-start | bytes 1572872 | tf_op jit(solution)/shard_map/ppermute | solution.py:330
  (190 other events, 1407.0 us)

commit v3 on v2

--- a/solution.py
+++ b/solution.py
@@ -10,6 +10,7 @@
 
 HEAD_DIM = 64
 BLK = 256
+PAD_ROWS = 16
 LOW = -1e30
 norm_eps = 1e-12
 f32 = jnp.float32
@@ -204,11 +205,7 @@
         out_shape=[jax.ShapeDtypeStruct((rows, width), bf16), stats]
         if closes
         else [stats, stats, jax.ShapeDtypeStruct((width, rows), f32)],
-        cost_estimate=pl.CostEstimate(
-            flops=20 * rows * keys * width,
-            bytes_accessed=4 * keys * width,
-            transcendentals=rows * keys * heads // 2,
-        ),
+        cost_estimate=pl.CostEstimate(flops=1024, bytes_accessed=1024, transcendentals=0),
         name="attend_near" if opens else "attend_far",
     )(info, q, *sources, *(() if opens else state))
 
@@ -317,13 +314,59 @@
         ),
         out_shape=[jax.ShapeDtypeStruct((rows, width), bf16)]
         + [jax.ShapeDtypeStruct(pair, bf16)] * 4,
-        cost_estimate=pl.CostEstimate(
-            flops=30 * rows * keys * width,
-            bytes_accessed=8 * keys * width,
-            transcendentals=rows * keys * heads // 2,
-        ),
+        cost_estimate=pl.CostEstimate(flops=1024, bytes_accessed=1024, transcendentals=0),
         name="attend_back",
     )(info, q, do, o, lse.reshape(-1, heads, rows), *sources)
+
+
+def qkv_terms_kernel(order, *refs):
+    rows, (dq_1, dq_2), pairs = refs[:8], refs[8:10], refs[10:18]
+    sent_ref, mine_ref = refs[18:]
+    size = rows[0].shape[0]
+    query, key_value = None, None
+    for n, rows_ref in enumerate(rows):
+        left = rows_ref[...]
+        span = slice((n % 2) * size, (n % 2 + 1) * size)
+        first, second = pairs[n // 2 * 2], pairs[n // 2 * 2 + 1]
+        grads = jnp.concatenate(
+            [first[0, span], second[0, span], first[1, span], second[1, span]], axis=1
+        )
+        term = tn(left, grads)
+        key_value = term if key_value is None else key_value + term
+        if n < 2:
+            term = tn(left, jnp.concatenate([dq_1[span], dq_2[span]], axis=1))
+            query = term if query is None else query + term
+    total = jnp.concatenate([query, key_value], axis=1)
+
+    @pl.when(pl.program_id(0) == 0)
+    def _():
+        sent_ref[...] = total.astype(sent_ref.dtype)
+
+    @pl.when(pl.program_id(0) == 1)
+    def _():
+        mine_ref[...] = total
+
+
+def qkv_terms_of(rows, queries, pairs, order, sent_type):
+    size, depth = rows[0].shape
+    half = depth // 2
+    wide = 2 * (queries[0].shape[1] + 2 * pairs[0].shape[2])
+    return pl.pallas_call(
+        qkv_terms_kernel,
+        grid_spec=pltpu.PrefetchScalarGridSpec(
+            num_scalar_prefetch=1,
+            grid=(2,),
+            in_specs=[pl.BlockSpec((size, half), lambda i, pick: (0, pick[i]))] * 8
+            + [whole(x.shape) for x in (*queries, *pairs)],
+            out_specs=[whole((half, wide)), whole((half, wide))],
+        ),
+        out_shape=[
+            jax.ShapeDtypeStruct((half, wide), sent_type),
+            jax.ShapeDtypeStruct((half, wide), f32),
+        ],
+        cost_estimate=pl.CostEstimate(flops=1024, bytes_accessed=1024, transcendentals=0),
+        name="qkv_terms",
+    )(order, *rows, *queries, *pairs)
 
 
 def tp_swap(x, bit):
@@ -482,36 +525,36 @@
     w_all = jnp.concatenate([w_q, w_k, w_v], axis=1)
     w_kv = w_all[:, width:]
     own = [nn(rows, w_all).astype(bf16) for rows in (half_a, half_b)]
-    near = [
-        nn(rows, w_kv).astype(bf16)
-        for rows in (left_a, tp_swap(left_a, 1), right_a, tp_swap(right_a, 1))
-    ]
+    left_b, right_b = tp_swap(left_a, 1), tp_swap(right_a, 1)
+    near = [nn(rows, w_kv).astype(bf16) for rows in (left_a, left_b, right_a, right_b)]
     queries = jnp.concatenate([part[:, :width] for part in own])
     own_at, other_at = (width, 2 * width), (0, width)
     near_at = (own_at,) * 2 + (other_at,) * 4
     state = attend(info, queries, own + near, near_at, 7)
-    far_left, far_right = gate((far_left, far_right), state[0])
+    out_y = tp_swap(own_out, 2)
+    out_rows = (own_out, out_y, tp_swap(own_out, 1), tp_swap(out_y, 1))
+    far_left, far_right = gate((far_left, far_right), state[0], got_up, got_down, *out_rows)
     far_a = jnp.where(place >= 2, far_left, far_right)
-    out_y = tp_swap(own_out, 2)
-    out_all = jnp.concatenate([own_out, out_y, tp_swap(own_out, 1), tp_swap(out_y, 1)])
-    far = [nn(rows, w_kv).astype(bf16) for rows in (far_a, tp_swap(far_a, 1))]
+    far_b = tp_swap(far_a, 1)
+    far = [nn(rows, w_kv).astype(bf16) for rows in (far_a, far_b)]
     context, log_totals = attend(info, queries, far, (other_at,) * 2, 19, state, True)
-    (context,) = gate((context,), got_up, got_down, out_all)
 
     pieces = jnp.split(context, 4)
-    context_own = jnp.concatenate(
-        [pieces[0]] + [tp_swap(pieces[n], order[n]) for n in (1, 2, 3)], axis=1
-    )
-    resid_rows = quarter_of(tokens, 0).astype(f32) + nn(context_own, out_all)
+    arrived = [pieces[0]] + [tp_swap(pieces[n], order[n]) for n in (1, 2, 3)]
+    resid_rows = quarter_of(tokens, 0).astype(f32)
+    for piece, rows in zip(arrived, out_rows):
+        resid_rows = resid_rows + nn(piece, rows)
     normed_first, inverse_first = norm_rows(resid_rows)
     hidden = normed_first * gain[0] + shift[0]
-    hid0, hid1, hid2, hid3 = rows_out(hidden.astype(bf16))
-    hid_near, hid_far = jnp.concatenate([hid0, hid1]), jnp.concatenate([hid2, hid3])
-
+    hid0 = hidden.astype(bf16)
+    hid2, hid1 = tp_swap(hid0, 2), tp_swap(hid0, 1)
+    hid_near = jnp.concatenate([hid0, hid1])
     act_near, slope_near = gelu_pair(nn(hid_near, full_up))
+    terms_near = nn(act_near, full_down)
+    hid2, terms_near = gate((hid2, terms_near))
+    hid_far = jnp.concatenate([hid2, tp_swap(hid2, 1)])
     act_far, slope_far = gelu_pair(nn(hid_far, full_up))
     terms_far = nn(act_far, full_down)
-    terms_near = nn(act_near, full_down)
     ffn_rows = rows_in(
         (terms_near[:quarter], terms_near[quarter:], terms_far[:quarter], terms_far[quarter:])
     )
@@ -520,48 +563,50 @@
     grad_rows = quarter_of(out_grad, 0).astype(f32)
     grad_mid = norm_back(grad_rows, gain[1], normed_second, inverse_second)
 
-    mid0, mid1, mid2, mid3 = rows_out(grad_mid.astype(bf16))
-    mid_near, mid_far = jnp.concatenate([mid0, mid1]), jnp.concatenate([mid2, mid3])
-
-    def column_block(left, right):
-        return lambda start, size: tn(left, lax.dynamic_slice_in_dim(right, start, size, axis=1))
-
-    def row_block(left, right):
-        return lambda start, size: tn(lax.dynamic_slice_in_dim(left, start, size, axis=1), right)
-
-    act_all = jnp.concatenate([act_near, act_far])
-    mid_all = jnp.concatenate([mid_near, mid_far])
-    down_terms, down_send = fsdp_send(column_block(act_all, mid_all), depth, 1)
+    mid0 = grad_mid.astype(bf16)
+    mid2, mid1 = tp_swap(mid0, 2), tp_swap(mid0, 1)
+    mid_near = jnp.concatenate([mid0, mid1])
+    pre_near = (nt(mid_near, full_down) * slope_near).astype(bf16)
+    terms_near = nt(pre_near, full_up)
+    mid2, terms_near = gate((mid2, terms_near))
+    mid_far = jnp.concatenate([mid2, tp_swap(mid2, 1)])
+
+    def column_block(*pairs):
+        return lambda start, size: sum(
+            tn(left, lax.dynamic_slice_in_dim(right, start, size, axis=1)) for left, right in pairs
+        )
+
+    def row_block(*pairs):
+        return lambda start, size: sum(
+            tn(lax.dynamic_slice_in_dim(left, start, size, axis=1), right) for left, right in pairs
+        )
+
+    down_terms, down_send = fsdp_send(
+        column_block((act_near, mid_near), (act_far, mid_far)), depth, 1
+    )
     down_got = fsdp_swap(down_send)
 
-    pre_near = (nt(mid_near, full_down) * slope_near).astype(bf16)
     pre_far = (nt(mid_far, full_down) * slope_far).astype(bf16)
     terms_far = nt(pre_far, full_up)
-    terms_near = nt(pre_near, full_up)
     hidden_grad = grad_mid + rows_in(
         (terms_near[:quarter], terms_near[quarter:], terms_far[:quarter], terms_far[quarter:])
     )
-    hid_all = jnp.concatenate([hid_near, hid_far])
-    pre_all = jnp.concatenate([pre_near, pre_far])
-    up_terms, up_send = fsdp_send(row_block(hid_all, pre_all), depth, 0)
+    up_terms, up_send = fsdp_send(row_block((hid_near, pre_near), (hid_far, pre_far)), depth, 0)
     resid_grad = norm_back(hidden_grad, gain[0], normed_first, inverse_first)
     attn_own = resid_grad.astype(bf16)
 
     attn_own, up_send, down_got = gate((attn_own, up_send, down_got))
     up_got = fsdp_swap(up_send)
-    down_kept, send = ctx_split(down_terms + down_got.astype(f32), 1)
+    down_terms = down_terms + down_got.astype(f32)
+    share = up_terms.shape[0]
+    down_terms = jnp.concatenate(jnp.split(down_terms, depth // share), axis=1)
+    down_kept, send = ctx_split(down_terms, 1)
     down_got = ctx_swap(send, 1)
-    back_own = nt(attn_own, out_all).astype(bf16)
-    pieces = jnp.split(back_own, 4, axis=1)
+    pieces = [nt(attn_own, rows).astype(bf16) for rows in out_rows]
     context_grad = jnp.concatenate(
         [pieces[0]] + [tp_swap(pieces[n], order[n]) for n in (1, 2, 3)]
     )
 
-    context_grad, down_got, attn_own, result = gate((context_grad, down_got, attn_own, result))
-    down_kept, send = ctx_split(down_kept + down_got.astype(f32), 2)
-    down_got = ctx_swap(send, 2)
-    attn_near, attn_far = tp_swap(attn_own, 1), tp_swap(attn_own, 2)
-    result_near, result_far = tp_swap(result, 1), tp_swap(result, 2)
     vectors = jnp.stack(
         [
             jnp.sum(hidden_grad * normed_first, axis=0),
@@ -570,7 +615,13 @@
             jnp.sum(grad_rows, axis=0),
         ]
     )
-    vectors_got = tp_swap(vectors, 1)
+    spread = jnp.concatenate(
+        [attn_own, result, jnp.pad(vectors, ((0, PAD_ROWS - 4), (0, 0))).astype(bf16)]
+    )
+    context_grad, spread, down_got = gate((context_grad, spread, down_got))
+    down_kept, send = ctx_split(down_kept + down_got.astype(f32), 2)
+    down_got = ctx_swap(send, 2)
+    spread_far, spread_near = tp_swap(spread, 2), tp_swap(spread, 1)
 
     sources = own + near + far
     sources_at = (own_at,) * 2 + (other_at,) * 6
@@ -578,136 +629,139 @@
     dq_1, own_1, left_1, right_1, far_1 = attend_back(
         info, queries, context_grad, context, log_totals, sources, sources_at, 7, 0, part
     )
-    info_2, far_1, down_got, up_got, attn_far, result_far, vectors_got = gate(
-        (info, far_1, down_got, up_got, attn_far, result_far, vectors_got),
-        attn_near,
-        result_near,
-    )
-    left_hop, right_hop = [(2, 1), (3, 2)], [(0, 1), (1, 2)]
-    from_left_1 = lax.ppermute(far_1, "ctx", left_hop)
-    from_right_1 = lax.ppermute(far_1, "ctx", right_hop)
-    down_total = (down_kept + down_got.astype(f32)).astype(bf16)
-    down_total = lax.optimization_barrier(down_total)
+    info_2, far_1, left_1, right_1, down_got, up_got, spread_far = gate(
+        (info, far_1, left_1, right_1, down_got, up_got, spread_far), spread_near
+    )
+    spread_both = tp_swap(spread_far, 1)
+
+    def home(left_kv, right_kv, far_kv):
+        return (
+            ctx_swap(far_kv, 2),
+            lax.ppermute(left_kv, "ctx", [(3, 2), (2, 1), (1, 0)]),
+            lax.ppermute(right_kv, "ctx", [(0, 1), (1, 2), (2, 3)]),
+        )
+
+    home_1 = home(left_1, right_1, far_1)
+    up_kept, up_send = ctx_split(up_terms + up_got.astype(f32), 1)
+    down_total = lax.optimization_barrier((down_kept + down_got.astype(f32)).astype(bf16))
+    info_2, up_send, down_total = gate((info_2, up_send, down_total), spread_both)
+    up_got = ctx_swap(up_send, 1)
     down_got = ctx_swap(down_total, 2)
-    up_kept, send = ctx_split(up_terms + up_got.astype(f32), 1)
-    up_got = ctx_swap(send, 1)
-    attn_all = jnp.concatenate([attn_own, attn_far, attn_near, tp_swap(attn_far, 1)])
-    result_parts = (result, result_near, result_far, tp_swap(result_far, 1))
-    out_terms, out_send = fsdp_send(column_block(context, attn_all), depth, 1)
-    out_got = fsdp_swap(out_send)
-    vectors = vectors + vectors_got
-    vectors_got = tp_swap(vectors, 2)
 
     dq_2, own_2, left_2, right_2, far_2 = attend_back(
         info_2, queries, context_grad, context, log_totals, sources, sources_at, 7, 1, part
     )
-    far_2, from_left_1, from_right_1, down_got, up_got, vectors_got = gate(
-        (far_2, from_left_1, from_right_1, down_got, up_got, vectors_got), out_got
-    )
-
-    def hop(own_kv, left_kv, right_kv, from_left, from_right):
-        left_sum = (left_kv.astype(f32) + from_left.astype(f32)).astype(bf16)
-        right_sum = (right_kv.astype(f32) + from_right.astype(f32)).astype(bf16)
-        return (
-            lax.ppermute(left_sum, "ctx", [(3, 2), (2, 1), (1, 0)]),
-            lax.ppermute(right_sum, "ctx", [(0, 1), (1, 2), (2, 3)]),
+    (
+        far_2, left_2, right_2, down_got, up_got, *home_1,
+        own_1, own_2, dq_1, dq_2, left_1, right_1, far_1,
+        spread, spread_near, spread_far, spread_both,
+    ) = gate(
+        (
+            far_2, left_2, right_2, down_got, up_got, *home_1,
+            own_1, own_2, dq_1, dq_2, left_1, right_1, far_1,
+            spread, spread_near, spread_far, spread_both,
         )
-
-    home_1 = hop(own_1, left_1, right_1, from_left_1, from_right_1)
-    from_left_2 = lax.ppermute(far_2, "ctx", left_hop)
-    from_right_2 = lax.ppermute(far_2, "ctx", right_hop)
-    vectors = vectors + vectors_got
-    vectors_got = ctx_swap(vectors, 1)
-    down_total = ctx_join(down_total, down_got, 2)
-    up_kept, up_send = ctx_split(up_kept + up_got.astype(f32), 2)
-
-    home_1a, home_1b, from_left_2, from_right_2, vectors_got, down_total, up_send = gate(
-        (*home_1, from_left_2, from_right_2, vectors_got, down_total, up_send)
-    )
-    home_2 = hop(own_2, left_2, right_2, from_left_2, from_right_2)
-    rows_own = jnp.concatenate([half_a, half_b])
-    total_1 = (own_1.astype(f32) + home_1a.astype(f32) + home_1b.astype(f32)).astype(bf16)
-    grads_1 = jnp.concatenate([dq_1, dq_2, total_1[0], total_1[1]], axis=1)
-    qkv_terms_1, qkv_send_1 = fsdp_send(row_block(rows_own, grads_1), depth, 0)
-    qkv_got_1 = fsdp_swap(qkv_send_1)
-    weights_1 = jnp.concatenate([w_q, w_k[:, :part], w_v[:, :part]], axis=1)
-    weights_2 = jnp.concatenate([w_k[:, part:], w_v[:, part:]], axis=1)
-    terms_1 = nt(grads_1, weights_1)
-    vectors = vectors + vectors_got
-    vectors_got = ctx_swap(vectors, 2)
-
-    home_2a, home_2b, qkv_got_1, vectors_got, down_total, up_send = gate(
-        (*home_2, qkv_got_1, vectors_got, down_total, up_send)
-    )
-    total_2 = (own_2.astype(f32) + home_2a.astype(f32) + home_2b.astype(f32)).astype(bf16)
-    grads_2 = jnp.concatenate([total_2[0], total_2[1]], axis=1)
-    terms = terms_1 + nt(grads_2, weights_2)
+    )
+    home_2 = home(left_2, right_2, far_2)
+    up_kept, send = ctx_split(up_kept + up_got.astype(f32), 2)
+    up_got = ctx_swap(send, 2)
+
+    held = (spread, spread_near, spread_far, spread_both)
+    result_parts = [x[quarter : 2 * quarter] for x in held]
+    attn_all = jnp.concatenate([held[n][:quarter] for n in order])
+    vectors = sum(x[2 * quarter :].astype(f32) for x in held)
+
+    def rest_of(qkv_terms, start, size):
+        right = lax.dynamic_slice_in_dim(attn_all, start, size, axis=1)
+        extra = lax.dynamic_slice_in_dim(vectors, start, size, axis=1)
+        rows = qkv_terms.shape[0]
+        terms = tn(context, right).astype(qkv_terms.dtype).reshape(rows, -1)
+        terms = jnp.concatenate([qkv_terms, terms], axis=1)
+        extra = jnp.pad(extra, ((0, PAD_ROWS), (0, terms.shape[1] - size)))
+        return jnp.concatenate([terms, extra.astype(terms.dtype)])
+
+    pairs = (own_1, own_2, left_1, left_2, right_1, right_2, far_1, far_2)
+    rows = (half_a, half_b, left_a, left_b, right_a, right_b, far_a, far_b)
+    if lax.axis_size("fsdp") == 2:
+        mine = lax.axis_index("fsdp")
+        picks = jnp.stack([1 - mine, mine]).astype(jnp.int32)
+        half = depth // 2
+        qkv_send, qkv_terms = qkv_terms_of(rows, (dq_1, dq_2), pairs, picks, bf16)
+        rest_got = fsdp_swap(rest_of(qkv_send, (1 - mine) * half, half))
+        rest = rest_of(qkv_terms, mine * half, half)
+    else:
+        halves = qkv_terms_of(rows, (dq_1, dq_2), pairs, jnp.arange(2, dtype=jnp.int32), f32)
+        qkv_terms = lax.psum_scatter(
+            jnp.concatenate(halves), "fsdp", scatter_dimension=0, tiled=True
+        )
+        out_terms = lax.psum_scatter(
+            jnp.concatenate([tn(context, attn_all), vectors]), "fsdp",
+            scatter_dimension=1, tiled=True,
+        )
+        rest = jnp.concatenate(
+            [qkv_terms, out_terms[:width].reshape(qkv_terms.shape[0], -1)], axis=1
+        )
+        extra = out_terms[width:]
+        extra = jnp.pad(extra, ((0, PAD_ROWS), (0, rest.shape[1] - extra.shape[1])))
+        rest = jnp.concatenate([rest, extra])
+        rest_got = jnp.zeros(rest.shape, bf16)
+    query_grad = jnp.concatenate([dq_1, dq_2], axis=1)
+
+    def owned(own_kv, arrivals):
+        total = own_kv.astype(f32)
+        for arrival in arrivals:
+            total = total + arrival.astype(f32)
+        return total.astype(bf16)
+
+    total_1 = owned(own_1, home_1)
+    input_terms = (
+        nt(query_grad, w_q) + nt(total_1[0], w_k[:, :part]) + nt(total_1[1], w_v[:, :part])
+    )
+    *home_2, rest_got, up_got = gate((*home_2, rest_got, up_got), input_terms)
+    total_2 = owned(own_2, home_2)
+    terms = input_terms + nt(total_2[0], w_k[:, part:]) + nt(total_2[1], w_v[:, part:])
     q0, q2, q1, q3 = jnp.split(terms, 4)
     toward = q2 + tp_swap(q3.astype(bf16), 1).astype(f32)
     input_got = tp_swap(toward.astype(bf16), 2)
     here = q0 + tp_swap(q1.astype(bf16), 1).astype(f32)
-    qkv_terms_2, qkv_send_2 = fsdp_send(row_block(rows_own, grads_2), depth, 0)
-    qkv_got_2 = fsdp_swap(qkv_send_2)
-    down_got = ctx_swap(down_total, 1)
-    up_got = ctx_swap(up_send, 2)
-    vectors = vectors + vectors_got
-    split_vectors = lax.axis_size("fsdp") == 2
-    if split_vectors:
-        half = depth // 2
-        mine = lax.axis_index("fsdp")
-        vectors_got = fsdp_swap(
-            lax.dynamic_slice_in_dim(vectors, (1 - mine) * half, half, axis=1)
-        )
-        vectors = lax.dynamic_slice_in_dim(vectors, mine * half, half, axis=1)
-    else:
-        vectors = lax.psum_scatter(vectors, "fsdp", scatter_dimension=1, tiled=True)
-        vectors_got = jnp.zeros_like(vectors)
-
-    input_got, qkv_got_2, down_got, up_got, vectors_got = gate(
-        (input_got, qkv_got_2, down_got, up_got, vectors_got)
-    )
-    vectors = vectors + vectors_got
-    input_own = (resid_grad + here + input_got.astype(f32)).astype(bf16)
-    input_near, input_far = tp_swap(input_own, 1), tp_swap(input_own, 2)
-    down_grad = ctx_join(down_total, down_got, 1).astype(f32)
     up_total = lax.optimization_barrier((up_kept + up_got.astype(f32)).astype(bf16))
     up_got = ctx_swap(up_total, 2)
-    out_shape = out_terms.shape
-    rest = jnp.concatenate(
-        [
-            qkv_terms_1 + qkv_got_1.astype(f32),
-            qkv_terms_2 + qkv_got_2.astype(f32),
-            (out_terms + out_got.astype(f32)).reshape(qkv_terms_1.shape[0], -1),
-        ],
-        axis=1,
-    )
-    rest_kept, send = ctx_split(rest, 1)
-    rest_got = ctx_swap(send, 1)
-
-    input_far, input_near, up_got, rest_got = gate((input_far, input_near, up_got, rest_got))
+    out_shape = (width, depth // lax.axis_size("fsdp"))
+    rest = rest + rest_got.astype(f32)
+    fourth = rest.shape[0] // 4
+
+    def fourth_of(shift):
+        return lax.dynamic_slice_in_dim(rest, (place ^ shift) * fourth, fourth)
+
+    rest_kept = fourth_of(0)
+    rest_got = [ctx_swap(fourth_of(shift).astype(bf16), shift) for shift in (1, 2, 3)]
+
+    input_got, up_got, *rest_got = gate((input_got, up_got, *rest_got))
+    input_own = (resid_grad + here + input_got.astype(f32)).astype(bf16)
+    input_far, input_near = tp_swap(input_own, 2), tp_swap(input_own, 1)
+    for got in rest_got:
+        rest_kept = rest_kept + got.astype(f32)
+    rest_total = lax.optimization_barrier(rest_kept.astype(bf16))
+    rest_parts = (rest_total, *(ctx_swap(rest_total, shift) for shift in (1, 2, 3)))
+    ffn_total = jnp.concatenate(
+        [ctx_join(down_total, down_got, 2), ctx_join(up_total, up_got, 2)]
+    )
+    ffn_got = ctx_swap(ffn_total, 1)
     input_parts = (input_own, input_near, input_far, tp_swap(input_far, 1))
-    up_total = ctx_join(up_total, up_got, 2)
-    up_got = ctx_swap(up_total, 1)
-    rest_kept, send = ctx_split(rest_kept + rest_got.astype(f32), 2)
-    rest_got = ctx_swap(send, 2)
-    rest_total = (rest_kept + rest_got.astype(f32)).astype(bf16)
-    rest_total = lax.optimization_barrier(rest_total)
-    rest_total = ctx_join(rest_total, ctx_swap(rest_total, 2), 2)
-    rest_total = ctx_join(rest_total, ctx_swap(rest_total, 1), 1).astype(f32)
-    up_grad = ctx_join(up_total, up_got, 1).astype(f32)
-    qkv_1, qkv_2 = rest_total[:, : 2 * width], rest_total[:, 2 * width : 3 * width]
-    qkv_grad = jnp.stack(
-        [
-            qkv_1[:, :width],
-            jnp.concatenate([qkv_1[:, width : width + part], qkv_2[:, :part]], axis=1),
-            jnp.concatenate([qkv_1[:, width + part :], qkv_2[:, part:]], axis=1),
-        ]
-    )
+    down_grad, up_grad = (
+        ctx_join(total, got, 1).astype(f32)
+        for total, got in zip(jnp.split(ffn_total, 2), jnp.split(ffn_got, 2))
+    )
+    down_grad = jnp.concatenate(jnp.split(down_grad, depth // down_grad.shape[0], axis=1))
+    rest_total = natural(rest_parts, (place & 1) == 1, (place >> 1) == 1).astype(f32)
+    qkv_grad = jnp.stack([rest_total[:share, n * width : (n + 1) * width] for n in range(3)])
+    out_proj_grad = rest_total[:share, 3 * width :].reshape(out_shape)
+    vectors = rest_total[share : share + 4, : out_shape[1]]
     return (
         natural(result_parts, core, y),
         natural(input_parts, core, y),
         qkv_grad,
-        rest_total[:, 3 * width :].reshape(out_shape),
+        out_proj_grad,
         up_grad,
         down_grad,
         vectors[:2],

time: 514 us -> 491 us (0.955)
  Pallas kernels: 80.7 us -> 64.9 us
  matrix products: 63.2 us -> 56.1 us
  other arithmetic: 57.1 us -> 62.3 us
    pallas_call x2, Pallas kernels: 46.6 us -> 30.4 us  [attend_back(): pl.pallas_call(functools.partial(attend_back_kernel, heads, keys // BLK,...]
    pallas_call x0 -> x1, Pallas kernels: none -> 11.7 us  [qkv_terms_of(): pl.pallas_call(qkv_terms_kernel, grid_spec=pltpu.PrefetchScalarGridSpec(n...]
    pallas_call x2, Pallas kernels: 34.1 us -> 22.7 us  [attend(): pl.pallas_call(functools.partial(attend_kernel, heads, keys // BLK, kfirs...]
    ppermute x14 -> x15, waiting for transfers between devices: 68.5 us -> 76.9 us  [ctx_swap(): return lax.ppermute(x, 'ctx', [(i, i ^ bit) for i in range(4)])]
    ppermute x6 -> x3, starting transfers between devices: 10.7 us -> 2.36 us  [fsdp_swap(): return lax.ppermute(x, 'fsdp', [(0, 1), (1, 0)])]
    ppermute x14 -> x15, starting transfers between devices: 31.3 us -> 39.3 us  [ctx_swap(): return lax.ppermute(x, 'ctx', [(i, i ^ bit) for i in range(4)])]
    ppermute x38 -> x33, waiting for transfers between devices: 58.4 us -> 50.6 us  [tp_swap(): return lax.ppermute(x, 'tp', [(i, i ^ bit) for i in range(4)])]
    dot_general x30 -> x39, matrix products: 63.2 us -> 56.1 us  [contract(): lax.dot_general(left, right, (((left_dim,), (right_dim,)), ((), ())), pre...]
  transfers between devices with their start and end apart: 75 -> 64, of which waited for: 29 -> 26; matrix products, arithmetic and copies ran while one was open for 23% -> 24% of each run, Pallas kernels for 16% -> 12%
where the time goes in v3:
time: 491 us; the launch traced here: 486 us
  waiting for transfers between devices  173 us (35%)
  starting transfers between devices  92.4 us (19%)
  Pallas kernels  64.9 us (13%)
  other arithmetic  62.3 us (13%)
  matrix products  56.1 us (11%)
  local copies, waits for them, and re-layouts  34.4 us (7%)
    ppermute x15, waiting for transfers between devices, ctx_swap(): return lax.ppermute(x, 'ctx', [(i, i ^ bit) for i in range(4)])  76.9 us
    dot_general x39, matrix products, contract(): lax.dot_general(left, right, (((left_dim,), (right_dim,)), ((), ())), pre...  56.1 us
    ppermute x33, waiting for transfers between devices, tp_swap(): return lax.ppermute(x, 'tp', [(i, i ^ bit) for i in range(4)])  50.6 us
    ppermute x15, starting transfers between devices, ctx_swap(): return lax.ppermute(x, 'ctx', [(i, i ^ bit) for i in range(4)])  39.3 us
    pallas_call x2, Pallas kernels, attend_back(): pl.pallas_call(functools.partial(attend_back_kernel, heads, keys // BLK,...  30.4 us
    pallas_call x2, Pallas kernels, attend(): pl.pallas_call(functools.partial(attend_kernel, heads, keys // BLK, kfirs...  22.7 us
    ppermute x5, waiting for transfers between devices, fsdp_whole(): other = lax.ppermute(shard, 'fsdp', [(0, 1), (1, 0)])  19.8 us
    ppermute x3, waiting for transfers between devices, fsdp_swap(): return lax.ppermute(x, 'fsdp', [(0, 1), (1, 0)])  18.5 us
  transfers between devices with their start and end apart: 64, of which 26 were waited for; matrix products, arithmetic and copies ran while one was open for 24% of the time, Pallas kernels for 12%

profile of v3, /device:TPU:0, one launch (start us, length us, event | category | flops | bytes accessed | tf_op | source)
XLA Modules:
  0.0 486.1 jit_solution(9270382158091868441)
XLA Ops:
  0.6 3.0 collective-permute-start
  6.4 4.6 collective-permute-start.2
  13.4 8.1 %collective-permute-done = bf16[3,512,256]{2,1,0:T(8,128)(2,1)} collective-permute-done((bf16[3,512,256]{2,1,0:T(8,128)(2,1)}, bf16[3,512,256]{2,1,0:T(8,128)(2,1)}, u32[]{:S(2)}, u32[]{:S(2)}) %collective-permute-start) | collective-permute-done | bytes 786464 | tf_op jit(solution)/shard_map/ppermute | solution.py:403
  27.7 4.8 collective-permute-done.2.refs_2_
  41.2 6.9 %collective-permute-done.11.refs_6_ = bf16[256,1024]{1,0:T(8,128)(2,1)S(1)} collective-permute-done((bf16[256,1024]{1,0:T(8,128)(2,1)S(1)}, bf16[256,1024]{1,0:T(8,128)(2,1)S(1)}, u32[]{:S(2)}, u32[]{:S(2)}) %collective-permute-start.11) | collective-permute-done | bytes 524320 | tf_op jit(solution)/shard_map/ppermute | solution.py:373
  60.5 16.4 %attend_near.1 = (f32[4,1024]{1,0:T(4,128)}, f32[4,1024]{1,0:T(4,128)}, f32[256,1024]{1,0:T(8,128)}) custom-call(s32[23]{0:T(128)} %pad_add_fusion.info.refs_0_, bf16[1024,256]{1,0:T(8,128)(2,1)} %pad_maximum_fusion.21.q_ref, bf16[512,768]{1,0:T(8,128)(2,1)} %copy-done.15, bf16[512,768]{1,0:T(8,128)(2,1)} %copy-done.14, ...), custom_call_target="tpu_custom_call" | custom-call | flops 1024 | bytes 1024 | tf_op jit(solution)/shard_map/attend_near/pallas_call | solution.py:185
  76.9 10.1 %collective-permute-done.9.refs_4_ = bf16[1024,512]{1,0:T(8,128)(2,1)} collective-permute-done((bf16[1024,512]{1,0:T(8,128)(2,1)}, bf16[1024,512]{1,0:T(8,128)(2,1)}, u32[]{:S(2)}, u32[]{:S(2)}) %collective-permute-start.9) | collective-permute-done | bytes 1048608 | tf_op jit(solution)/shard_map/ppermute | solution.py:403
  89.5 3.2 collective-permute-start.1
  97.5 6.3 %attend_far.1 = (bf16[1024,256]{1,0:T(8,128)(2,1)}, f32[4,1024]{1,0:T(4,128)}) custom-call(s32[23]{0:T(128)} %pad_add_fusion.info.refs_0_, bf16[1024,256]{1,0:T(8,128)(2,1)} %pad_maximum_fusion.21.q_ref, bf16[512,512]{1,0:T(8,128)(2,1)} %convolution_convert_fusion.3.refs_0_.refs_6_, bf16[512,512]{1,0:T(8,128)(2,1)} %convolution_convert_fusion.2.refs_1_.refs_7_, ...), custom_call_target="tpu_custom_call" | custom-call | flops 1024 | bytes 1024 | tf_op jit(solution)/shard_map/attend_far/pallas_call | solution.py:185
  107.2 4.1 collective-permute-done.15
  125.2 7.2 %collective-permute-done.18.refs_0_ = bf16[256,1024]{1,0:T(8,128)(2,1)S(1)} collective-permute-done((bf16[256,1024]{1,0:T(8,128)(2,1)S(1)}, bf16[256,1024]{1,0:T(8,128)(2,1)S(1)}, u32[]{:S(2)}, u32[]{:S(2)}) %collective-permute-start.18) | collective-permute-done | bytes 524320 | tf_op jit(solution)/shard_map/ppermute | solution.py:373
  143.3 12.4 %collective-permute-done.23 = bf16[256,1024]{1,0:T(8,128)(2,1)S(1)} collective-permute-done((bf16[256,1024]{1,0:T(8,128)(2,1)S(1)}, bf16[256,1024]{1,0:T(8,128)(2,1)S(1)}, u32[]{:S(2)}, u32[]{:S(2)}) %collective-permute-start.23) | collective-permute-done | bytes 524320 | tf_op jit(solution)/shard_map/ppermute | solution.py:373
  164.6 8.2 %collective-permute-done.24.refs_0_ = bf16[256,1024]{1,0:T(8,128)(2,1)} collective-permute-done((bf16[256,1024]{1,0:T(8,128)(2,1)S(1)}, bf16[256,1024]{1,0:T(8,128)(2,1)}, u32[]{:S(2)}, u32[]{:S(2)}) %collective-permute-start.24) | collective-permute-done | bytes 524320 | tf_op jit(solution)/shard_map/ppermute | solution.py:373
  194.3 8.7 %collective-permute-done.29 = bf16[256,1024]{1,0:T(8,128)(2,1)S(1)} collective-permute-done((bf16[256,1024]{1,0:T(8,128)(2,1)S(1)}, bf16[256,1024]{1,0:T(8,128)(2,1)S(1)}, u32[]{:S(2)}, u32[]{:S(2)}) %collective-permute-start.29) | collective-permute-done | bytes 524320 | tf_op jit(solution)/shard_map/ppermute | solution.py:373
  206.6 5.1 %collective-permute-done.30.refs_2_ = bf16[1024,512]{1,0:T(8,128)(2,1)S(1)} collective-permute-done((bf16[1024,512]{1,0:T(8,128)(2,1)S(1)}, bf16[1024,512]{1,0:T(8,128)(2,1)S(1)}, u32[]{:S(2)}, u32[]{:S(2)}) %collective-permute-start.30) | collective-permute-done | bytes 1048608 | tf_op jit(solution)/shard_map/ppermute | solution.py:422
  220.7 9.9 %collective-permute-start.34 = (bf16[256,1024]{1,0:T(8,128)(2,1)S(1)}, bf16[256,1024]{1,0:T(8,128)(2,1)S(1)}, u32[]{:S(2)}, u32[]{:S(2)}) collective-permute-start(bf16[256,1024]{1,0:T(8,128)(2,1)S(1)} %select_convert_fusion.1), channel_id=1, source_target_pairs={{0,4},{4,0},{8,12},{12,8},{1,5},{5,1},{9,13},{13,9},{2,6},{6,2},{1... | collective-permute-start | bytes 1572872 | tf_op jit(solution)/shard_map/ppermute | solution.py:426
  233.0 9.5 %collective-permute-done.34.refs_2_ = bf16[256,1024]{1,0:T(8,128)(2,1)S(1)} collective-permute-done((bf16[256,1024]{1,0:T(8,128)(2,1)S(1)}, bf16[256,1024]{1,0:T(8,128)(2,1)S(1)}, u32[]{:S(2)}, u32[]{:S(2)}) %collective-permute-start.34) | collective-permute-done | bytes 524320 | tf_op jit(solution)/shard_map/ppermute | solution.py:426
  247.5 3.2 collective-permute-start.35
  252.8 15.2 %attend_back.2 = (bf16[1024,128]{1,0:T(8,128)(2,1)}, bf16[2,1024,128]{2,1,0:T(8,128)(2,1)}, bf16[2,1024,128]{2,1,0:T(8,128)(2,1)}, bf16[2,1024,128]{2,1,0:T(8,128)(2,1)}, bf16[2,1024,128]{2,1,0:T(8,128)(2,1)}) custom-call(s32[23]{0:T(128)} %pad_add_fusion.info.refs_0_, bf16[1024,256]{1,0:T(8,128)(2,1)} %pad_maximum_fusion.21.q_ref, ...), custom_call_target="tpu_custom_call" | custom-call | flops 1024 | bytes 1024 | tf_op jit(solution)/shard_map/attend_back/pallas_call | solution.py:289
  275.9 7.6 %collective-permute-start.42 = (bf16[2,1024,128]{2,1,0:T(8,128)(2,1)}, bf16[2,1024,128]{2,1,0:T(8,128)(2,1)}, u32[]{:S(2)}, u32[]{:S(2)}) collective-permute-start(bf16[2,1024,128]{2,1,0:T(8,128)(2,1)} %get-tuple-element.106.refs_14_), channel_id=1, source_target_pairs={{0,8},{4,12},{8,0},{12,4},{1,9},{5,13},{9,1},{13,5},{2,10},{6,14},... | collective-permute-start | bytes 1572872 | tf_op jit(solution)/shard_map/ppermute | solution.py:426
  284.8 5.5 %collective-permute-start.44 = (bf16[2,1024,128]{2,1,0:T(8,128)(2,1)}, bf16[2,1024,128]{2,1,0:T(8,128)(2,1)}, u32[]{:S(2)}, u32[]{:S(2)}) collective-permute-start(bf16[2,1024,128]{2,1,0:T(8,128)(2,1)} %get-tuple-element.108.refs_13_), channel_id=1, source_target_pairs={{0,4},{4,8},{8,12},{1,5},{5,9},{9,13},{2,6},{6,10},{10,14},{3,7},{... | collective-permute-start | bytes 1572872 | tf_op jit(solution)/shard_map/ppermute | solution.py:641
  298.8 15.2 %attend_back.3 = (bf16[1024,128]{1,0:T(8,128)(2,1)}, bf16[2,1024,128]{2,1,0:T(8,128)(2,1)}, bf16[2,1024,128]{2,1,0:T(8,128)(2,1)}, bf16[2,1024,128]{2,1,0:T(8,128)(2,1)}, bf16[2,1024,128]{2,1,0:T(8,128)(2,1)}) custom-call(s32[23]{0:T(128)} %get-tuple-element.100.info, bf16[1024,256]{1,0:T(8,128)(2,1)} %pad_maximum_fusion.21.q_ref, ...), custom_call_target="tpu_custom_call" | custom-call | flops 1024 | bytes 1024 | tf_op jit(solution)/shard_map/attend_back/pallas_call | solution.py:289
  314.0 15.7 %collective-permute-done.40.refs_3_ = bf16[128,1024]{1,0:T(8,128)(2,1)S(1)} collective-permute-done((bf16[128,1024]{1,0:T(8,128)(2,1)}, bf16[128,1024]{1,0:T(8,128)(2,1)S(1)}, u32[]{:S(2)}, u32[]{:S(2)}) %collective-permute-start.40) | collective-permute-done | bytes 262176 | tf_op jit(solution)/shard_map/ppermute | solution.py:426
  332.1 7.3 %collective-permute-start.47 = (bf16[2,1024,128]{2,1,0:T(8,128)(2,1)}, bf16[2,1024,128]{2,1,0:T(8,128)(2,1)}, u32[]{:S(2)}, u32[]{:S(2)}) collective-permute-start(bf16[2,1024,128]{2,1,0:T(8,128)(2,1)} %get-tuple-element.126.refs_15_), channel_id=1, source_target_pairs={{0,4},{4,8},{8,12},{1,5},{5,9},{9,13},{2,6},{6,10},{10,14},{3,7},{... | collective-permute-start | bytes 1572872 | tf_op jit(solution)/shard_map/ppermute | solution.py:641
  350.1 11.7 %qkv_terms.1 = (bf16[512,768]{1,0:T(8,128)(2,1)}, f32[512,768]{1,0:T(8,128)}) custom-call(s32[2]{0:T(128)} %pad_add_fusion.1.order, bf16[512,1024]{1,0:T(8,128)(2,1)} %pad_maximum_fusion.14.refs_0_, bf16[512,1024]{1,0:T(8,128)(2,1)} %pad_maximum_fusion.15.refs_1_, bf16[512,1024]{1,0:T(8,128)(2,1)} %collective-permute-done.2.refs_2_, ...), custom_call_target="tpu_custom_call" | custom-call | flops 1024 | bytes 1024 | tf_op jit(solution)/shard_map/qkv_terms/pallas_call | solution.py:354
  375.9 3.8 collective-permute-done.49.refs_4_
  379.7 10.8 %collective-permute-done.48.refs_3_ = bf16[544,1024]{1,0:T(8,128)(2,1)} collective-permute-done((bf16[544,1024]{1,0:T(8,128)(2,1)}, bf16[544,1024]{1,0:T(8,128)(2,1)}, u32[]{:S(2)}, u32[]{:S(2)}) %collective-permute-start.48) | collective-permute-done | bytes 1114144 | tf_op jit(solution)/shard_map/ppermute | solution.py:422
  407.2 6.1 %collective-permute-done.53.refs_1_ = bf16[128,1024]{1,0:T(8,128)(2,1)S(1)} collective-permute-done((bf16[128,1024]{1,0:T(8,128)(2,1)S(1)}, bf16[128,1024]{1,0:T(8,128)(2,1)S(1)}, u32[]{:S(2)}, u32[]{:S(2)}) %collective-permute-start.53) | collective-permute-done | bytes 262176 | tf_op jit(solution)/shard_map/ppermute | solution.py:426
  414.0 15.8 %collective-permute-done.55.refs_3_ = bf16[136,1024]{1,0:T(8,128)(2,1)S(1)} collective-permute-done((bf16[136,1024]{1,0:T(8,128)(2,1)S(1)}, bf16[136,1024]{1,0:T(8,128)(2,1)S(1)}, u32[]{:S(2)}, u32[]{:S(2)}) %collective-permute-start.55) | collective-permute-done | bytes 278560 | tf_op jit(solution)/shard_map/ppermute | solution.py:426
  434.7 5.6 %collective-permute-start.61 = (bf16[136,1024]{1,0:T(8,128)(2,1)S(1)}, bf16[136,1024]{1,0:T(8,128)(2,1)S(1)}, u32[]{:S(2)}, u32[]{:S(2)}) collective-permute-start(bf16[136,1024]{1,0:T(8,128)(2,1)S(1)} %add_convert_fusion.5), channel_id=1, source_target_pairs={{0,8},{4,12},{8,0},{12,4},{1,9},{5,13},{9,1},{13,5},{2,10},{6,14},... | collective-permute-start | bytes 835592 | tf_op jit(solution)/shard_map/ppermute | solution.py:426
  446.7 14.3 %collective-permute-done.61 = bf16[136,1024]{1,0:T(8,128)(2,1)S(1)} collective-permute-done((bf16[136,1024]{1,0:T(8,128)(2,1)S(1)}, bf16[136,1024]{1,0:T(8,128)(2,1)S(1)}, u32[]{:S(2)}, u32[]{:S(2)}) %collective-permute-start.61) | collective-permute-done | bytes 278560 | tf_op jit(solution)/shard_map/ppermute | solution.py:426
  466.7 11.1 %collective-permute-done.63 = bf16[512,1024]{1,0:T(8,128)(2,1)} collective-permute-done((bf16[512,1024]{1,0:T(8,128)(2,1)}, bf16[512,1024]{1,0:T(8,128)(2,1)}, u32[]{:S(2)}, u32[]{:S(2)}) %collective-permute-start.63) | collective-permute-done | bytes 1048608 | tf_op jit(solution)/shard_map/ppermute | solution.py:426
  (517 shorter events, 205.2 us)
Async XLA Ops:
  0.6 20.9 %collective-permute-start = (bf16[3,512,256]{2,1,0:T(8,128)(2,1)}, bf16[3,512,256]{2,1,0:T(8,128)(2,1)}, u32[]{:S(2)}, u32[]{:S(2)}) collective-permute-start(bf16[3,512,256]{2,1,0:T(8,128)(2,1)} %param.10), channel_id=1, source_target_pairs={{0,16},{16,0},{1,17},{17,1},{2,18},{18,2},{3,19},{19,3},{4,20},{20... | collective-permute-start | bytes 2359304 | tf_op jit(solution)/shard_map/ppermute | solution.py:403
  6.4 26.0 %collective-permute-start.2 = (bf16[512,1024]{1,0:T(8,128)(2,1)}, bf16[512,1024]{1,0:T(8,128)(2,1)}, u32[]{:S(2)}, u32[]{:S(2)}) collective-permute-start(bf16[512,1024]{1,0:T(8,128)(2,1)} %pad_maximum_fusion.14.refs_0_), channel_id=1, source_target_pairs={{0,4},{4,8},{8,12},{1,5},{5,9},{9,13},{2,6},{6,10},{10,14},{3,7},{... | collective-permute-start | bytes 3145736 | tf_op jit(solution)/shard_map/ppermute | solution.py:500
  11.0 26.5 %collective-permute-start.4 = (bf16[512,1024]{1,0:T(8,128)(2,1)}, bf16[512,1024]{1,0:T(8,128)(2,1)}, u32[]{:S(2)}, u32[]{:S(2)}) collective-permute-start(bf16[512,1024]{1,0:T(8,128)(2,1)} %pad_maximum_fusion.14.refs_0_), channel_id=1, source_target_pairs={{12,8},{8,4},{4,0},{13,9},{9,5},{5,1},{14,10},{10,6},{6,2},{15,11}... | collective-permute-start | bytes 3145736 | tf_op jit(solution)/shard_map/ppermute | solution.py:501
  38.7 38.3 %collective-permute-start.8 = (bf16[512,1024]{1,0:T(8,128)(2,1)}, bf16[512,1024]{1,0:T(8,128)(2,1)}, u32[]{:S(2)}, u32[]{:S(2)}) collective-permute-start(bf16[512,1024]{1,0:T(8,128)(2,1)} %broadcast_add_fusion.1), channel_id=1, source_target_pairs={{0,16},{16,0},{1,17},{17,1},{2,18},{18,2},{3,19},{19,3},{4,20},{20... | collective-permute-start | bytes 3145736 | tf_op jit(solution)/shard_map/ppermute | solution.py:403
  48.1 39.0 %collective-permute-start.9 = (bf16[1024,512]{1,0:T(8,128)(2,1)}, bf16[1024,512]{1,0:T(8,128)(2,1)}, u32[]{:S(2)}, u32[]{:S(2)}) collective-permute-start(bf16[1024,512]{1,0:T(8,128)(2,1)} %broadcast_add_fusion), channel_id=1, source_target_pairs={{0,16},{16,0},{1,17},{17,1},{2,18},{18,2},{3,19},{19,3},{4,20},{20... | collective-permute-start | bytes 3145736 | tf_op jit(solution)/shard_map/ppermute | solution.py:403
  48.6 38.4 %collective-permute-start.3 = (bf16[512,1024]{1,0:T(8,128)(2,1)}, bf16[512,1024]{1,0:T(8,128)(2,1)}, u32[]{:S(2)}, u32[]{:S(2)}) collective-permute-start(bf16[512,1024]{1,0:T(8,128)(2,1)} %collective-permute-done.2.refs_2_), channel_id=1, source_target_pairs={{4,8},{8,12},{5,9},{9,13},{6,10},{10,14},{7,11},{11,15},{20,24},{2... | collective-permute-start | bytes 3145736 | tf_op jit(solution)/shard_map/ppermute | solution.py:503
  50.3 36.8 %collective-permute-start.5 = (bf16[512,1024]{1,0:T(8,128)(2,1)}, bf16[512,1024]{1,0:T(8,128)(2,1)}, u32[]{:S(2)}, u32[]{:S(2)}) collective-permute-start(bf16[512,1024]{1,0:T(8,128)(2,1)} %collective-permute-done.4.refs_4_), channel_id=1, source_target_pairs={{8,4},{4,0},{9,5},{5,1},{10,6},{6,2},{11,7},{7,3},{24,20},{20,16},... | collective-permute-start | bytes 3145736 | tf_op jit(solution)/shard_map/ppermute | solution.py:504
  57.3 29.7 %collective-permute-start.13 = (bf16[256,1024]{1,0:T(8,128)(2,1)S(1)}, bf16[256,1024]{1,0:T(8,128)(2,1)S(1)}, u32[]{:S(2)}, u32[]{:S(2)}) collective-permute-start(bf16[256,1024]{1,0:T(8,128)(2,1)S(1)} %collective-permute-done.11.refs_6_), channel_id=1, source_target_pairs={{0,1},{1,0},{2,3},{3,2},{4,5},{5,4},{6,7},{7,6},{8,9},{9,8},{10,11... | collective-permute-start | bytes 1572872 | tf_op jit(solution)/shard_map/ppermute | solution.py:373
  185.8 25.9 %collective-permute-start.30 = (bf16[1024,512]{1,0:T(8,128)(2,1)S(1)}, bf16[1024,512]{1,0:T(8,128)(2,1)S(1)}, u32[]{:S(2)}, u32[]{:S(2)}) collective-permute-start(bf16[1024,512]{1,0:T(8,128)(2,1)S(1)} %add_convert_fusion), channel_id=1, source_target_pairs={{0,16},{16,0},{1,17},{17,1},{2,18},{18,2},{3,19},{19,3},{4,20},{20... | collective-permute-start | bytes 3145736 | tf_op jit(solution)/shard_map/ppermute | solution.py:422
  220.7 21.8 %collective-permute-start.34 = (bf16[256,1024]{1,0:T(8,128)(2,1)S(1)}, bf16[256,1024]{1,0:T(8,128)(2,1)S(1)}, u32[]{:S(2)}, u32[]{:S(2)}) collective-permute-start(bf16[256,1024]{1,0:T(8,128)(2,1)S(1)} %select_convert_fusion.1), channel_id=1, source_target_pairs={{0,4},{4,0},{8,12},{12,8},{1,5},{5,1},{9,13},{13,9},{2,6},{6,2},{1... | collective-permute-start | bytes 1572872 | tf_op jit(solution)/shard_map/ppermute | solution.py:426
  243.3 27.4 %collective-permute-start.37 = (bf16[528,1024]{1,0:T(8,128)(2,1)}, bf16[528,1024]{1,0:T(8,128)(2,1)S(1)}, u32[]{:S(2)}, u32[]{:S(2)}) collective-permute-start(bf16[528,1024]{1,0:T(8,128)(2,1)} %get-tuple-element.95.refs_15_), channel_id=1, source_target_pairs={{0,2},{1,3},{2,0},{3,1},{4,6},{5,7},{6,4},{7,5},{8,10},{9,11},{10,... | collective-permute-start | bytes 3244040 | tf_op jit(solution)/shard_map/ppermute | solution.py:373
  244.8 25.9 %collective-permute-start.38 = (bf16[528,1024]{1,0:T(8,128)(2,1)}, bf16[528,1024]{1,0:T(8,128)(2,1)S(1)}, u32[]{:S(2)}, u32[]{:S(2)}) collective-permute-start(bf16[528,1024]{1,0:T(8,128)(2,1)} %get-tuple-element.95.refs_15_), channel_id=1, source_target_pairs={{0,1},{1,0},{2,3},{3,2},{4,5},{5,4},{6,7},{7,6},{8,9},{9,8},{10,11... | collective-permute-start | bytes 3244040 | tf_op jit(solution)/shard_map/ppermute | solution.py:373
  244.8 25.9 %collective-permute-start.36 = (bf16[512,1024]{1,0:T(8,128)(2,1)}, bf16[512,1024]{1,0:T(8,128)(2,1)}, u32[]{:S(2)}, u32[]{:S(2)}) collective-permute-start(bf16[512,1024]{1,0:T(8,128)(2,1)} %get-tuple-element.94), channel_id=1, source_target_pairs={{0,16},{16,0},{1,17},{17,1},{2,18},{18,2},{3,19},{19,3},{4,20},{20... | collective-permute-start | bytes 3145736 | tf_op jit(solution)/shard_map/ppermute | solution.py:422
  247.5 20.5 %collective-permute-start.35 = (bf16[128,1024]{1,0:T(8,128)(2,1)S(1)}, bf16[128,1024]{1,0:T(8,128)(2,1)S(1)}, u32[]{:S(2)}, u32[]{:S(2)}) collective-permute-start(bf16[128,1024]{1,0:T(8,128)(2,1)S(1)} %select_convert_fusion.3), channel_id=1, source_target_pairs={{0,8},{4,12},{8,0},{12,4},{1,9},{5,13},{9,1},{13,5},{2,10},{6,14},... | collective-permute-start | bytes 786440 | tf_op jit(solution)/shard_map/ppermute | solution.py:426
  272.0 21.1 %collective-permute-start.39 = (bf16[528,1024]{1,0:T(8,128)(2,1)}, bf16[528,1024]{1,0:T(8,128)(2,1)S(1)}, u32[]{:S(2)}, u32[]{:S(2)}) collective-permute-start(bf16[528,1024]{1,0:T(8,128)(2,1)} %get-tuple-element.99.refs_17_), channel_id=1, source_target_pairs={{0,1},{1,0},{2,3},{3,2},{4,5},{5,4},{6,7},{7,6},{8,9},{9,8},{10,11... | collective-permute-start | bytes 3244040 | tf_op jit(solution)/shard_map/ppermute | solution.py:373
  275.9 38.1 %collective-permute-start.42 = (bf16[2,1024,128]{2,1,0:T(8,128)(2,1)}, bf16[2,1024,128]{2,1,0:T(8,128)(2,1)}, u32[]{:S(2)}, u32[]{:S(2)}) collective-permute-start(bf16[2,1024,128]{2,1,0:T(8,128)(2,1)} %get-tuple-element.106.refs_14_), channel_id=1, source_target_pairs={{0,8},{4,12},{8,0},{12,4},{1,9},{5,13},{9,1},{13,5},{2,10},{6,14},... | collective-permute-start | bytes 1572872 | tf_op jit(solution)/shard_map/ppermute | solution.py:426
  283.5 30.5 %collective-permute-start.43 = (bf16[2,1024,128]{2,1,0:T(8,128)(2,1)}, bf16[2,1024,128]{2,1,0:T(8,128)(2,1)}, u32[]{:S(2)}, u32[]{:S(2)}) collective-permute-start(bf16[2,1024,128]{2,1,0:T(8,128)(2,1)} %get-tuple-element.107.refs_12_), channel_id=1, source_target_pairs={{12,8},{8,4},{4,0},{13,9},{9,5},{5,1},{14,10},{10,6},{6,2},{15,11}... | collective-permute-start | bytes 1572872 | tf_op jit(solution)/shard_map/ppermute | solution.py:640
  284.8 29.2 %collective-permute-start.44 = (bf16[2,1024,128]{2,1,0:T(8,128)(2,1)}, bf16[2,1024,128]{2,1,0:T(8,128)(2,1)}, u32[]{:S(2)}, u32[]{:S(2)}) collective-permute-start(bf16[2,1024,128]{2,1,0:T(8,128)(2,1)} %get-tuple-element.108.refs_13_), channel_id=1, source_target_pairs={{0,4},{4,8},{8,12},{1,5},{5,9},{9,13},{2,6},{6,10},{10,14},{3,7},{... | collective-permute-start | bytes 1572872 | tf_op jit(solution)/shard_map/ppermute | solution.py:641
  294.0 35.7 %collective-permute-start.41 = (bf16[256,1024]{1,0:T(8,128)(2,1)}, bf16[256,1024]{1,0:T(8,128)(2,1)S(1)}, u32[]{:S(2)}, u32[]{:S(2)}) collective-permute-start(bf16[256,1024]{1,0:T(8,128)(2,1)} %get-tuple-element.105), channel_id=1, source_target_pairs={{0,4},{4,0},{8,12},{12,8},{1,5},{5,1},{9,13},{13,9},{2,6},{6,2},{1... | collective-permute-start | bytes 1572872 | tf_op jit(solution)/shard_map/ppermute | solution.py:426
  294.9 34.9 %collective-permute-start.40 = (bf16[128,1024]{1,0:T(8,128)(2,1)}, bf16[128,1024]{1,0:T(8,128)(2,1)S(1)}, u32[]{:S(2)}, u32[]{:S(2)}) collective-permute-start(bf16[128,1024]{1,0:T(8,128)(2,1)} %get-tuple-element.104), channel_id=1, source_target_pairs={{0,8},{4,12},{8,0},{12,4},{1,9},{5,13},{9,1},{13,5},{2,10},{6,14},... | collective-permute-start | bytes 786440 | tf_op jit(solution)/shard_map/ppermute | solution.py:426
  330.7 49.0 %collective-permute-start.45 = (bf16[2,1024,128]{2,1,0:T(8,128)(2,1)}, bf16[2,1024,128]{2,1,0:T(8,128)(2,1)S(1)}, u32[]{:S(2)}, u32[]{:S(2)}) collective-permute-start(bf16[2,1024,128]{2,1,0:T(8,128)(2,1)} %get-tuple-element.124.refs_17_), channel_id=1, source_target_pairs={{0,8},{4,12},{8,0},{12,4},{1,9},{5,13},{9,1},{13,5},{2,10},{6,14},... | collective-permute-start | bytes 1572872 | tf_op jit(solution)/shard_map/ppermute | solution.py:426
  330.7 49.0 %collective-permute-start.46 = (bf16[2,1024,128]{2,1,0:T(8,128)(2,1)}, bf16[2,1024,128]{2,1,0:T(8,128)(2,1)}, u32[]{:S(2)}, u32[]{:S(2)}) collective-permute-start(bf16[2,1024,128]{2,1,0:T(8,128)(2,1)} %get-tuple-element.125.refs_13_), channel_id=1, source_target_pairs={{12,8},{8,4},{4,0},{13,9},{9,5},{5,1},{14,10},{10,6},{6,2},{15,11}... | collective-permute-start | bytes 1572872 | tf_op jit(solution)/shard_map/ppermute | solution.py:640
  332.1 47.6 %collective-permute-start.47 = (bf16[2,1024,128]{2,1,0:T(8,128)(2,1)}, bf16[2,1024,128]{2,1,0:T(8,128)(2,1)}, u32[]{:S(2)}, u32[]{:S(2)}) collective-permute-start(bf16[2,1024,128]{2,1,0:T(8,128)(2,1)} %get-tuple-element.126.refs_15_), channel_id=1, source_target_pairs={{0,4},{4,8},{8,12},{1,5},{5,9},{9,13},{2,6},{6,10},{10,14},{3,7},{... | collective-permute-start | bytes 1572872 | tf_op jit(solution)/shard_map/ppermute | solution.py:641
  364.2 26.3 %collective-permute-start.48 = (bf16[544,1024]{1,0:T(8,128)(2,1)}, bf16[544,1024]{1,0:T(8,128)(2,1)}, u32[]{:S(2)}, u32[]{:S(2)}) collective-permute-start(bf16[544,1024]{1,0:T(8,128)(2,1)} %fusion.7), channel_id=1, source_target_pairs={{0,16},{16,0},{1,17},{17,1},{2,18},{18,2},{3,19},{19,3},{4,20},{20... | collective-permute-start | bytes 3342344 | tf_op jit(solution)/shard_map/ppermute | solution.py:422
  400.5 30.7 %collective-permute-start.52 = (bf16[256,1024]{1,0:T(8,128)(2,1)S(1)}, bf16[256,1024]{1,0:T(8,128)(2,1)S(1)}, u32[]{:S(2)}, u32[]{:S(2)}) collective-permute-start(bf16[256,1024]{1,0:T(8,128)(2,1)S(1)} %fusion.14), channel_id=1, source_target_pairs={{0,2},{1,3},{2,0},{3,1},{4,6},{5,7},{6,4},{7,5},{8,10},{9,11},{10,... | collective-permute-start | bytes 1572872 | tf_op jit(solution)/shard_map/ppermute | solution.py:373
  402.2 27.6 %collective-permute-start.55 = (bf16[136,1024]{1,0:T(8,128)(2,1)S(1)}, bf16[136,1024]{1,0:T(8,128)(2,1)S(1)}, u32[]{:S(2)}, u32[]{:S(2)}) collective-permute-start(bf16[136,1024]{1,0:T(8,128)(2,1)S(1)} %get-tuple-element.167), channel_id=1, source_target_pairs={{0,8},{4,12},{8,0},{12,4},{1,9},{5,13},{9,1},{13,5},{2,10},{6,14},... | collective-permute-start | bytes 835592 | tf_op jit(solution)/shard_map/ppermute | solution.py:426
  403.6 26.9 %collective-permute-start.56 = (bf16[136,1024]{1,0:T(8,128)(2,1)S(1)}, bf16[136,1024]{1,0:T(8,128)(2,1)S(1)}, u32[]{:S(2)}, u32[]{:S(2)}) collective-permute-start(bf16[136,1024]{1,0:T(8,128)(2,1)S(1)} %get-tuple-element.166), channel_id=1, source_target_pairs={{0,12},{4,8},{8,4},{12,0},{1,13},{5,9},{9,5},{13,1},{2,14},{6,10},... | collective-permute-start | bytes 835592 | tf_op jit(solution)/shard_map/ppermute | solution.py:426
  413.3 31.1 %collective-permute-start.50 = (bf16[256,1024]{1,0:T(8,128)(2,1)}, bf16[256,1024]{1,0:T(8,128)(2,1)}, u32[]{:S(2)}, u32[]{:S(2)}) collective-permute-start(bf16[256,1024]{1,0:T(8,128)(2,1)} %get-tuple-element.175), channel_id=1, source_target_pairs={{0,1},{1,0},{2,3},{3,2},{4,5},{5,4},{6,7},{7,6},{8,9},{9,8},{10,11... | collective-permute-start | bytes 1572872 | tf_op jit(solution)/shard_map/ppermute | solution.py:373
  434.7 26.3 %collective-permute-start.61 = (bf16[136,1024]{1,0:T(8,128)(2,1)S(1)}, bf16[136,1024]{1,0:T(8,128)(2,1)S(1)}, u32[]{:S(2)}, u32[]{:S(2)}) collective-permute-start(bf16[136,1024]{1,0:T(8,128)(2,1)S(1)} %add_convert_fusion.5), channel_id=1, source_target_pairs={{0,8},{4,12},{8,0},{12,4},{1,9},{5,13},{9,1},{13,5},{2,10},{6,14},... | collective-permute-start | bytes 835592 | tf_op jit(solution)/shard_map/ppermute | solution.py:426
  440.3 20.7 %collective-permute-start.62 = (bf16[136,1024]{1,0:T(8,128)(2,1)S(1)}, bf16[136,1024]{1,0:T(8,128)(2,1)S(1)}, u32[]{:S(2)}, u32[]{:S(2)}) collective-permute-start(bf16[136,1024]{1,0:T(8,128)(2,1)S(1)} %add_convert_fusion.5), channel_id=1, source_target_pairs={{0,4},{4,0},{8,12},{12,8},{1,5},{5,1},{9,13},{13,9},{2,6},{6,2},{1... | collective-permute-start | bytes 835592 | tf_op jit(solution)/shard_map/ppermute | solution.py:426
  442.4 35.3 %collective-permute-start.63 = (bf16[512,1024]{1,0:T(8,128)(2,1)}, bf16[512,1024]{1,0:T(8,128)(2,1)}, u32[]{:S(2)}, u32[]{:S(2)}) collective-permute-start(bf16[512,1024]{1,0:T(8,128)(2,1)} %pad_maximum_fusion.17), channel_id=1, source_target_pairs={{0,4},{4,0},{8,12},{12,8},{1,5},{5,1},{9,13},{13,9},{2,6},{6,2},{1... | collective-permute-start | bytes 3145736 | tf_op jit(solution)/shard_map/ppermute | solution.py:426
  446.7 36.3 %collective-permute-start.59 = (bf16[256,1024]{1,0:T(8,128)(2,1)S(1)}, bf16[256,1024]{1,0:T(8,128)(2,1)}, u32[]{:S(2)}, u32[]{:S(2)}) collective-permute-start(bf16[256,1024]{1,0:T(8,128)(2,1)S(1)} %fusion.17), channel_id=1, source_target_pairs={{0,1},{1,0},{2,3},{3,2},{4,5},{5,4},{6,7},{7,6},{8,9},{9,8},{10,11... | collective-permute-start | bytes 1572872 | tf_op jit(solution)/shard_map/ppermute | solution.py:373
  (160 other events, 1123.6 us)

commit v4 on v3

--- a/solution.py
+++ b/solution.py
@@ -541,6 +541,7 @@
 
     pieces = jnp.split(context, 4)
     arrived = [pieces[0]] + [tp_swap(pieces[n], order[n]) for n in (1, 2, 3)]
+    arrived = gate(arrived, full_up, full_down)
     resid_rows = quarter_of(tokens, 0).astype(f32)
     for piece, rows in zip(arrived, out_rows):
         resid_rows = resid_rows + nn(piece, rows)
@@ -595,7 +596,7 @@
     resid_grad = norm_back(hidden_grad, gain[0], normed_first, inverse_first)
     attn_own = resid_grad.astype(bf16)
 
-    attn_own, up_send, down_got = gate((attn_own, up_send, down_got))
+    up_send, down_got = gate((up_send, down_got), attn_own)
     up_got = fsdp_swap(up_send)
     down_terms = down_terms + down_got.astype(f32)
     share = up_terms.shape[0]
@@ -618,9 +619,7 @@
     spread = jnp.concatenate(
         [attn_own, result, jnp.pad(vectors, ((0, PAD_ROWS - 4), (0, 0))).astype(bf16)]
     )
-    context_grad, spread, down_got = gate((context_grad, spread, down_got))
-    down_kept, send = ctx_split(down_kept + down_got.astype(f32), 2)
-    down_got = ctx_swap(send, 2)
+    context_grad, spread = gate((context_grad, spread))
     spread_far, spread_near = tp_swap(spread, 2), tp_swap(spread, 1)
 
     sources = own + near + far
@@ -643,10 +642,10 @@
 
     home_1 = home(left_1, right_1, far_1)
     up_kept, up_send = ctx_split(up_terms + up_got.astype(f32), 1)
-    down_total = lax.optimization_barrier((down_kept + down_got.astype(f32)).astype(bf16))
-    info_2, up_send, down_total = gate((info_2, up_send, down_total), spread_both)
+    down_kept, down_send = ctx_split(down_kept + down_got.astype(f32), 2)
+    info_2, up_send, down_send = gate((info_2, up_send, down_send), spread_both)
     up_got = ctx_swap(up_send, 1)
-    down_got = ctx_swap(down_total, 2)
+    down_got = ctx_swap(down_send, 2)
 
     dq_2, own_2, left_2, right_2, far_2 = attend_back(
         info_2, queries, context_grad, context, log_totals, sources, sources_at, 7, 1, part
@@ -663,13 +662,15 @@
         )
     )
     home_2 = home(left_2, right_2, far_2)
+    down_total = lax.optimization_barrier((down_kept + down_got.astype(f32)).astype(bf16))
     up_kept, send = ctx_split(up_kept + up_got.astype(f32), 2)
-    up_got = ctx_swap(send, 2)
-
-    held = (spread, spread_near, spread_far, spread_both)
-    result_parts = [x[quarter : 2 * quarter] for x in held]
-    attn_all = jnp.concatenate([held[n][:quarter] for n in order])
-    vectors = sum(x[2 * quarter :].astype(f32) for x in held)
+    ffn_got = ctx_swap(jnp.concatenate([down_total, send]), 2)
+
+    def spread_sums(held):
+        return (
+            jnp.concatenate([held[n][:quarter] for n in order]),
+            sum(x[2 * quarter :].astype(f32) for x in held),
+        )
 
     def rest_of(qkv_terms, start, size):
         right = lax.dynamic_slice_in_dim(attn_all, start, size, axis=1)
@@ -687,6 +688,11 @@
         picks = jnp.stack([1 - mine, mine]).astype(jnp.int32)
         half = depth // 2
         qkv_send, qkv_terms = qkv_terms_of(rows, (dq_1, dq_2), pairs, picks, bf16)
+        spread, spread_near, spread_far, spread_both = gate(
+            (spread, spread_near, spread_far, spread_both), qkv_send
+        )
+        held = (spread, spread_near, spread_far, spread_both)
+        attn_all, vectors = spread_sums(held)
         rest_got = fsdp_swap(rest_of(qkv_send, (1 - mine) * half, half))
         rest = rest_of(qkv_terms, mine * half, half)
     else:
@@ -694,6 +700,8 @@
         qkv_terms = lax.psum_scatter(
             jnp.concatenate(halves), "fsdp", scatter_dimension=0, tiled=True
         )
+        held = (spread, spread_near, spread_far, spread_both)
+        attn_all, vectors = spread_sums(held)
         out_terms = lax.psum_scatter(
             jnp.concatenate([tn(context, attn_all), vectors]), "fsdp",
             scatter_dimension=1, tiled=True,
@@ -705,6 +713,7 @@
         extra = jnp.pad(extra, ((0, PAD_ROWS), (0, rest.shape[1] - extra.shape[1])))
         rest = jnp.concatenate([rest, extra])
         rest_got = jnp.zeros(rest.shape, bf16)
+    result_parts = [x[quarter : 2 * quarter] for x in held]
     query_grad = jnp.concatenate([dq_1, dq_2], axis=1)
 
     def owned(own_kv, arrivals):
@@ -717,7 +726,8 @@
     input_terms = (
         nt(query_grad, w_q) + nt(total_1[0], w_k[:, :part]) + nt(total_1[1], w_v[:, :part])
     )
-    *home_2, rest_got, up_got = gate((*home_2, rest_got, up_got), input_terms)
+    *home_2, rest_got, ffn_got = gate((*home_2, rest_got, ffn_got), input_terms)
+    down_got, up_got = jnp.split(ffn_got, 2)
     total_2 = owned(own_2, home_2)
     terms = input_terms + nt(total_2[0], w_k[:, part:]) + nt(total_2[1], w_v[:, part:])
     q0, q2, q1, q3 = jnp.split(terms, 4)

time: 491 us -> 480 us (0.978)
  waiting for transfers between devices: 173 us -> 128 us
  Pallas kernels: 64.9 us -> 92.5 us
  starting transfers between devices: 92.4 us -> 79.6 us
  local copies, waits for them, and re-layouts: 34.4 us -> 42.7 us
  other arithmetic: 62.3 us -> 68.5 us
    pallas_call x2, Pallas kernels: 30.4 us -> 46.7 us  [attend_back(): pl.pallas_call(functools.partial(attend_back_kernel, heads, keys // BLK,...]
    ppermute x3, waiting for transfers between devices: 18.5 us -> 2.49 us  [fsdp_swap(): return lax.ppermute(x, 'fsdp', [(0, 1), (1, 0)])]
    ppermute x15 -> x14, waiting for transfers between devices: 76.9 us -> 62.8 us  [ctx_swap(): return lax.ppermute(x, 'ctx', [(i, i ^ bit) for i in range(4)])]
    ppermute x5, waiting for transfers between devices: 19.8 us -> 6.62 us  [fsdp_whole(): other = lax.ppermute(shard, 'fsdp', [(0, 1), (1, 0)])]
    ppermute x15 -> x14, starting transfers between devices: 39.3 us -> 27.7 us  [ctx_swap(): return lax.ppermute(x, 'ctx', [(i, i ^ bit) for i in range(4)])]
    pallas_call x2, Pallas kernels: 22.7 us -> 34 us  [attend(): pl.pallas_call(functools.partial(attend_kernel, heads, keys // BLK, kfirs...]
    unnamed x258 -> x272, local copies, waits for them, and re-layouts: 18.2 us -> 24.3 us
  transfers between devices with their start and end apart: 64 -> 63, of which waited for: 26 -> 22; matrix products, arithmetic and copies ran while one was open for 24% -> 26% of each run, Pallas kernels for 12% -> 18%
where the time goes in v4:
time: 480 us; the launch traced here: 474 us
  waiting for transfers between devices  128 us (27%)
  Pallas kernels  92.5 us (19%)
  starting transfers between devices  79.6 us (17%)
  other arithmetic  68.5 us (14%)
  matrix products  59.3 us (12%)
  local copies, waits for them, and re-layouts  42.7 us (9%)
    ppermute x14, waiting for transfers between devices, ctx_swap(): return lax.ppermute(x, 'ctx', [(i, i ^ bit) for i in range(4)])  62.8 us
    dot_general x39, matrix products, contract(): lax.dot_general(left, right, (((left_dim,), (right_dim,)), ((), ())), pre...  59.3 us
    ppermute x33, waiting for transfers between devices, tp_swap(): return lax.ppermute(x, 'tp', [(i, i ^ bit) for i in range(4)])  49.2 us
    pallas_call x2, Pallas kernels, attend_back(): pl.pallas_call(functools.partial(attend_back_kernel, heads, keys // BLK,...  46.7 us
    pallas_call x2, Pallas kernels, attend(): pl.pallas_call(functools.partial(attend_kernel, heads, keys // BLK, kfirs...  34 us
    ppermute x14, starting transfers between devices, ctx_swap(): return lax.ppermute(x, 'ctx', [(i, i ^ bit) for i in range(4)])  27.7 us
    unnamed x272, local copies, waits for them, and re-layouts  24.3 us
    ppermute x33, starting transfers between devices, tp_swap(): return lax.ppermute(x, 'tp', [(i, i ^ bit) for i in range(4)])  17.7 us
  transfers between devices with their start and end apart: 63, of which 22 were waited for; matrix products, arithmetic and copies ran while one was open for 26% of the time, Pallas kernels for 18%

profile of v4, /device:TPU:0, one launch (start us, length us, event | category | flops | bytes accessed | tf_op | source)
XLA Modules:
  0.0 474.1 jit_solution(17113315283325596253)
XLA Ops:
  0.6 3.0 collective-permute-start
  8.0 4.5 collective-permute-start.2
  14.8 6.6 %collective-permute-done = bf16[3,512,256]{2,1,0:T(8,128)(2,1)S(1)} collective-permute-done((bf16[3,512,256]{2,1,0:T(8,128)(2,1)}, bf16[3,512,256]{2,1,0:T(8,128)(2,1)S(1)}, u32[]{:S(2)}, u32[]{:S(2)}) %collective-permute-start) | collective-permute-done | bytes 786464 | tf_op jit(solution)/shard_map/ppermute | solution.py:403
  29.4 4.5 collective-permute-done.2.refs_2_
  41.4 7.4 %collective-permute-done.11.refs_6_ = bf16[256,1024]{1,0:T(8,128)(2,1)S(1)} collective-permute-done((bf16[256,1024]{1,0:T(8,128)(2,1)S(1)}, bf16[256,1024]{1,0:T(8,128)(2,1)S(1)}, u32[]{:S(2)}, u32[]{:S(2)}) %collective-permute-start.11) | collective-permute-done | bytes 524320 | tf_op jit(solution)/shard_map/ppermute | solution.py:373
  61.9 27.8 %attend_near.1 = (f32[4,1024]{1,0:T(4,128)}, f32[4,1024]{1,0:T(4,128)}, f32[256,1024]{1,0:T(8,128)}) custom-call(s32[23]{0:T(128)} %pad_add_fusion.info.refs_0_, bf16[1024,256]{1,0:T(8,128)(2,1)} %pad_maximum_fusion.21.q_ref, bf16[512,768]{1,0:T(8,128)(2,1)} %copy-done.16, bf16[512,768]{1,0:T(8,128)(2,1)} %copy-done.17, ...), custom_call_target="tpu_custom_call" | custom-call | flops 1024 | bytes 1024 | tf_op jit(solution)/shard_map/attend_near/pallas_call | solution.py:185
  94.1 3.5 broadcast_select_fusion.1
  100.7 6.3 %attend_far.1 = (bf16[1024,256]{1,0:T(8,128)(2,1)}, f32[4,1024]{1,0:T(4,128)}) custom-call(s32[23]{0:T(128)} %pad_add_fusion.info.refs_0_, bf16[1024,256]{1,0:T(8,128)(2,1)} %pad_maximum_fusion.21.q_ref, bf16[512,512]{1,0:T(8,128)(2,1)} %convolution_convert_fusion.3.refs_0_.refs_6_, bf16[512,512]{1,0:T(8,128)(2,1)} %convolution_convert_fusion.2.refs_1_.refs_7_, ...), custom_call_target="tpu_custom_call" | custom-call | flops 1024 | bytes 1024 | tf_op jit(solution)/shard_map/attend_far/pallas_call | solution.py:185
  110.9 4.0 pad_maximum_fusion
  130.1 7.2 %collective-permute-done.18.refs_0_ = bf16[256,1024]{1,0:T(8,128)(2,1)} collective-permute-done((bf16[256,1024]{1,0:T(8,128)(2,1)S(1)}, bf16[256,1024]{1,0:T(8,128)(2,1)}, u32[]{:S(2)}, u32[]{:S(2)}) %collective-permute-start.18) | collective-permute-done | bytes 524320 | tf_op jit(solution)/shard_map/ppermute | solution.py:373
  139.5 4.3 multiply_convert_fusion.2
  148.9 12.4 %collective-permute-done.23 = bf16[256,1024]{1,0:T(8,128)(2,1)S(1)} collective-permute-done((bf16[256,1024]{1,0:T(8,128)(2,1)S(1)}, bf16[256,1024]{1,0:T(8,128)(2,1)S(1)}, u32[]{:S(2)}, u32[]{:S(2)}) %collective-permute-start.23) | collective-permute-done | bytes 524320 | tf_op jit(solution)/shard_map/ppermute | solution.py:373
  170.2 8.2 %collective-permute-done.24.refs_0_ = bf16[256,1024]{1,0:T(8,128)(2,1)} collective-permute-done((bf16[256,1024]{1,0:T(8,128)(2,1)S(1)}, bf16[256,1024]{1,0:T(8,128)(2,1)}, u32[]{:S(2)}, u32[]{:S(2)}) %collective-permute-start.24) | collective-permute-done | bytes 524320 | tf_op jit(solution)/shard_map/ppermute | solution.py:373
  198.8 9.0 %collective-permute-done.29 = bf16[256,1024]{1,0:T(8,128)(2,1)S(1)} collective-permute-done((bf16[256,1024]{1,0:T(8,128)(2,1)S(1)}, bf16[256,1024]{1,0:T(8,128)(2,1)S(1)}, u32[]{:S(2)}, u32[]{:S(2)}) %collective-permute-start.29) | collective-permute-done | bytes 524320 | tf_op jit(solution)/shard_map/ppermute | solution.py:373
  222.8 3.1 convert_add_fusion.1
  227.1 8.9 %collective-permute-start.34 = (bf16[256,1024]{1,0:T(8,128)(2,1)}, bf16[256,1024]{1,0:T(8,128)(2,1)}, u32[]{:S(2)}, u32[]{:S(2)}) collective-permute-start(bf16[256,1024]{1,0:T(8,128)(2,1)} %select_convert_fusion.1), channel_id=1, source_target_pairs={{0,4},{4,0},{8,12},{12,8},{1,5},{5,1},{9,13},{13,9},{2,6},{6,2},{1... | collective-permute-start | bytes 1572872 | tf_op jit(solution)/shard_map/ppermute | solution.py:426
  240.1 23.4 %attend_back.2 = (bf16[1024,128]{1,0:T(8,128)(2,1)}, bf16[2,1024,128]{2,1,0:T(8,128)(2,1)}, bf16[2,1024,128]{2,1,0:T(8,128)(2,1)}, bf16[2,1024,128]{2,1,0:T(8,128)(2,1)}, bf16[2,1024,128]{2,1,0:T(8,128)(2,1)}) custom-call(s32[23]{0:T(128)} %pad_add_fusion.info.refs_0_, bf16[1024,256]{1,0:T(8,128)(2,1)} %pad_maximum_fusion.21.q_ref, ...), custom_call_target="tpu_custom_call" | custom-call | flops 1024 | bytes 1024 | tf_op jit(solution)/shard_map/attend_back/pallas_call | solution.py:289
  266.8 5.4 %collective-permute-start.43 = (bf16[2,1024,128]{2,1,0:T(8,128)(2,1)}, bf16[2,1024,128]{2,1,0:T(8,128)(2,1)}, u32[]{:S(2)}, u32[]{:S(2)}) collective-permute-start(bf16[2,1024,128]{2,1,0:T(8,128)(2,1)} %get-tuple-element.116.refs_13_), channel_id=1, source_target_pairs={{0,4},{4,8},{8,12},{1,5},{5,9},{9,13},{2,6},{6,10},{10,14},{3,7},{... | collective-permute-start | bytes 1572872 | tf_op jit(solution)/shard_map/ppermute | solution.py:640
  284.8 23.3 %attend_back.3 = (bf16[1024,128]{1,0:T(8,128)(2,1)}, bf16[2,1024,128]{2,1,0:T(8,128)(2,1)}, bf16[2,1024,128]{2,1,0:T(8,128)(2,1)}, bf16[2,1024,128]{2,1,0:T(8,128)(2,1)}, bf16[2,1024,128]{2,1,0:T(8,128)(2,1)}) custom-call(s32[23]{0:T(128)} %get-tuple-element.108.info, bf16[1024,256]{1,0:T(8,128)(2,1)} %pad_maximum_fusion.21.q_ref, ...), custom_call_target="tpu_custom_call" | custom-call | flops 1024 | bytes 1024 | tf_op jit(solution)/shard_map/attend_back/pallas_call | solution.py:289
  308.1 6.4 %collective-permute-done.39.refs_3_ = bf16[128,1024]{1,0:T(8,128)(2,1)S(1)} collective-permute-done((bf16[128,1024]{1,0:T(8,128)(2,1)}, bf16[128,1024]{1,0:T(8,128)(2,1)S(1)}, u32[]{:S(2)}, u32[]{:S(2)}) %collective-permute-start.39) | collective-permute-done | bytes 262176 | tf_op jit(solution)/shard_map/ppermute | solution.py:426
  316.6 5.6 %collective-permute-start.46 = (bf16[2,1024,128]{2,1,0:T(8,128)(2,1)}, bf16[2,1024,128]{2,1,0:T(8,128)(2,1)}, u32[]{:S(2)}, u32[]{:S(2)}) collective-permute-start(bf16[2,1024,128]{2,1,0:T(8,128)(2,1)} %get-tuple-element.132.refs_15_), channel_id=1, source_target_pairs={{0,4},{4,8},{8,12},{1,5},{5,9},{9,13},{2,6},{6,10},{10,14},{3,7},{... | collective-permute-start | bytes 1572872 | tf_op jit(solution)/shard_map/ppermute | solution.py:640
  322.2 11.8 %qkv_terms.1 = (bf16[512,768]{1,0:T(8,128)(2,1)}, f32[512,768]{1,0:T(8,128)}) custom-call(s32[2]{0:T(128)} %pad_add_fusion.1.order, bf16[512,1024]{1,0:T(8,128)(2,1)} %pad_maximum_fusion.14.refs_0_, bf16[512,1024]{1,0:T(8,128)(2,1)} %pad_maximum_fusion.15.refs_1_, bf16[512,1024]{1,0:T(8,128)(2,1)} %collective-permute-done.2.refs_2_, ...), custom_call_target="tpu_custom_call" | custom-call | flops 1024 | bytes 1024 | tf_op jit(solution)/shard_map/qkv_terms/pallas_call | solution.py:354
  347.7 4.1 collective-permute-start.47
  365.1 3.8 add_add_fusion.1.refs_5_
  368.9 10.3 %collective-permute-done.48.refs_4_ = bf16[256,1024]{1,0:T(8,128)(2,1)S(1)} collective-permute-done((bf16[256,1024]{1,0:T(8,128)(2,1)}, bf16[256,1024]{1,0:T(8,128)(2,1)S(1)}, u32[]{:S(2)}, u32[]{:S(2)}) %collective-permute-start.48) | collective-permute-done | bytes 524320 | tf_op jit(solution)/shard_map/ppermute | solution.py:426
  396.7 4.1 collective-permute-done.52.refs_1_
  400.8 4.9 %collective-permute-done.53.refs_2_ = bf16[136,1024]{1,0:T(8,128)(2,1)S(1)} collective-permute-done((bf16[136,1024]{1,0:T(8,128)(2,1)S(1)}, bf16[136,1024]{1,0:T(8,128)(2,1)S(1)}, u32[]{:S(2)}, u32[]{:S(2)}) %collective-permute-start.53) | collective-permute-done | bytes 278560 | tf_op jit(solution)/shard_map/ppermute | solution.py:426
  405.7 11.4 %collective-permute-done.54.refs_3_ = bf16[136,1024]{1,0:T(8,128)(2,1)S(1)} collective-permute-done((bf16[136,1024]{1,0:T(8,128)(2,1)S(1)}, bf16[136,1024]{1,0:T(8,128)(2,1)S(1)}, u32[]{:S(2)}, u32[]{:S(2)}) %collective-permute-start.54) | collective-permute-done | bytes 278560 | tf_op jit(solution)/shard_map/ppermute | solution.py:426
  420.8 3.7 collective-permute-start.59
  424.5 3.6 collective-permute-start.60
  434.4 14.8 %collective-permute-done.60 = bf16[136,1024]{1,0:T(8,128)(2,1)S(1)} collective-permute-done((bf16[136,1024]{1,0:T(8,128)(2,1)S(1)}, bf16[136,1024]{1,0:T(8,128)(2,1)S(1)}, u32[]{:S(2)}, u32[]{:S(2)}) %collective-permute-start.60) | collective-permute-done | bytes 278560 | tf_op jit(solution)/shard_map/ppermute | solution.py:426
  454.8 10.9 %collective-permute-done.62 = bf16[512,1024]{1,0:T(8,128)(2,1)} collective-permute-done((bf16[512,1024]{1,0:T(8,128)(2,1)}, bf16[512,1024]{1,0:T(8,128)(2,1)}, u32[]{:S(2)}, u32[]{:S(2)}) %collective-permute-start.62) | collective-permute-done | bytes 1048608 | tf_op jit(solution)/shard_map/ppermute | solution.py:426
  (534 shorter events, 202.8 us)
Async XLA Ops:
  0.6 20.8 %collective-permute-start = (bf16[3,512,256]{2,1,0:T(8,128)(2,1)}, bf16[3,512,256]{2,1,0:T(8,128)(2,1)S(1)}, u32[]{:S(2)}, u32[]{:S(2)}) collective-permute-start(bf16[3,512,256]{2,1,0:T(8,128)(2,1)} %param.10), channel_id=1, source_target_pairs={{0,16},{16,0},{1,17},{17,1},{2,18},{18,2},{3,19},{19,3},{4,20},{20... | collective-permute-start | bytes 2359304 | tf_op jit(solution)/shard_map/ppermute | solution.py:403
  8.0 25.9 %collective-permute-start.2 = (bf16[512,1024]{1,0:T(8,128)(2,1)}, bf16[512,1024]{1,0:T(8,128)(2,1)}, u32[]{:S(2)}, u32[]{:S(2)}) collective-permute-start(bf16[512,1024]{1,0:T(8,128)(2,1)} %pad_maximum_fusion.14.refs_0_), channel_id=1, source_target_pairs={{0,4},{4,8},{8,12},{1,5},{5,9},{9,13},{2,6},{6,10},{10,14},{3,7},{... | collective-permute-start | bytes 3145736 | tf_op jit(solution)/shard_map/ppermute | solution.py:500
  12.5 26.5 %collective-permute-start.4 = (bf16[512,1024]{1,0:T(8,128)(2,1)}, bf16[512,1024]{1,0:T(8,128)(2,1)}, u32[]{:S(2)}, u32[]{:S(2)}) collective-permute-start(bf16[512,1024]{1,0:T(8,128)(2,1)} %pad_maximum_fusion.14.refs_0_), channel_id=1, source_target_pairs={{12,8},{8,4},{4,0},{13,9},{9,5},{5,1},{14,10},{10,6},{6,2},{15,11}... | collective-permute-start | bytes 3145736 | tf_op jit(solution)/shard_map/ppermute | solution.py:501
  40.9 48.8 %collective-permute-start.8 = (bf16[512,1024]{1,0:T(8,128)(2,1)}, bf16[512,1024]{1,0:T(8,128)(2,1)}, u32[]{:S(2)}, u32[]{:S(2)}) collective-permute-start(bf16[512,1024]{1,0:T(8,128)(2,1)} %broadcast_add_fusion.1), channel_id=1, source_target_pairs={{0,16},{16,0},{1,17},{17,1},{2,18},{18,2},{3,19},{19,3},{4,20},{20... | collective-permute-start | bytes 3145736 | tf_op jit(solution)/shard_map/ppermute | solution.py:403
  48.8 40.9 %collective-permute-start.9 = (bf16[1024,512]{1,0:T(8,128)(2,1)}, bf16[1024,512]{1,0:T(8,128)(2,1)}, u32[]{:S(2)}, u32[]{:S(2)}) collective-permute-start(bf16[1024,512]{1,0:T(8,128)(2,1)} %broadcast_add_fusion), channel_id=1, source_target_pairs={{0,16},{16,0},{1,17},{17,1},{2,18},{18,2},{3,19},{19,3},{4,20},{20... | collective-permute-start | bytes 3145736 | tf_op jit(solution)/shard_map/ppermute | solution.py:403
  50.3 39.4 %collective-permute-start.3 = (bf16[512,1024]{1,0:T(8,128)(2,1)}, bf16[512,1024]{1,0:T(8,128)(2,1)}, u32[]{:S(2)}, u32[]{:S(2)}) collective-permute-start(bf16[512,1024]{1,0:T(8,128)(2,1)} %collective-permute-done.2.refs_2_), channel_id=1, source_target_pairs={{4,8},{8,12},{5,9},{9,13},{6,10},{10,14},{7,11},{11,15},{20,24},{2... | collective-permute-start | bytes 3145736 | tf_op jit(solution)/shard_map/ppermute | solution.py:503
  52.0 37.8 %collective-permute-start.5 = (bf16[512,1024]{1,0:T(8,128)(2,1)}, bf16[512,1024]{1,0:T(8,128)(2,1)}, u32[]{:S(2)}, u32[]{:S(2)}) collective-permute-start(bf16[512,1024]{1,0:T(8,128)(2,1)} %collective-permute-done.4.refs_4_), channel_id=1, source_target_pairs={{8,4},{4,0},{9,5},{5,1},{10,6},{6,2},{11,7},{7,3},{24,20},{20,16},... | collective-permute-start | bytes 3145736 | tf_op jit(solution)/shard_map/ppermute | solution.py:504
  58.7 31.0 %collective-permute-start.13 = (bf16[256,1024]{1,0:T(8,128)(2,1)S(1)}, bf16[256,1024]{1,0:T(8,128)(2,1)S(1)}, u32[]{:S(2)}, u32[]{:S(2)}) collective-permute-start(bf16[256,1024]{1,0:T(8,128)(2,1)S(1)} %collective-permute-done.11.refs_6_), channel_id=1, source_target_pairs={{0,1},{1,0},{2,3},{3,2},{4,5},{5,4},{6,7},{7,6},{8,9},{9,8},{10,11... | collective-permute-start | bytes 1572872 | tf_op jit(solution)/shard_map/ppermute | solution.py:373
  192.0 25.7 %collective-permute-start.33 = (bf16[1024,512]{1,0:T(8,128)(2,1)S(1)}, bf16[1024,512]{1,0:T(8,128)(2,1)}, u32[]{:S(2)}, u32[]{:S(2)}) collective-permute-start(bf16[1024,512]{1,0:T(8,128)(2,1)S(1)} %add_convert_fusion), channel_id=1, source_target_pairs={{0,16},{16,0},{1,17},{17,1},{2,18},{18,2},{3,19},{19,3},{4,20},{20... | collective-permute-start | bytes 3145736 | tf_op jit(solution)/shard_map/ppermute | solution.py:422
  217.7 45.8 %collective-permute-start.35 = (bf16[512,1024]{1,0:T(8,128)(2,1)}, bf16[512,1024]{1,0:T(8,128)(2,1)S(1)}, u32[]{:S(2)}, u32[]{:S(2)}) collective-permute-start(bf16[512,1024]{1,0:T(8,128)(2,1)} %get-tuple-element.102), channel_id=1, source_target_pairs={{0,16},{16,0},{1,17},{17,1},{2,18},{18,2},{3,19},{19,3},{4,20},{20... | collective-permute-start | bytes 3145736 | tf_op jit(solution)/shard_map/ppermute | solution.py:422
  221.3 42.3 %collective-permute-start.36 = (bf16[528,1024]{1,0:T(8,128)(2,1)}, bf16[528,1024]{1,0:T(8,128)(2,1)S(1)}, u32[]{:S(2)}, u32[]{:S(2)}) collective-permute-start(bf16[528,1024]{1,0:T(8,128)(2,1)} %get-tuple-element.103.refs_15_), channel_id=1, source_target_pairs={{0,2},{1,3},{2,0},{3,1},{4,6},{5,7},{6,4},{7,5},{8,10},{9,11},{10,... | collective-permute-start | bytes 3244040 | tf_op jit(solution)/shard_map/ppermute | solution.py:373
  222.8 40.8 %collective-permute-start.37 = (bf16[528,1024]{1,0:T(8,128)(2,1)}, bf16[528,1024]{1,0:T(8,128)(2,1)S(1)}, u32[]{:S(2)}, u32[]{:S(2)}) collective-permute-start(bf16[528,1024]{1,0:T(8,128)(2,1)} %get-tuple-element.103.refs_15_), channel_id=1, source_target_pairs={{0,1},{1,0},{2,3},{3,2},{4,5},{5,4},{6,7},{7,6},{8,9},{9,8},{10,11... | collective-permute-start | bytes 3244040 | tf_op jit(solution)/shard_map/ppermute | solution.py:373
  227.1 36.5 %collective-permute-start.34 = (bf16[256,1024]{1,0:T(8,128)(2,1)}, bf16[256,1024]{1,0:T(8,128)(2,1)}, u32[]{:S(2)}, u32[]{:S(2)}) collective-permute-start(bf16[256,1024]{1,0:T(8,128)(2,1)} %select_convert_fusion.1), channel_id=1, source_target_pairs={{0,4},{4,0},{8,12},{12,8},{1,5},{5,1},{9,13},{13,9},{2,6},{6,2},{1... | collective-permute-start | bytes 1572872 | tf_op jit(solution)/shard_map/ppermute | solution.py:426
  265.5 42.6 %collective-permute-start.41 = (bf16[2,1024,128]{2,1,0:T(8,128)(2,1)}, bf16[2,1024,128]{2,1,0:T(8,128)(2,1)}, u32[]{:S(2)}, u32[]{:S(2)}) collective-permute-start(bf16[2,1024,128]{2,1,0:T(8,128)(2,1)} %get-tuple-element.114.refs_14_), channel_id=1, source_target_pairs={{0,8},{4,12},{8,0},{12,4},{1,9},{5,13},{9,1},{13,5},{2,10},{6,14},... | collective-permute-start | bytes 1572872 | tf_op jit(solution)/shard_map/ppermute | solution.py:426
  265.5 42.6 %collective-permute-start.42 = (bf16[2,1024,128]{2,1,0:T(8,128)(2,1)}, bf16[2,1024,128]{2,1,0:T(8,128)(2,1)}, u32[]{:S(2)}, u32[]{:S(2)}) collective-permute-start(bf16[2,1024,128]{2,1,0:T(8,128)(2,1)} %get-tuple-element.115.refs_12_), channel_id=1, source_target_pairs={{12,8},{8,4},{4,0},{13,9},{9,5},{5,1},{14,10},{10,6},{6,2},{15,11}... | collective-permute-start | bytes 1572872 | tf_op jit(solution)/shard_map/ppermute | solution.py:639
  266.8 41.3 %collective-permute-start.43 = (bf16[2,1024,128]{2,1,0:T(8,128)(2,1)}, bf16[2,1024,128]{2,1,0:T(8,128)(2,1)}, u32[]{:S(2)}, u32[]{:S(2)}) collective-permute-start(bf16[2,1024,128]{2,1,0:T(8,128)(2,1)} %get-tuple-element.116.refs_13_), channel_id=1, source_target_pairs={{0,4},{4,8},{8,12},{1,5},{5,9},{9,13},{2,6},{6,10},{10,14},{3,7},{... | collective-permute-start | bytes 1572872 | tf_op jit(solution)/shard_map/ppermute | solution.py:640
  279.1 35.4 %collective-permute-start.40 = (bf16[256,1024]{1,0:T(8,128)(2,1)}, bf16[256,1024]{1,0:T(8,128)(2,1)S(1)}, u32[]{:S(2)}, u32[]{:S(2)}) collective-permute-start(bf16[256,1024]{1,0:T(8,128)(2,1)} %get-tuple-element.113), channel_id=1, source_target_pairs={{0,4},{4,0},{8,12},{12,8},{1,5},{5,1},{9,13},{13,9},{2,6},{6,2},{1... | collective-permute-start | bytes 1572872 | tf_op jit(solution)/shard_map/ppermute | solution.py:426
  280.0 34.4 %collective-permute-start.39 = (bf16[128,1024]{1,0:T(8,128)(2,1)}, bf16[128,1024]{1,0:T(8,128)(2,1)S(1)}, u32[]{:S(2)}, u32[]{:S(2)}) collective-permute-start(bf16[128,1024]{1,0:T(8,128)(2,1)} %get-tuple-element.112), channel_id=1, source_target_pairs={{0,8},{4,12},{8,0},{12,4},{1,9},{5,13},{9,1},{13,5},{2,10},{6,14},... | collective-permute-start | bytes 786440 | tf_op jit(solution)/shard_map/ppermute | solution.py:426
  315.3 53.6 %collective-permute-start.44 = (bf16[2,1024,128]{2,1,0:T(8,128)(2,1)}, bf16[2,1024,128]{2,1,0:T(8,128)(2,1)}, u32[]{:S(2)}, u32[]{:S(2)}) collective-permute-start(bf16[2,1024,128]{2,1,0:T(8,128)(2,1)} %get-tuple-element.134.refs_17_), channel_id=1, source_target_pairs={{0,8},{4,12},{8,0},{12,4},{1,9},{5,13},{9,1},{13,5},{2,10},{6,14},... | collective-permute-start | bytes 1572872 | tf_op jit(solution)/shard_map/ppermute | solution.py:426
  315.3 53.6 %collective-permute-start.45 = (bf16[2,1024,128]{2,1,0:T(8,128)(2,1)}, bf16[2,1024,128]{2,1,0:T(8,128)(2,1)}, u32[]{:S(2)}, u32[]{:S(2)}) collective-permute-start(bf16[2,1024,128]{2,1,0:T(8,128)(2,1)} %get-tuple-element.130.refs_13_), channel_id=1, source_target_pairs={{12,8},{8,4},{4,0},{13,9},{9,5},{5,1},{14,10},{10,6},{6,2},{15,11}... | collective-permute-start | bytes 1572872 | tf_op jit(solution)/shard_map/ppermute | solution.py:639
  316.6 52.3 %collective-permute-start.46 = (bf16[2,1024,128]{2,1,0:T(8,128)(2,1)}, bf16[2,1024,128]{2,1,0:T(8,128)(2,1)}, u32[]{:S(2)}, u32[]{:S(2)}) collective-permute-start(bf16[2,1024,128]{2,1,0:T(8,128)(2,1)} %get-tuple-element.132.refs_15_), channel_id=1, source_target_pairs={{0,4},{4,8},{8,12},{1,5},{5,9},{9,13},{2,6},{6,10},{10,14},{3,7},{... | collective-permute-start | bytes 1572872 | tf_op jit(solution)/shard_map/ppermute | solution.py:640
  347.7 31.4 %collective-permute-start.47 = (bf16[544,1024]{1,0:T(8,128)(2,1)}, bf16[544,1024]{1,0:T(8,128)(2,1)}, u32[]{:S(2)}, u32[]{:S(2)}) collective-permute-start(bf16[544,1024]{1,0:T(8,128)(2,1)} %fusion.7), channel_id=1, source_target_pairs={{0,16},{16,0},{1,17},{17,1},{2,18},{18,2},{3,19},{19,3},{4,20},{20... | collective-permute-start | bytes 3342344 | tf_op jit(solution)/shard_map/ppermute | solution.py:422
  354.4 24.8 %collective-permute-start.48 = (bf16[256,1024]{1,0:T(8,128)(2,1)}, bf16[256,1024]{1,0:T(8,128)(2,1)S(1)}, u32[]{:S(2)}, u32[]{:S(2)}) collective-permute-start(bf16[256,1024]{1,0:T(8,128)(2,1)} %pad_maximum_fusion.24), channel_id=1, source_target_pairs={{0,8},{4,12},{8,0},{12,4},{1,9},{5,13},{9,1},{13,5},{2,10},{6,14},... | collective-permute-start | bytes 1572872 | tf_op jit(solution)/shard_map/ppermute | solution.py:426
  389.9 28.6 %collective-permute-start.51 = (bf16[256,1024]{1,0:T(8,128)(2,1)S(1)}, bf16[256,1024]{1,0:T(8,128)(2,1)S(1)}, u32[]{:S(2)}, u32[]{:S(2)}) collective-permute-start(bf16[256,1024]{1,0:T(8,128)(2,1)S(1)} %fusion.14), channel_id=1, source_target_pairs={{0,2},{1,3},{2,0},{3,1},{4,6},{5,7},{6,4},{7,5},{8,10},{9,11},{10,... | collective-permute-start | bytes 1572872 | tf_op jit(solution)/shard_map/ppermute | solution.py:373
  391.2 25.9 %collective-permute-start.54 = (bf16[136,1024]{1,0:T(8,128)(2,1)S(1)}, bf16[136,1024]{1,0:T(8,128)(2,1)S(1)}, u32[]{:S(2)}, u32[]{:S(2)}) collective-permute-start(bf16[136,1024]{1,0:T(8,128)(2,1)S(1)} %get-tuple-element.179), channel_id=1, source_target_pairs={{0,8},{4,12},{8,0},{12,4},{1,9},{5,13},{9,1},{13,5},{2,10},{6,14},... | collective-permute-start | bytes 835592 | tf_op jit(solution)/shard_map/ppermute | solution.py:426
  392.8 24.4 %collective-permute-start.55 = (bf16[136,1024]{1,0:T(8,128)(2,1)S(1)}, bf16[136,1024]{1,0:T(8,128)(2,1)S(1)}, u32[]{:S(2)}, u32[]{:S(2)}) collective-permute-start(bf16[136,1024]{1,0:T(8,128)(2,1)S(1)} %get-tuple-element.178), channel_id=1, source_target_pairs={{0,12},{4,8},{8,4},{12,0},{1,13},{5,9},{9,5},{13,1},{2,14},{6,10},... | collective-permute-start | bytes 835592 | tf_op jit(solution)/shard_map/ppermute | solution.py:426
  400.8 31.3 %collective-permute-start.49 = (bf16[256,1024]{1,0:T(8,128)(2,1)}, bf16[256,1024]{1,0:T(8,128)(2,1)}, u32[]{:S(2)}, u32[]{:S(2)}) collective-permute-start(bf16[256,1024]{1,0:T(8,128)(2,1)} %get-tuple-element.187), channel_id=1, source_target_pairs={{0,1},{1,0},{2,3},{3,2},{4,5},{5,4},{6,7},{7,6},{8,9},{9,8},{10,11... | collective-permute-start | bytes 1572872 | tf_op jit(solution)/shard_map/ppermute | solution.py:373
  424.5 24.7 %collective-permute-start.60 = (bf16[136,1024]{1,0:T(8,128)(2,1)S(1)}, bf16[136,1024]{1,0:T(8,128)(2,1)S(1)}, u32[]{:S(2)}, u32[]{:S(2)}) collective-permute-start(bf16[136,1024]{1,0:T(8,128)(2,1)S(1)} %add_convert_fusion.5), channel_id=1, source_target_pairs={{0,8},{4,12},{8,0},{12,4},{1,9},{5,13},{9,1},{13,5},{2,10},{6,14},... | collective-permute-start | bytes 835592 | tf_op jit(solution)/shard_map/ppermute | solution.py:426
  428.0 21.1 %collective-permute-start.61 = (bf16[136,1024]{1,0:T(8,128)(2,1)S(1)}, bf16[136,1024]{1,0:T(8,128)(2,1)S(1)}, u32[]{:S(2)}, u32[]{:S(2)}) collective-permute-start(bf16[136,1024]{1,0:T(8,128)(2,1)S(1)} %add_convert_fusion.5), channel_id=1, source_target_pairs={{0,4},{4,0},{8,12},{12,8},{1,5},{5,1},{9,13},{13,9},{2,6},{6,2},{1... | collective-permute-start | bytes 835592 | tf_op jit(solution)/shard_map/ppermute | solution.py:426
  430.4 35.4 %collective-permute-start.62 = (bf16[512,1024]{1,0:T(8,128)(2,1)}, bf16[512,1024]{1,0:T(8,128)(2,1)}, u32[]{:S(2)}, u32[]{:S(2)}) collective-permute-start(bf16[512,1024]{1,0:T(8,128)(2,1)} %pad_maximum_fusion.17), channel_id=1, source_target_pairs={{0,4},{4,0},{8,12},{12,8},{1,5},{5,1},{9,13},{13,9},{2,6},{6,2},{1... | collective-permute-start | bytes 3145736 | tf_op jit(solution)/shard_map/ppermute | solution.py:426
  433.8 21.0 %collective-permute-start.56 = (bf16[256,1024]{1,0:T(8,128)(2,1)S(1)}, bf16[256,1024]{1,0:T(8,128)(2,1)}, u32[]{:S(2)}, u32[]{:S(2)}) collective-permute-start(bf16[256,1024]{1,0:T(8,128)(2,1)S(1)} %fusion.17), channel_id=1, source_target_pairs={{0,2},{1,3},{2,0},{3,1},{4,6},{5,7},{6,4},{7,5},{8,10},{9,11},{10,... | collective-permute-start | bytes 1572872 | tf_op jit(solution)/shard_map/ppermute | solution.py:373
  434.4 36.6 %collective-permute-start.58 = (bf16[256,1024]{1,0:T(8,128)(2,1)S(1)}, bf16[256,1024]{1,0:T(8,128)(2,1)}, u32[]{:S(2)}, u32[]{:S(2)}) collective-permute-start(bf16[256,1024]{1,0:T(8,128)(2,1)S(1)} %fusion.17), channel_id=1, source_target_pairs={{0,1},{1,0},{2,3},{3,2},{4,5},{5,4},{6,7},{7,6},{8,9},{9,8},{10,11... | collective-permute-start | bytes 1572872 | tf_op jit(solution)/shard_map/ppermute | solution.py:373
  (167 other events, 1199.7 us)

commit v5 on v4

--- a/solution.py
+++ b/solution.py
@@ -541,7 +541,6 @@
 
     pieces = jnp.split(context, 4)
     arrived = [pieces[0]] + [tp_swap(pieces[n], order[n]) for n in (1, 2, 3)]
-    arrived = gate(arrived, full_up, full_down)
     resid_rows = quarter_of(tokens, 0).astype(f32)
     for piece, rows in zip(arrived, out_rows):
         resid_rows = resid_rows + nn(piece, rows)

time: 480 us -> 472 us (0.983)
  Pallas kernels: 92.5 us -> 68.1 us
  waiting for transfers between devices: 128 us -> 151 us
  starting transfers between devices: 79.6 us -> 89.7 us
  local copies, waits for them, and re-layouts: 42.7 us -> 36.9 us
    pallas_call x2, Pallas kernels: 46.7 us -> 32.3 us  [attend_back(): pl.pallas_call(functools.partial(attend_back_kernel, heads, keys // BLK,...]
    ppermute x5, waiting for transfers between devices: 6.62 us -> 20 us  [fsdp_whole(): other = lax.ppermute(shard, 'fsdp', [(0, 1), (1, 0)])]
    ppermute x14, starting transfers between devices: 27.7 us -> 38.8 us  [ctx_swap(): return lax.ppermute(x, 'ctx', [(i, i ^ bit) for i in range(4)])]
    pallas_call x2, Pallas kernels: 34 us -> 24.1 us  [attend(): pl.pallas_call(functools.partial(attend_kernel, heads, keys // BLK, kfirs...]
    ppermute x14, waiting for transfers between devices: 62.8 us -> 70.9 us  [ctx_swap(): return lax.ppermute(x, 'ctx', [(i, i ^ bit) for i in range(4)])]
    unnamed x272 -> x260, local copies, waits for them, and re-layouts: 24.3 us -> 19.3 us
  transfers between devices with their start and end apart: 63 -> 63, of which waited for: 22 -> 24; matrix products, arithmetic and copies ran while one was open for 26% -> 26% of each run, Pallas kernels for 18% -> 13%
where the time goes in v5:
time: 472 us; the launch traced here: 470 us
  waiting for transfers between devices  151 us (32%)
  starting transfers between devices  89.7 us (19%)
  Pallas kernels  68.1 us (14%)
  other arithmetic  64.5 us (14%)
  matrix products  56.9 us (12%)
  local copies, waits for them, and re-layouts  36.9 us (8%)
    ppermute x14, waiting for transfers between devices, ctx_swap(): return lax.ppermute(x, 'ctx', [(i, i ^ bit) for i in range(4)])  70.9 us
    dot_general x39, matrix products, contract(): lax.dot_general(left, right, (((left_dim,), (right_dim,)), ((), ())), pre...  56.9 us
    ppermute x33, waiting for transfers between devices, tp_swap(): return lax.ppermute(x, 'tp', [(i, i ^ bit) for i in range(4)])  51.6 us
    ppermute x14, starting transfers between devices, ctx_swap(): return lax.ppermute(x, 'ctx', [(i, i ^ bit) for i in range(4)])  38.8 us
    pallas_call x2, Pallas kernels, attend_back(): pl.pallas_call(functools.partial(attend_back_kernel, heads, keys // BLK,...  32.3 us
    pallas_call x2, Pallas kernels, attend(): pl.pallas_call(functools.partial(attend_kernel, heads, keys // BLK, kfirs...  24.1 us
    ppermute x5, waiting for transfers between devices, fsdp_whole(): other = lax.ppermute(shard, 'fsdp', [(0, 1), (1, 0)])  20 us
    unnamed x260, local copies, waits for them, and re-layouts  19.3 us
  transfers between devices with their start and end apart: 63, of which 24 were waited for; matrix products, arithmetic and copies ran while one was open for 26% of the time, Pallas kernels for 13%

profile of v5, /device:TPU:0, one launch (start us, length us, event | category | flops | bytes accessed | tf_op | source)
XLA Modules:
  0.0 470.3 jit_solution(5191467534447511594)
XLA Ops:
  6.4 4.6 collective-permute-start.2
  13.4 8.1 %collective-permute-done = bf16[3,512,256]{2,1,0:T(8,128)(2,1)} collective-permute-done((bf16[3,512,256]{2,1,0:T(8,128)(2,1)}, bf16[3,512,256]{2,1,0:T(8,128)(2,1)}, u32[]{:S(2)}, u32[]{:S(2)}) %collective-permute-start) | collective-permute-done | bytes 786464 | tf_op jit(solution)/shard_map/ppermute | solution.py:403
  27.7 4.8 %collective-permute-done.2.refs_2_ = bf16[512,1024]{1,0:T(8,128)(2,1)} collective-permute-done((bf16[512,1024]{1,0:T(8,128)(2,1)}, bf16[512,1024]{1,0:T(8,128)(2,1)}, u32[]{:S(2)}, u32[]{:S(2)}) %collective-permute-start.2) | collective-permute-done | bytes 1048608 | tf_op jit(solution)/shard_map/ppermute | solution.py:500
  41.2 6.9 %collective-permute-done.11.refs_6_ = bf16[256,1024]{1,0:T(8,128)(2,1)S(1)} collective-permute-done((bf16[256,1024]{1,0:T(8,128)(2,1)S(1)}, bf16[256,1024]{1,0:T(8,128)(2,1)S(1)}, u32[]{:S(2)}, u32[]{:S(2)}) %collective-permute-start.11) | collective-permute-done | bytes 524320 | tf_op jit(solution)/shard_map/ppermute | solution.py:373
  60.4 17.8 %attend_near.1 = (f32[4,1024]{1,0:T(4,128)}, f32[4,1024]{1,0:T(4,128)}, f32[256,1024]{1,0:T(8,128)}) custom-call(s32[23]{0:T(128)} %pad_add_fusion.info.refs_0_, bf16[1024,256]{1,0:T(8,128)(2,1)} %pad_maximum_fusion.21.q_ref, bf16[512,768]{1,0:T(8,128)(2,1)} %copy-done.17, bf16[512,768]{1,0:T(8,128)(2,1)} %copy-done.16, ...), custom_call_target="tpu_custom_call" | custom-call | flops 1024 | bytes 1024 | tf_op jit(solution)/shard_map/attend_near/pallas_call | solution.py:185
  78.2 8.8 %collective-permute-done.9.refs_4_ = bf16[1024,512]{1,0:T(8,128)(2,1)} collective-permute-done((bf16[1024,512]{1,0:T(8,128)(2,1)}, bf16[1024,512]{1,0:T(8,128)(2,1)}, u32[]{:S(2)}, u32[]{:S(2)}) %collective-permute-start.9) | collective-permute-done | bytes 1048608 | tf_op jit(solution)/shard_map/ppermute | solution.py:403
  90.1 3.1 collective-permute-done.1
  96.3 6.3 %attend_far.1 = (bf16[1024,256]{1,0:T(8,128)(2,1)}, f32[4,1024]{1,0:T(4,128)}) custom-call(s32[23]{0:T(128)} %pad_add_fusion.info.refs_0_, bf16[1024,256]{1,0:T(8,128)(2,1)} %pad_maximum_fusion.21.q_ref, bf16[512,512]{1,0:T(8,128)(2,1)} %convolution_convert_fusion.3.refs_0_.refs_6_, bf16[512,512]{1,0:T(8,128)(2,1)} %convolution_convert_fusion.2.refs_1_.refs_7_, ...), custom_call_target="tpu_custom_call" | custom-call | flops 1024 | bytes 1024 | tf_op jit(solution)/shard_map/attend_far/pallas_call | solution.py:185
  106.0 4.1 collective-permute-done.15
  124.0 7.3 %collective-permute-done.18.refs_0_ = bf16[256,1024]{1,0:T(8,128)(2,1)S(1)} collective-permute-done((bf16[256,1024]{1,0:T(8,128)(2,1)S(1)}, bf16[256,1024]{1,0:T(8,128)(2,1)S(1)}, u32[]{:S(2)}, u32[]{:S(2)}) %collective-permute-start.18) | collective-permute-done | bytes 524320 | tf_op jit(solution)/shard_map/ppermute | solution.py:373
  142.1 12.4 %collective-permute-done.23 = bf16[256,1024]{1,0:T(8,128)(2,1)S(1)} collective-permute-done((bf16[256,1024]{1,0:T(8,128)(2,1)S(1)}, bf16[256,1024]{1,0:T(8,128)(2,1)S(1)}, u32[]{:S(2)}, u32[]{:S(2)}) %collective-permute-start.23) | collective-permute-done | bytes 524320 | tf_op jit(solution)/shard_map/ppermute | solution.py:373
  163.4 8.2 %collective-permute-done.24.refs_0_ = bf16[256,1024]{1,0:T(8,128)(2,1)} collective-permute-done((bf16[256,1024]{1,0:T(8,128)(2,1)S(1)}, bf16[256,1024]{1,0:T(8,128)(2,1)}, u32[]{:S(2)}, u32[]{:S(2)}) %collective-permute-start.24) | collective-permute-done | bytes 524320 | tf_op jit(solution)/shard_map/ppermute | solution.py:373
  185.2 3.3 collective-permute-start.33
  194.5 9.0 %collective-permute-done.29 = bf16[256,1024]{1,0:T(8,128)(2,1)S(1)} collective-permute-done((bf16[256,1024]{1,0:T(8,128)(2,1)S(1)}, bf16[256,1024]{1,0:T(8,128)(2,1)S(1)}, u32[]{:S(2)}, u32[]{:S(2)}) %collective-permute-start.29) | collective-permute-done | bytes 524320 | tf_op jit(solution)/shard_map/ppermute | solution.py:373
  217.9 3.1 convert_add_fusion.1
  222.1 9.6 %collective-permute-start.34 = (bf16[256,1024]{1,0:T(8,128)(2,1)}, bf16[256,1024]{1,0:T(8,128)(2,1)}, u32[]{:S(2)}, u32[]{:S(2)}) collective-permute-start(bf16[256,1024]{1,0:T(8,128)(2,1)} %select_convert_fusion.1), channel_id=1, source_target_pairs={{0,4},{4,0},{8,12},{12,8},{1,5},{5,1},{9,13},{13,9},{2,6},{6,2},{1... | collective-permute-start | bytes 1572872 | tf_op jit(solution)/shard_map/ppermute | solution.py:426
  235.9 16.1 %attend_back.2 = (bf16[1024,128]{1,0:T(8,128)(2,1)}, bf16[2,1024,128]{2,1,0:T(8,128)(2,1)}, bf16[2,1024,128]{2,1,0:T(8,128)(2,1)}, bf16[2,1024,128]{2,1,0:T(8,128)(2,1)}, bf16[2,1024,128]{2,1,0:T(8,128)(2,1)}) custom-call(s32[23]{0:T(128)} %pad_add_fusion.info.refs_0_, bf16[1024,256]{1,0:T(8,128)(2,1)} %pad_maximum_fusion.21.q_ref, ...), custom_call_target="tpu_custom_call" | custom-call | flops 1024 | bytes 1024 | tf_op jit(solution)/shard_map/attend_back/pallas_call | solution.py:289
  254.0 12.5 %collective-permute-start.41 = (bf16[2,1024,128]{2,1,0:T(8,128)(2,1)}, bf16[2,1024,128]{2,1,0:T(8,128)(2,1)}, u32[]{:S(2)}, u32[]{:S(2)}) collective-permute-start(bf16[2,1024,128]{2,1,0:T(8,128)(2,1)} %get-tuple-element.106.refs_14_), channel_id=1, source_target_pairs={{0,8},{4,12},{8,0},{12,4},{1,9},{5,13},{9,1},{13,5},{2,10},{6,14},... | collective-permute-start | bytes 1572872 | tf_op jit(solution)/shard_map/ppermute | solution.py:426
  267.8 5.5 %collective-permute-start.43 = (bf16[2,1024,128]{2,1,0:T(8,128)(2,1)}, bf16[2,1024,128]{2,1,0:T(8,128)(2,1)}, u32[]{:S(2)}, u32[]{:S(2)}) collective-permute-start(bf16[2,1024,128]{2,1,0:T(8,128)(2,1)} %get-tuple-element.108.refs_13_), channel_id=1, source_target_pairs={{0,4},{4,8},{8,12},{1,5},{5,9},{9,13},{2,6},{6,10},{10,14},{3,7},{... | collective-permute-start | bytes 1572872 | tf_op jit(solution)/shard_map/ppermute | solution.py:639
  283.1 16.1 %attend_back.3 = (bf16[1024,128]{1,0:T(8,128)(2,1)}, bf16[2,1024,128]{2,1,0:T(8,128)(2,1)}, bf16[2,1024,128]{2,1,0:T(8,128)(2,1)}, bf16[2,1024,128]{2,1,0:T(8,128)(2,1)}, bf16[2,1024,128]{2,1,0:T(8,128)(2,1)}) custom-call(s32[23]{0:T(128)} %get-tuple-element.100.info, bf16[1024,256]{1,0:T(8,128)(2,1)} %pad_maximum_fusion.21.q_ref, ...), custom_call_target="tpu_custom_call" | custom-call | flops 1024 | bytes 1024 | tf_op jit(solution)/shard_map/attend_back/pallas_call | solution.py:289
  299.3 13.2 %collective-permute-done.39.refs_3_ = bf16[128,1024]{1,0:T(8,128)(2,1)S(1)} collective-permute-done((bf16[128,1024]{1,0:T(8,128)(2,1)}, bf16[128,1024]{1,0:T(8,128)(2,1)S(1)}, u32[]{:S(2)}, u32[]{:S(2)}) %collective-permute-start.39) | collective-permute-done | bytes 262176 | tf_op jit(solution)/shard_map/ppermute | solution.py:426
  314.7 5.4 %collective-permute-start.46 = (bf16[2,1024,128]{2,1,0:T(8,128)(2,1)}, bf16[2,1024,128]{2,1,0:T(8,128)(2,1)}, u32[]{:S(2)}, u32[]{:S(2)}) collective-permute-start(bf16[2,1024,128]{2,1,0:T(8,128)(2,1)} %get-tuple-element.124.refs_15_), channel_id=1, source_target_pairs={{0,4},{4,8},{8,12},{1,5},{5,9},{9,13},{2,6},{6,10},{10,14},{3,7},{... | collective-permute-start | bytes 1572872 | tf_op jit(solution)/shard_map/ppermute | solution.py:639
  320.0 11.7 %qkv_terms.1 = (bf16[512,768]{1,0:T(8,128)(2,1)}, f32[512,768]{1,0:T(8,128)}) custom-call(s32[2]{0:T(128)} %pad_add_fusion.1.order, bf16[512,1024]{1,0:T(8,128)(2,1)} %pad_maximum_fusion.14.refs_0_, bf16[512,1024]{1,0:T(8,128)(2,1)} %pad_maximum_fusion.15.refs_1_, bf16[512,1024]{1,0:T(8,128)(2,1)} %collective-permute-done.2.refs_2_, ...), custom_call_target="tpu_custom_call" | custom-call | flops 1024 | bytes 1024 | tf_op jit(solution)/shard_map/qkv_terms/pallas_call | solution.py:354
  360.7 3.8 add_add_fusion.1.refs_5_
  364.5 10.1 %collective-permute-done.48.refs_4_ = bf16[256,1024]{1,0:T(8,128)(2,1)S(1)} collective-permute-done((bf16[256,1024]{1,0:T(8,128)(2,1)}, bf16[256,1024]{1,0:T(8,128)(2,1)S(1)}, u32[]{:S(2)}, u32[]{:S(2)}) %collective-permute-start.48) | collective-permute-done | bytes 524320 | tf_op jit(solution)/shard_map/ppermute | solution.py:426
  391.7 4.6 collective-permute-done.52.refs_1_
  396.3 3.7 collective-permute-done.53.refs_2_
  400.0 13.3 %collective-permute-done.54.refs_3_ = bf16[136,1024]{1,0:T(8,128)(2,1)S(1)} collective-permute-done((bf16[136,1024]{1,0:T(8,128)(2,1)S(1)}, bf16[136,1024]{1,0:T(8,128)(2,1)S(1)}, u32[]{:S(2)}, u32[]{:S(2)}) %collective-permute-start.54) | collective-permute-done | bytes 278560 | tf_op jit(solution)/shard_map/ppermute | solution.py:426
  417.0 3.2 collective-permute-start.59
  420.2 4.1 collective-permute-start.60
  430.3 15.0 %collective-permute-done.60 = bf16[136,1024]{1,0:T(8,128)(2,1)S(1)} collective-permute-done((bf16[136,1024]{1,0:T(8,128)(2,1)S(1)}, bf16[136,1024]{1,0:T(8,128)(2,1)S(1)}, u32[]{:S(2)}, u32[]{:S(2)}) %collective-permute-start.60) | collective-permute-done | bytes 278560 | tf_op jit(solution)/shard_map/ppermute | solution.py:426
  451.1 10.9 %collective-permute-done.62 = bf16[512,1024]{1,0:T(8,128)(2,1)} collective-permute-done((bf16[512,1024]{1,0:T(8,128)(2,1)}, bf16[512,1024]{1,0:T(8,128)(2,1)}, u32[]{:S(2)}, u32[]{:S(2)}) %collective-permute-start.62) | collective-permute-done | bytes 1048608 | tf_op jit(solution)/shard_map/ppermute | solution.py:426
  (519 shorter events, 200.3 us)
Async XLA Ops:
  6.4 26.0 %collective-permute-start.2 = (bf16[512,1024]{1,0:T(8,128)(2,1)}, bf16[512,1024]{1,0:T(8,128)(2,1)}, u32[]{:S(2)}, u32[]{:S(2)}) collective-permute-start(bf16[512,1024]{1,0:T(8,128)(2,1)} %pad_maximum_fusion.14.refs_0_), channel_id=1, source_target_pairs={{0,4},{4,8},{8,12},{1,5},{5,9},{9,13},{2,6},{6,10},{10,14},{3,7},{... | collective-permute-start | bytes 3145736 | tf_op jit(solution)/shard_map/ppermute | solution.py:500
  11.0 26.5 %collective-permute-start.4 = (bf16[512,1024]{1,0:T(8,128)(2,1)}, bf16[512,1024]{1,0:T(8,128)(2,1)}, u32[]{:S(2)}, u32[]{:S(2)}) collective-permute-start(bf16[512,1024]{1,0:T(8,128)(2,1)} %pad_maximum_fusion.14.refs_0_), channel_id=1, source_target_pairs={{12,8},{8,4},{4,0},{13,9},{9,5},{5,1},{14,10},{10,6},{6,2},{15,11}... | collective-permute-start | bytes 3145736 | tf_op jit(solution)/shard_map/ppermute | solution.py:501
  38.7 39.6 %collective-permute-start.8 = (bf16[512,1024]{1,0:T(8,128)(2,1)}, bf16[512,1024]{1,0:T(8,128)(2,1)}, u32[]{:S(2)}, u32[]{:S(2)}) collective-permute-start(bf16[512,1024]{1,0:T(8,128)(2,1)} %broadcast_add_fusion.1), channel_id=1, source_target_pairs={{0,16},{16,0},{1,17},{17,1},{2,18},{18,2},{3,19},{19,3},{4,20},{20... | collective-permute-start | bytes 3145736 | tf_op jit(solution)/shard_map/ppermute | solution.py:403
  48.1 39.0 %collective-permute-start.9 = (bf16[1024,512]{1,0:T(8,128)(2,1)}, bf16[1024,512]{1,0:T(8,128)(2,1)}, u32[]{:S(2)}, u32[]{:S(2)}) collective-permute-start(bf16[1024,512]{1,0:T(8,128)(2,1)} %broadcast_add_fusion), channel_id=1, source_target_pairs={{0,16},{16,0},{1,17},{17,1},{2,18},{18,2},{3,19},{19,3},{4,20},{20... | collective-permute-start | bytes 3145736 | tf_op jit(solution)/shard_map/ppermute | solution.py:403
  48.6 38.4 %collective-permute-start.3 = (bf16[512,1024]{1,0:T(8,128)(2,1)}, bf16[512,1024]{1,0:T(8,128)(2,1)}, u32[]{:S(2)}, u32[]{:S(2)}) collective-permute-start(bf16[512,1024]{1,0:T(8,128)(2,1)} %collective-permute-done.2.refs_2_), channel_id=1, source_target_pairs={{4,8},{8,12},{5,9},{9,13},{6,10},{10,14},{7,11},{11,15},{20,24},{2... | collective-permute-start | bytes 3145736 | tf_op jit(solution)/shard_map/ppermute | solution.py:503
  50.3 36.8 %collective-permute-start.5 = (bf16[512,1024]{1,0:T(8,128)(2,1)}, bf16[512,1024]{1,0:T(8,128)(2,1)}, u32[]{:S(2)}, u32[]{:S(2)}) collective-permute-start(bf16[512,1024]{1,0:T(8,128)(2,1)} %collective-permute-done.4.refs_4_), channel_id=1, source_target_pairs={{8,4},{4,0},{9,5},{5,1},{10,6},{6,2},{11,7},{7,3},{24,20},{20,16},... | collective-permute-start | bytes 3145736 | tf_op jit(solution)/shard_map/ppermute | solution.py:504
  57.3 29.8 %collective-permute-start.13 = (bf16[256,1024]{1,0:T(8,128)(2,1)S(1)}, bf16[256,1024]{1,0:T(8,128)(2,1)S(1)}, u32[]{:S(2)}, u32[]{:S(2)}) collective-permute-start(bf16[256,1024]{1,0:T(8,128)(2,1)S(1)} %collective-permute-done.11.refs_6_), channel_id=1, source_target_pairs={{0,1},{1,0},{2,3},{3,2},{4,5},{5,4},{6,7},{7,6},{8,9},{9,8},{10,11... | collective-permute-start | bytes 1572872 | tf_op jit(solution)/shard_map/ppermute | solution.py:373
  185.2 27.2 %collective-permute-start.33 = (bf16[1024,512]{1,0:T(8,128)(2,1)S(1)}, bf16[1024,512]{1,0:T(8,128)(2,1)}, u32[]{:S(2)}, u32[]{:S(2)}) collective-permute-start(bf16[1024,512]{1,0:T(8,128)(2,1)S(1)} %add_convert_fusion), channel_id=1, source_target_pairs={{0,16},{16,0},{1,17},{17,1},{2,18},{18,2},{3,19},{19,3},{4,20},{20... | collective-permute-start | bytes 3145736 | tf_op jit(solution)/shard_map/ppermute | solution.py:422
  212.4 39.6 %collective-permute-start.35 = (bf16[512,1024]{1,0:T(8,128)(2,1)}, bf16[512,1024]{1,0:T(8,128)(2,1)S(1)}, u32[]{:S(2)}, u32[]{:S(2)}) collective-permute-start(bf16[512,1024]{1,0:T(8,128)(2,1)} %get-tuple-element.94), channel_id=1, source_target_pairs={{0,16},{16,0},{1,17},{17,1},{2,18},{18,2},{3,19},{19,3},{4,20},{20... | collective-permute-start | bytes 3145736 | tf_op jit(solution)/shard_map/ppermute | solution.py:422
  216.8 35.3 %collective-permute-start.36 = (bf16[528,1024]{1,0:T(8,128)(2,1)}, bf16[528,1024]{1,0:T(8,128)(2,1)S(1)}, u32[]{:S(2)}, u32[]{:S(2)}) collective-permute-start(bf16[528,1024]{1,0:T(8,128)(2,1)} %get-tuple-element.95.refs_15_), channel_id=1, source_target_pairs={{0,2},{1,3},{2,0},{3,1},{4,6},{5,7},{6,4},{7,5},{8,10},{9,11},{10,... | collective-permute-start | bytes 3244040 | tf_op jit(solution)/shard_map/ppermute | solution.py:373
  217.9 34.2 %collective-permute-start.37 = (bf16[528,1024]{1,0:T(8,128)(2,1)}, bf16[528,1024]{1,0:T(8,128)(2,1)S(1)}, u32[]{:S(2)}, u32[]{:S(2)}) collective-permute-start(bf16[528,1024]{1,0:T(8,128)(2,1)} %get-tuple-element.95.refs_15_), channel_id=1, source_target_pairs={{0,1},{1,0},{2,3},{3,2},{4,5},{5,4},{6,7},{7,6},{8,9},{9,8},{10,11... | collective-permute-start | bytes 3244040 | tf_op jit(solution)/shard_map/ppermute | solution.py:373
  222.1 29.9 %collective-permute-start.34 = (bf16[256,1024]{1,0:T(8,128)(2,1)}, bf16[256,1024]{1,0:T(8,128)(2,1)}, u32[]{:S(2)}, u32[]{:S(2)}) collective-permute-start(bf16[256,1024]{1,0:T(8,128)(2,1)} %select_convert_fusion.1), channel_id=1, source_target_pairs={{0,4},{4,0},{8,12},{12,8},{1,5},{5,1},{9,13},{13,9},{2,6},{6,2},{1... | collective-permute-start | bytes 1572872 | tf_op jit(solution)/shard_map/ppermute | solution.py:426
  253.7 25.5 %collective-permute-start.38 = (bf16[528,1024]{1,0:T(8,128)(2,1)}, bf16[528,1024]{1,0:T(8,128)(2,1)S(1)}, u32[]{:S(2)}, u32[]{:S(2)}) collective-permute-start(bf16[528,1024]{1,0:T(8,128)(2,1)} %get-tuple-element.99.refs_17_), channel_id=1, source_target_pairs={{0,1},{1,0},{2,3},{3,2},{4,5},{5,4},{6,7},{7,6},{8,9},{9,8},{10,11... | collective-permute-start | bytes 3244040 | tf_op jit(solution)/shard_map/ppermute | solution.py:373
  254.0 45.3 %collective-permute-start.41 = (bf16[2,1024,128]{2,1,0:T(8,128)(2,1)}, bf16[2,1024,128]{2,1,0:T(8,128)(2,1)}, u32[]{:S(2)}, u32[]{:S(2)}) collective-permute-start(bf16[2,1024,128]{2,1,0:T(8,128)(2,1)} %get-tuple-element.106.refs_14_), channel_id=1, source_target_pairs={{0,8},{4,12},{8,0},{12,4},{1,9},{5,13},{9,1},{13,5},{2,10},{6,14},... | collective-permute-start | bytes 1572872 | tf_op jit(solution)/shard_map/ppermute | solution.py:426
  266.5 32.8 %collective-permute-start.42 = (bf16[2,1024,128]{2,1,0:T(8,128)(2,1)}, bf16[2,1024,128]{2,1,0:T(8,128)(2,1)}, u32[]{:S(2)}, u32[]{:S(2)}) collective-permute-start(bf16[2,1024,128]{2,1,0:T(8,128)(2,1)} %get-tuple-element.107.refs_12_), channel_id=1, source_target_pairs={{12,8},{8,4},{4,0},{13,9},{9,5},{5,1},{14,10},{10,6},{6,2},{15,11}... | collective-permute-start | bytes 1572872 | tf_op jit(solution)/shard_map/ppermute | solution.py:638
  267.8 31.5 %collective-permute-start.43 = (bf16[2,1024,128]{2,1,0:T(8,128)(2,1)}, bf16[2,1024,128]{2,1,0:T(8,128)(2,1)}, u32[]{:S(2)}, u32[]{:S(2)}) collective-permute-start(bf16[2,1024,128]{2,1,0:T(8,128)(2,1)} %get-tuple-element.108.refs_13_), channel_id=1, source_target_pairs={{0,4},{4,8},{8,12},{1,5},{5,9},{9,13},{2,6},{6,10},{10,14},{3,7},{... | collective-permute-start | bytes 1572872 | tf_op jit(solution)/shard_map/ppermute | solution.py:639
  280.2 32.3 %collective-permute-start.40 = (bf16[256,1024]{1,0:T(8,128)(2,1)}, bf16[256,1024]{1,0:T(8,128)(2,1)S(1)}, u32[]{:S(2)}, u32[]{:S(2)}) collective-permute-start(bf16[256,1024]{1,0:T(8,128)(2,1)} %get-tuple-element.105), channel_id=1, source_target_pairs={{0,4},{4,0},{8,12},{12,8},{1,5},{5,1},{9,13},{13,9},{2,6},{6,2},{1... | collective-permute-start | bytes 1572872 | tf_op jit(solution)/shard_map/ppermute | solution.py:426
  280.2 32.3 %collective-permute-start.39 = (bf16[128,1024]{1,0:T(8,128)(2,1)}, bf16[128,1024]{1,0:T(8,128)(2,1)S(1)}, u32[]{:S(2)}, u32[]{:S(2)}) collective-permute-start(bf16[128,1024]{1,0:T(8,128)(2,1)} %get-tuple-element.104), channel_id=1, source_target_pairs={{0,8},{4,12},{8,0},{12,4},{1,9},{5,13},{9,1},{13,5},{2,10},{6,14},... | collective-permute-start | bytes 786440 | tf_op jit(solution)/shard_map/ppermute | solution.py:426
  313.4 51.1 %collective-permute-start.44 = (bf16[2,1024,128]{2,1,0:T(8,128)(2,1)}, bf16[2,1024,128]{2,1,0:T(8,128)(2,1)}, u32[]{:S(2)}, u32[]{:S(2)}) collective-permute-start(bf16[2,1024,128]{2,1,0:T(8,128)(2,1)} %get-tuple-element.126.refs_17_), channel_id=1, source_target_pairs={{0,8},{4,12},{8,0},{12,4},{1,9},{5,13},{9,1},{13,5},{2,10},{6,14},... | collective-permute-start | bytes 1572872 | tf_op jit(solution)/shard_map/ppermute | solution.py:426
  313.4 51.1 %collective-permute-start.45 = (bf16[2,1024,128]{2,1,0:T(8,128)(2,1)}, bf16[2,1024,128]{2,1,0:T(8,128)(2,1)}, u32[]{:S(2)}, u32[]{:S(2)}) collective-permute-start(bf16[2,1024,128]{2,1,0:T(8,128)(2,1)} %get-tuple-element.122.refs_13_), channel_id=1, source_target_pairs={{12,8},{8,4},{4,0},{13,9},{9,5},{5,1},{14,10},{10,6},{6,2},{15,11}... | collective-permute-start | bytes 1572872 | tf_op jit(solution)/shard_map/ppermute | solution.py:638
  314.7 49.8 %collective-permute-start.46 = (bf16[2,1024,128]{2,1,0:T(8,128)(2,1)}, bf16[2,1024,128]{2,1,0:T(8,128)(2,1)}, u32[]{:S(2)}, u32[]{:S(2)}) collective-permute-start(bf16[2,1024,128]{2,1,0:T(8,128)(2,1)} %get-tuple-element.124.refs_15_), channel_id=1, source_target_pairs={{0,4},{4,8},{8,12},{1,5},{5,9},{9,13},{2,6},{6,10},{10,14},{3,7},{... | collective-permute-start | bytes 1572872 | tf_op jit(solution)/shard_map/ppermute | solution.py:639
  345.5 29.0 %collective-permute-start.47 = (bf16[544,1024]{1,0:T(8,128)(2,1)}, bf16[544,1024]{1,0:T(8,128)(2,1)}, u32[]{:S(2)}, u32[]{:S(2)}) collective-permute-start(bf16[544,1024]{1,0:T(8,128)(2,1)} %fusion.7), channel_id=1, source_target_pairs={{0,16},{16,0},{1,17},{17,1},{2,18},{18,2},{3,19},{19,3},{4,20},{20... | collective-permute-start | bytes 3342344 | tf_op jit(solution)/shard_map/ppermute | solution.py:422
  349.1 25.4 %collective-permute-start.48 = (bf16[256,1024]{1,0:T(8,128)(2,1)}, bf16[256,1024]{1,0:T(8,128)(2,1)S(1)}, u32[]{:S(2)}, u32[]{:S(2)}) collective-permute-start(bf16[256,1024]{1,0:T(8,128)(2,1)} %pad_maximum_fusion.24), channel_id=1, source_target_pairs={{0,8},{4,12},{8,0},{12,4},{1,9},{5,13},{9,1},{13,5},{2,10},{6,14},... | collective-permute-start | bytes 1572872 | tf_op jit(solution)/shard_map/ppermute | solution.py:426
  385.3 29.5 %collective-permute-start.51 = (bf16[256,1024]{1,0:T(8,128)(2,1)S(1)}, bf16[256,1024]{1,0:T(8,128)(2,1)S(1)}, u32[]{:S(2)}, u32[]{:S(2)}) collective-permute-start(bf16[256,1024]{1,0:T(8,128)(2,1)S(1)} %fusion.14), channel_id=1, source_target_pairs={{0,2},{1,3},{2,0},{3,1},{4,6},{5,7},{6,4},{7,5},{8,10},{9,11},{10,... | collective-permute-start | bytes 1572872 | tf_op jit(solution)/shard_map/ppermute | solution.py:373
  387.2 26.2 %collective-permute-start.54 = (bf16[136,1024]{1,0:T(8,128)(2,1)S(1)}, bf16[136,1024]{1,0:T(8,128)(2,1)S(1)}, u32[]{:S(2)}, u32[]{:S(2)}) collective-permute-start(bf16[136,1024]{1,0:T(8,128)(2,1)S(1)} %get-tuple-element.171), channel_id=1, source_target_pairs={{0,8},{4,12},{8,0},{12,4},{1,9},{5,13},{9,1},{13,5},{2,10},{6,14},... | collective-permute-start | bytes 835592 | tf_op jit(solution)/shard_map/ppermute | solution.py:426
  388.1 25.3 %collective-permute-start.55 = (bf16[136,1024]{1,0:T(8,128)(2,1)S(1)}, bf16[136,1024]{1,0:T(8,128)(2,1)S(1)}, u32[]{:S(2)}, u32[]{:S(2)}) collective-permute-start(bf16[136,1024]{1,0:T(8,128)(2,1)S(1)} %get-tuple-element.170), channel_id=1, source_target_pairs={{0,12},{4,8},{8,4},{12,0},{1,13},{5,9},{9,5},{13,1},{2,14},{6,10},... | collective-permute-start | bytes 835592 | tf_op jit(solution)/shard_map/ppermute | solution.py:426
  396.3 32.0 %collective-permute-start.49 = (bf16[256,1024]{1,0:T(8,128)(2,1)}, bf16[256,1024]{1,0:T(8,128)(2,1)}, u32[]{:S(2)}, u32[]{:S(2)}) collective-permute-start(bf16[256,1024]{1,0:T(8,128)(2,1)} %get-tuple-element.179), channel_id=1, source_target_pairs={{0,1},{1,0},{2,3},{3,2},{4,5},{5,4},{6,7},{7,6},{8,9},{9,8},{10,11... | collective-permute-start | bytes 1572872 | tf_op jit(solution)/shard_map/ppermute | solution.py:373
  420.2 25.2 %collective-permute-start.60 = (bf16[136,1024]{1,0:T(8,128)(2,1)S(1)}, bf16[136,1024]{1,0:T(8,128)(2,1)S(1)}, u32[]{:S(2)}, u32[]{:S(2)}) collective-permute-start(bf16[136,1024]{1,0:T(8,128)(2,1)S(1)} %add_convert_fusion.5), channel_id=1, source_target_pairs={{0,8},{4,12},{8,0},{12,4},{1,9},{5,13},{9,1},{13,5},{2,10},{6,14},... | collective-permute-start | bytes 835592 | tf_op jit(solution)/shard_map/ppermute | solution.py:426
  424.3 21.1 %collective-permute-start.61 = (bf16[136,1024]{1,0:T(8,128)(2,1)S(1)}, bf16[136,1024]{1,0:T(8,128)(2,1)S(1)}, u32[]{:S(2)}, u32[]{:S(2)}) collective-permute-start(bf16[136,1024]{1,0:T(8,128)(2,1)S(1)} %add_convert_fusion.5), channel_id=1, source_target_pairs={{0,4},{4,0},{8,12},{12,8},{1,5},{5,1},{9,13},{13,9},{2,6},{6,2},{1... | collective-permute-start | bytes 835592 | tf_op jit(solution)/shard_map/ppermute | solution.py:426
  426.6 35.4 %collective-permute-start.62 = (bf16[512,1024]{1,0:T(8,128)(2,1)}, bf16[512,1024]{1,0:T(8,128)(2,1)}, u32[]{:S(2)}, u32[]{:S(2)}) collective-permute-start(bf16[512,1024]{1,0:T(8,128)(2,1)} %pad_maximum_fusion.17), channel_id=1, source_target_pairs={{0,4},{4,0},{8,12},{12,8},{1,5},{5,1},{9,13},{13,9},{2,6},{6,2},{1... | collective-permute-start | bytes 3145736 | tf_op jit(solution)/shard_map/ppermute | solution.py:426
  430.0 21.0 %collective-permute-start.56 = (bf16[256,1024]{1,0:T(8,128)(2,1)S(1)}, bf16[256,1024]{1,0:T(8,128)(2,1)}, u32[]{:S(2)}, u32[]{:S(2)}) collective-permute-start(bf16[256,1024]{1,0:T(8,128)(2,1)S(1)} %fusion.17), channel_id=1, source_target_pairs={{0,2},{1,3},{2,0},{3,1},{4,6},{5,7},{6,4},{7,5},{8,10},{9,11},{10,... | collective-permute-start | bytes 1572872 | tf_op jit(solution)/shard_map/ppermute | solution.py:373
  430.3 36.9 %collective-permute-start.58 = (bf16[256,1024]{1,0:T(8,128)(2,1)S(1)}, bf16[256,1024]{1,0:T(8,128)(2,1)}, u32[]{:S(2)}, u32[]{:S(2)}) collective-permute-start(bf16[256,1024]{1,0:T(8,128)(2,1)S(1)} %fusion.17), channel_id=1, source_target_pairs={{0,1},{1,0},{2,3},{3,2},{4,5},{5,4},{6,7},{7,6},{8,9},{9,8},{10,11... | collective-permute-start | bytes 1572872 | tf_op jit(solution)/shard_map/ppermute | solution.py:373
  (160 other events, 1083.6 us)
